TPU v7x, 32 devices: a whole 2x2x4 slice. The times are simulated.
32 devices in a mesh: group: 2 (over x), shard: 16 (over z, y, core).
Axes of the slice: x: 2, y: 2, z: 4, core: 2. Of those that a mesh axis runs over, the one named last changes fastest.
Arguments:
- offer_attribute_matrix: bfloat16 [128, 128, 1024], P(('group', 'shard')), may hold values from -6 to 6
- kept_offers: int32 [128, 32], P(('group', 'shard')), may hold values from 0 to 127, as said below
- expert_target: int32 [128, 6], P(('group', 'shard')), may hold values from 0 to 15, all different within a row; in each aligned block of 4 rows (0 to 3, 4 to 7, ...) at most 3 rows name the same one
- sequence_extent: int32 [128], P(('group', 'shard')), may hold values from 1 to 128
- behaviour_sequence: bfloat16 [128, 128, 512], P(('group', 'shard')), may hold values from -6 to 6
- inner_projection_matrix: bfloat16 [1024, 1024], replicated, may hold values from -0.1875 to 0.1875
- student_rating_vector: bfloat16 [1024], replicated, may hold values from -0.1875 to 0.1875
- asking_matrix: bfloat16 [16, 1024, 512], P('shard'), may hold values from -0.1875 to 0.1875
- lookup_matrix: bfloat16 [16, 512, 512], P('shard'), may hold values from -0.25 to 0.25
- content_matrix: bfloat16 [16, 512, 512], P('shard'), may hold values from -0.25 to 0.25
- expert_rating_vector: bfloat16 [16, 512], P('shard'), may hold values from -1.1953125 to 1.1953125
Outputs:
- grad_hidden: float32 [1024, 1024], P('shard')
- grad_score: float32 [1024], replicated
Inputs may be any that keep to these rules, and one draw needn't show every extreme that they name: `kept_offers`: the 32 survivors of a request are distinct candidates. `expert_target`: each request names 6 distinct experts; the requests of one device name any expert at most 3 times, a bound that some block reaches.
All inputs are finite; a program needn't handle non-finite values.
Results may differ from a plain program's by a relative error of at most 0.005.
Values may be sent and summed in bfloat16 or wider, within the bound.
No kernel may reach another device: no remote copies, remote signals or barrier semaphores. Data moves between devices by JAX's collectives and lax.ppermute only.
A program may use at most 128 MiB of HBM per device.

v0:
```python
import functools

import jax
import jax.numpy as jnp
from jax import lax
from jax.experimental import pallas as pl
from jax.experimental.pallas import tpu as pltpu
from jax.sharding import PartitionSpec as P


ATTENDER_GANGS = 8
META_ROWS = 16
VMEM = pltpu.VMEM
F32 = jnp.float32
BF16 = jnp.bfloat16


def full_vmem():
    return pl.BlockSpec(memory_space=pltpu.VMEM)


def in_place():
    return pl.BlockSpec(memory_space=pl.ANY)


def scalars():
    return pl.BlockSpec(memory_space=pltpu.SMEM)


def room(mib):
    return pltpu.CompilerParams(vmem_limit_bytes=mib * 2**20)


def stays(x):
    return pltpu.with_memory_space_constraint(x, pltpu.HBM)


def fetch(source, target, sem):
    copy = pltpu.make_async_copy(source, target, sem)
    copy.start()
    return copy.wait


def rows_of(requests, hist_slots, kept, feature_span, focus_span):
    hist_rows = requests * hist_slots
    kept_rows = requests * kept
    pieces = feature_span // focus_span
    return hist_rows, kept_rows, pieces, hist_rows + kept_rows * pieces


def pack_kernel(target_ref, extent_ref, x_hbm, kept_ref, hist_hbm, out_ref, x_ref, sems):
    requests, cand, _ = x_ref.shape
    kept = kept_ref.shape[1]
    focus = hist_hbm.shape[1]
    hist_rows = hist_hbm.shape[0]
    tops = target_ref.shape[1]
    pieces = x_ref.shape[2] // focus
    meta_at = hist_rows + pieces * requests * kept
    waits = [fetch(x_hbm.at[r], x_ref.at[r], sems.at[r]) for r in range(requests)]
    wait_hist = fetch(hist_hbm, out_ref.at[pl.ds(0, hist_rows), :], sems.at[requests])
    row = lax.broadcasted_iota(jnp.int32, (META_ROWS, focus), 0)
    lane = lax.broadcasted_iota(jnp.int32, (META_ROWS, focus), 1)
    meta = jnp.zeros((META_ROWS, focus), jnp.int32)
    for r in range(requests):
        for t in range(tops):
            meta = jnp.where((row == r) & (lane == t), target_ref[r, t], meta)
        meta = jnp.where((row == r) & (lane == tops), extent_ref[r], meta)
    out_ref[meta_at:, :] = meta.astype(F32).astype(BF16)
    for r in range(requests):
        waits[r]()
        cand_of = lax.broadcasted_iota(jnp.int32, (cand, kept), 0)
        pick = (cand_of == kept_ref[r : r + 1, :]).astype(F32).astype(BF16)
        for p in range(pieces):
            rows = lax.dot_general(
                pick,
                x_ref[r, :, p * focus : (p + 1) * focus],
                (((0,), (0,)), ((), ())),
                preferred_element_type=F32,
            )
            at = hist_rows + p * requests * kept + r * kept
            out_ref[at : at + kept, :] = rows.astype(BF16)
    wait_hist()


def pack(x, kept, hist, targets, extents):
    requests, _, feats = x.shape
    focus = hist.shape[2]
    flat_hist = hist.reshape(-1, focus)
    total = rows_of(requests, hist.shape[1], kept.shape[1], feats, focus)[3] + META_ROWS
    return pl.pallas_call(
        pack_kernel,
        out_shape=jax.ShapeDtypeStruct((total, focus), BF16),
        in_specs=[scalars(), scalars(), in_place(), full_vmem(), in_place()],
        out_specs=full_vmem(),
        scratch_shapes=[VMEM(x.shape, BF16), pltpu.SemaphoreType.DMA((requests + 1,))],
        cost_estimate=pl.CostEstimate(flops=10**8, bytes_accessed=3 * 10**6, transcendentals=0),
    )(targets, extents, stays(x), kept, stays(flat_hist))


def student_kernel(requests, chunk, order, me_ref, x_ref, w_ref, s_ref, c_ref, e_ref, *refs):
    grad_refs, (gs_ref, rate_ref, part_ref) = refs[:-3], refs[-3:]
    rows, feats = x_ref.shape
    units = w_ref.shape[1]
    cand = rows // requests
    score_vec = s_ref[...].astype(F32)

    def one(r, total):
        at = pl.ds(pl.multiple_of(r * cand, cand), cand)
        preact = jnp.dot(x_ref[at, :], w_ref[...], preferred_element_type=F32)
        hidden = jnp.maximum(preact, 0.0)
        exp_scores = jnp.exp(jnp.sum(hidden * score_vec, axis=-1, keepdims=True))
        student = exp_scores / jnp.sum(exp_scores, axis=0, keepdims=True)
        live = jnp.where(preact > 0, student * score_vec, 0.0)
        part_ref[at, :] = live.astype(BF16)
        return total + jnp.sum(student * hidden, axis=0, keepdims=True)

    gs_ref[...] = lax.fori_loop(0, requests, one, jnp.zeros((1, units), F32))
    step = min(256, feats)
    held = grad_refs[0].shape[0] // chunk

    def block(i, carry):
        at = pl.ds(pl.multiple_of(i * step, step), step)
        grad = lax.dot_general(
            x_ref[:, at], part_ref[...], (((0,), (0,)), ((), ())), preferred_element_type=F32
        )
        for j in range(step // chunk):
            piece = grad[j * chunk : (j + 1) * chunk, :]
            spot = order(i * (step // chunk) + j, me_ref[0])
            for half, ref in enumerate(grad_refs):

                @pl.when(spot // held == half)
                def _(ref=ref, half=half, piece=piece, spot=spot):
                    place = jnp.clip(spot - half * held, 0, held - 1)
                    ref[pl.ds(pl.multiple_of(place * chunk, chunk), chunk), :] = piece

        return carry

    lax.fori_loop(0, feats // step, block, 0)
    rated = c_ref[...].astype(F32) * e_ref[...].astype(F32)
    focus, wide = rate_ref.shape
    gangs = ATTENDER_GANGS
    head_row = lax.broadcasted_iota(jnp.int32, (focus, wide), 0) // (focus // gangs)
    head_col = lax.broadcasted_iota(jnp.int32, (focus, wide), 1) // (wide // gangs)
    same = (head_row == head_col).astype(F32).astype(BF16)
    high = rated.astype(BF16)
    middle = (rated - high.astype(F32)).astype(BF16)
    low = (rated - high.astype(F32) - middle.astype(F32)).astype(BF16)
    rate = jnp.dot(high, same, preferred_element_type=F32)
    rate += jnp.dot(middle, same, preferred_element_type=F32)
    rate += jnp.dot(low, same, preferred_element_type=F32)
    rate_ref[...] = rate.astype(BF16)


def student_part(x, w, s, content, rating, wide, me, pieces, halves, order):
    requests, cand, feats = x.shape
    units = w.shape[1]
    rows = requests * cand
    return pl.pallas_call(
        functools.partial(student_kernel, requests, feats // pieces, order),
        out_shape=(jax.ShapeDtypeStruct((feats // halves, units), F32),) * halves
        + (
            jax.ShapeDtypeStruct((1, units), F32),
            jax.ShapeDtypeStruct((content.shape[0], wide), BF16),
        ),
        in_specs=[scalars()] + [full_vmem()] * 5,
        out_specs=(full_vmem(),) * (halves + 2),
        scratch_shapes=[VMEM((rows, units), BF16)],
        compiler_params=room(20),
        cost_estimate=pl.CostEstimate(
            flops=4 * requests * cand * feats * units, bytes_accessed=8 * 10**6, transcendentals=0
        ),
    )(me, x.reshape(rows, feats), w, s.reshape(1, units), content, rating.reshape(1, -1))


def block_scores(dims, me, payload, ask, look, rate):
    requests, hist_slots, kept, tops, gangs = dims
    focus = look.shape[0]
    span = look.shape[1] // gangs
    hist_rows, kept_rows, pieces, meta_at = rows_of(
        requests, hist_slots, kept, ask.shape[0], focus
    )
    hist = payload[:hist_rows, :]
    keys = jnp.dot(hist, look[...], preferred_element_type=F32).astype(BF16)
    values = jnp.dot(hist, rate[...], preferred_element_type=F32)
    queries = None
    for p in range(pieces):
        rows = payload[hist_rows + p * kept_rows : hist_rows + (p + 1) * kept_rows, :]
        part = jnp.dot(rows, ask[p * focus : (p + 1) * focus, :], preferred_element_type=F32)
        queries = part if queries is None else queries + part
    queries = (queries * span**-0.5).astype(BF16)
    wide = gangs * kept
    head_row = lax.broadcasted_iota(jnp.int32, (wide, look.shape[1]), 0) // kept
    head_col = lax.broadcasted_iota(jnp.int32, (wide, look.shape[1]), 1) // span
    same_head = head_row == head_col
    slot = lax.broadcasted_iota(jnp.int32, (hist_slots, wide), 0).astype(F32)
    meta = payload[meta_at : meta_at + META_ROWS, :].astype(F32)
    meta_lane = lax.broadcasted_iota(jnp.int32, meta.shape, 1)
    hit = jnp.where((meta_lane < tops) & (meta == me.astype(F32)), 1.0, 0.0)
    routed = jnp.max(hit, axis=-1, keepdims=True)
    lengths = jnp.sum(jnp.where(meta_lane == tops, meta, 0.0), axis=-1, keepdims=True)
    lane = lax.broadcasted_iota(jnp.int32, (1, kept_rows), 1) // kept
    scores = jnp.zeros((1, kept_rows), F32)
    for r in range(requests):
        q = queries[r * kept : (r + 1) * kept, :]
        q_wide = jnp.where(same_head, jnp.concatenate([q] * gangs, axis=0), jnp.zeros((), BF16))
        logits = lax.dot_general(
            keys[r * hist_slots : (r + 1) * hist_slots, :],
            q_wide,
            (((1,), (1,)), ((), ())),
            preferred_element_type=F32,
        )
        weights = jnp.where(slot < lengths[r : r + 1, :], jnp.exp(logits), 0.0)
        mixed = weights * values[r * hist_slots : (r + 1) * hist_slots, :]
        per_head = jnp.sum(mixed, axis=0, keepdims=True) / jnp.sum(weights, axis=0, keepdims=True)
        folded = per_head[:, :kept_rows]
        for b in range(1, wide // kept_rows):
            folded = folded + per_head[:, b * kept_rows : (b + 1) * kept_rows]
        shift = kept
        while shift < kept_rows:
            folded = folded + pltpu.roll(folded, shift, 1)
            shift *= 2
        scores = jnp.where((lane == r) & (routed[r : r + 1, :] > 0), folded, scores)
    return scores


def own_columns(me, rows_of_piece, sel_rows):
    focus = rows_of_piece[0].shape[1]
    own = None
    for p, rows in enumerate(rows_of_piece):
        feature = lax.broadcasted_iota(jnp.int32, (sel_rows, focus), 1) + p * focus
        wanted = lax.broadcasted_iota(jnp.int32, (sel_rows, focus), 0) + me * sel_rows
        pick = (feature == wanted).astype(F32).astype(BF16)
        got = lax.dot_general(pick, rows, (((1,), (1,)), ((), ())), preferred_element_type=F32)
        own = got if own is None else own + got
    return own.astype(BF16)


def rank_kernel(dims, sel_rows, layout, wants, first, info_ref, *refs):
    want_scores, want_hidden, parts = wants
    requests, hist_slots, kept, _, _ = dims
    n_in = sum(layout) if layout else 1
    arrays, refs = refs[:n_in], refs[n_in:]
    if want_scores:
        (a_ref, l_ref, r_ref), refs = refs[:3], refs[3:]
    if want_hidden:
        w_ref, refs = refs[0], refs[1:]
    if parts is not None:
        earlier, gs_ref, refs = refs[: len(parts)], refs[len(parts)], refs[len(parts) + 1 :]
    if want_scores:
        o_ref, refs = refs[0], refs[1:]
    if want_hidden:
        h_ref, s_ref, refs = refs[0], refs[1], refs[2:]
    buf, sems = refs
    blocks, _, focus = buf.shape
    feats = (a_ref if want_scores else w_ref).shape[0]
    hist_rows, kept_rows, pieces, _ = rows_of(requests, hist_slots, kept, feats, focus)
    low = 0 if want_scores else hist_rows
    high = low + buf.shape[1]

    def start_block(b):
        if not layout:
            fetch(arrays[0].at[b, pl.ds(low, high - low), :], buf.at[b], sems.at[b])
            return
        at, i = 0, sum(layout[:b])
        for array in arrays[i : i + layout[b]]:
            rows = array.shape[0]
            begin, end = max(at, low), min(at + rows, high)
            if begin < end:
                fetch(
                    array.at[pl.ds(begin - at, end - begin), :],
                    buf.at[b, pl.ds(begin - low, end - begin), :],
                    sems.at[b],
                )
            at += rows

    def wait_block(b):
        pltpu.make_async_copy(buf.at[b], buf.at[b], sems.at[b]).wait()

    for b in range(blocks):
        start_block(b)
    if parts is not None:
        slot = 0
        for ref, count in zip(earlier, parts):
            for b in range(count):
                o_ref[pl.ds(info_ref[1] ^ slot, 1), :] = ref[b]
                slot += 1
        scored, lanes = slot + blocks, o_ref.shape[1]
        for i in range(o_ref.shape[0] - scored):
            o_ref[scored + i : scored + i + 1, :] = gs_ref[:, i * lanes : (i + 1) * lanes]
    me = info_ref[0]
    if want_scores:

        def one(b, carry):
            wait_block(b)
            row = block_scores(dims, me, buf.at[b], a_ref, l_ref, r_ref)
            if parts is not None:
                o_ref[pl.ds(info_ref[1] ^ (first + b), 1), :] = row
            else:
                o_ref[b] = row
            return carry

        lax.fori_loop(0, blocks, one, 0)
    else:
        for b in range(blocks):
            wait_block(b)
    if want_hidden:
        rows_of_piece = []
        for p in range(pieces):
            at = hist_rows - low + p * kept_rows
            rows_of_piece.append(
                jnp.concatenate([buf[b, at : at + kept_rows, :] for b in range(blocks)], axis=0)
            )
        preact = None
        for p, rows in enumerate(rows_of_piece):
            part = jnp.dot(
                rows, w_ref[p * focus : (p + 1) * focus, :], preferred_element_type=F32
            )
            preact = part if preact is None else preact + part
        h_ref[...] = jnp.maximum(preact, 0.0).astype(BF16)
        s_ref[...] = own_columns(me, rows_of_piece, sel_rows)


def rank(dims, me, payloads, score_weights, hidden_weights, sel_rows, first=0, message=None):
    requests, _, kept, _, _ = dims
    kept_rows = requests * kept
    want_scores, want_hidden = score_weights is not None, hidden_weights is not None
    if isinstance(payloads, list):
        blocks = len(payloads)
        layout = [len(p) for p in payloads]
        arrays = [a for p in payloads for a in p]
        rows, focus = sum(a.shape[0] for a in payloads[0]), arrays[0].shape[1]
    else:
        blocks, rows, focus = payloads.shape
        layout, arrays = None, [payloads]
    if not want_scores:
        rows = kept_rows * (hidden_weights[0].shape[0] // focus)
    scratch = [VMEM((blocks, rows, focus), BF16), pltpu.SemaphoreType.DMA((blocks,))]
    weights = list(score_weights or ()) + list(hidden_weights or ())
    shapes, outs, small, parts = [], [], [], None
    if want_scores:
        if message is None:
            shapes.append(jax.ShapeDtypeStruct((blocks, 1, kept_rows), F32))
        else:
            earlier, gs = message
            parts = [e.shape[0] for e in earlier]
            small = list(earlier) + [gs]
            total = sum(parts) + blocks + gs.shape[1] // kept_rows
            shapes.append(jax.ShapeDtypeStruct((total, kept_rows), F32))
        outs.append(full_vmem())
    if want_hidden:
        units = hidden_weights[0].shape[1]
        shapes.append(jax.ShapeDtypeStruct((blocks * kept_rows, units), BF16))
        shapes.append(jax.ShapeDtypeStruct((sel_rows, blocks * kept_rows), BF16))
        outs += [full_vmem()] * 2
    flops = blocks * (7 * 10**8 * want_scores + 3 * 10**8 * want_hidden)
    return pl.pallas_call(
        functools.partial(
            rank_kernel, dims, sel_rows, layout, (want_scores, want_hidden, parts), first
        ),
        out_shape=tuple(shapes),
        in_specs=[scalars()]
        + [in_place()] * len(arrays)
        + [full_vmem()] * (len(weights) + len(small)),
        out_specs=tuple(outs),
        scratch_shapes=scratch,
        compiler_params=room(22),
        cost_estimate=pl.CostEstimate(
            flops=flops, bytes_accessed=blocks * 10**6, transcendentals=0
        ),
    )(me, *arrays, *weights, *small)


def target_kernel(kept, tops, n_parts, me_ref, got_ref, s_ref, base_ref, *refs):
    sel_refs, hid_refs = refs[:n_parts], refs[n_parts : 2 * n_parts]
    out_ref, target_ref = refs[2 * n_parts :]
    kept_rows = got_ref.shape[1]
    units = s_ref.shape[1]
    blocks = got_ref.shape[0] - units // kept_rows
    sel_rows = sel_refs[0].shape[0]
    total = got_ref[...]
    exp_teacher = jnp.exp(total[:blocks, :] / tops)
    near = lax.broadcasted_iota(jnp.int32, (kept_rows, kept_rows), 0) // kept
    far = lax.broadcasted_iota(jnp.int32, (kept_rows, kept_rows), 1) // kept
    group = (near == far).astype(F32)
    sums = jnp.dot(
        exp_teacher, group, preferred_element_type=F32, precision=lax.Precision.HIGHEST
    )
    target_ref[...] = exp_teacher / sums
    grad = jnp.zeros((sel_rows, units), F32)
    lift = jnp.zeros((1, units), F32)
    slot = 0
    for sel_ref, hid_ref in zip(sel_refs, hid_refs):
        count = sel_ref.shape[1] // kept_rows
        target = jnp.concatenate(
            [target_ref[pl.ds(me_ref[1] ^ (slot + b), 1), :] for b in range(count)], axis=1
        )
        high = target.astype(BF16).astype(F32)
        hidden = hid_ref[...]
        slot += count
        live = jnp.where(hidden > 0, jnp.ones((), BF16), jnp.zeros((), BF16))
        scaled = (sel_ref[...].astype(F32) * target).astype(BF16)
        grad += jnp.dot(scaled, live, preferred_element_type=F32)
        both = jnp.concatenate([high, target - high], axis=0).astype(BF16)
        pair = jnp.dot(both, hidden, preferred_element_type=F32)
        lift += pair[0:1, :] + pair[1:2, :]
    out_ref[:sel_rows, :] = -grad * s_ref[...].astype(F32)
    held = base_ref.shape[0]
    at = pl.ds(pl.multiple_of(me_ref[2] * held, 8), held)
    out_ref[at, :] = out_ref[at, :] + base_ref[...]
    for i in range(units // kept_rows):
        at = slice(i * kept_rows, (i + 1) * kept_rows)
        out_ref[sel_rows : sel_rows + 1, at] = total[blocks + i : blocks + i + 1, :] - lift[:, at]
    out_ref[sel_rows + 1 :, :] = jnp.zeros((out_ref.shape[0] - sel_rows - 1, units), F32)


def target_part(kept, tops, me, got, hiddens, owns, s, base):
    sel_rows = owns[0].shape[0]
    units = hiddens[0].shape[1]
    blocks = got.shape[0] - units // got.shape[1]
    parts = len(hiddens)
    return pl.pallas_call(
        functools.partial(target_kernel, kept, tops, parts),
        out_shape=jax.ShapeDtypeStruct((sel_rows + 8, units), F32),
        in_specs=[scalars()] + [full_vmem()] * (3 + 2 * parts),
        out_specs=full_vmem(),
        scratch_shapes=[VMEM((blocks, got.shape[1]), F32)],
        compiler_params=room(22),
        cost_estimate=pl.CostEstimate(flops=10**9, bytes_accessed=6 * 10**6, transcendentals=0),
    )(me, got, s.reshape(1, units), base, *owns, *hiddens)


def along(pairs):
    table = []
    for z, z_to in pairs:
        for low in range(4):
            table.append((4 * z + low, 4 * z_to + low))
    return table


def flip(bits):
    return [(i, i ^ bits) for i in range(16)]


SIBLING, Y_OVER, Z_NEAR, Z_FAR = flip(1), flip(2), flip(4), flip(8)
Z_INNER = along([(1, 2), (2, 1)])
Z_OUT = along([(1, 0), (2, 3)])


def shift(x, table, axis="shard"):
    return lax.ppermute(x, axis, table)


def gather_stages(b, me):
    inner = ((me >> 2) ^ (me >> 3)) & 1 == 1
    cut = -(-b.shape[0] // 32) * 16
    near = shift(b, Z_NEAR)
    over = shift(b, Y_OVER)
    mid = shift(b, Z_INNER)
    mid_far = shift(near, Z_INNER)
    out_far = shift(mid, Z_OUT)
    over_near = shift(near, Y_OVER)
    far = jnp.where(inner, mid_far, out_far)
    out_last = shift(mid_far, Z_OUT)
    over_far = shift(far, Y_OVER)
    last = [jnp.where(inner, mid[:cut], out_last[:cut]), jnp.where(inner, mid[cut:], out_last[cut:])]
    over_last = shift(last[0], Y_OVER)
    rest_out = shift(over_far[cut:], Z_OUT)
    rest_mid = shift(over[cut:], Z_INNER)
    over_rest = jnp.where(inner, rest_mid, rest_out)

    def both(*pieces):
        return [list(pieces), [shift(p, SIBLING) for p in pieces]]

    return [
        both(b),
        both(over) + both(near),
        both(over_near) + both(far),
        both(over_far) + both(*last),
        both(over_last, over_rest),
    ]


def halving_order(block, me):
    away = block ^ me
    z1, z0, y, core, grp = [(away >> i) & 1 for i in (4, 3, 2, 1, 0)]
    return (core << 4) | (grp << 3) | (z0 << 2) | (z1 << 1) | y


def halve(keep, sent):
    for table, axis in (
        (SIBLING, "shard"),
        ([(0, 1), (1, 0)], "group"),
        (Z_NEAR, "shard"),
        (Z_FAR, "shard"),
        (Y_OVER, "shard"),
    ):
        wide = axis == "group" or table is SIBLING
        got = shift(sent if wide else sent.astype(BF16), table, axis).astype(F32)
        half = keep.shape[0] // 2
        if table is Y_OVER:
            return keep + got
        keep, sent = keep[:half] + got[:half], keep[half:] + got[half:]


def sum_over_shard(x):
    for table in (SIBLING, Y_OVER, Z_NEAR, Z_FAR):
        x = x + shift(x, table)
    return x


def sum_kernel(a_ref, b_ref, grad_ref, score_ref):
    rows = grad_ref.shape[0]
    grad_ref[...] = a_ref[:rows, :] + b_ref[:rows, :]
    score_ref[...] = a_ref[rows : rows + 1, :] + b_ref[rows : rows + 1, :]


def sum_two(a, b, rows):
    return pl.pallas_call(
        sum_kernel,
        out_shape=(
            jax.ShapeDtypeStruct((rows, a.shape[1]), F32),
            jax.ShapeDtypeStruct((1, a.shape[1]), F32),
        ),
        in_specs=[full_vmem()] * 2,
        out_specs=(full_vmem(),) * 2,
        compiler_params=room(4),
    )(a, b)


def body(
    offer_attribute_matrix,
    kept_offers,
    expert_target,
    sequence_extent,
    behaviour_sequence,
    inner_projection_matrix,
    student_rating_vector,
    asking_matrix,
    lookup_matrix,
    content_matrix,
    expert_rating_vector,
):
    requests, _, feats = offer_attribute_matrix.shape
    kept = kept_offers.shape[1]
    hist_slots, _ = behaviour_sequence.shape[1:]
    tops = expert_target.shape[1]
    units = inner_projection_matrix.shape[1]
    n_shard = lax.axis_size("shard")
    sel_rows = feats // n_shard
    me = lax.axis_index("shard")
    n_group = lax.axis_size("group")
    grp = lax.axis_index("group")

    payload = pack(
        offer_attribute_matrix, kept_offers, behaviour_sequence, expert_target, sequence_extent
    )
    linked = n_shard == 16 and n_group == 2
    place = (me * n_group + grp if linked else me).astype(jnp.int32).reshape(1)
    stack = (
        offer_attribute_matrix,
        inner_projection_matrix,
        student_rating_vector,
        content_matrix[0],
        expert_rating_vector[0],
        ATTENDER_GANGS * kept,
        place,
    )
    if linked:
        stages = gather_stages(payload, me)
        keep, sent, gs_student, rate = student_part(
            *stack, n_shard * n_group, 2, halving_order
        )
        base = halve(keep, sent)
        info = jnp.stack([me, me, grp]).astype(jnp.int32)
    else:
        payloads = lax.all_gather(payload, "shard", axis=0, tiled=False)
        stages = [payloads[b : b + 4] for b in range(0, n_shard, 4)]
        grad_student, gs_student, rate = student_part(
            *stack, n_shard, 1, lambda block, at: block
        )
        base = lax.psum_scatter(grad_student, "shard", scatter_dimension=0, tiled=True)
        info = jnp.stack([me, 0 * me, 0 * me]).astype(jnp.int32)

    dims = (requests, hist_slots, kept, tops, ATTENDER_GANGS)
    score_weights = (asking_matrix[0], lookup_matrix[0], rate)
    hidden_weights = (inner_projection_matrix,)
    scores, hiddens, owns = [], [], []
    late = len(stages) - 2 if linked else len(stages) - 1
    for number, stage in enumerate(stages[:-1]):
        if number < late:
            score, hidden, own = rank(dims, info, stage, score_weights, hidden_weights, sel_rows)
            hiddens.append(hidden)
            owns.append(own)
        else:
            (score,) = rank(dims, info, stage, score_weights, None, sel_rows)
        scores.append(score)
    known = sum(s.shape[0] for s in scores)
    (send,) = rank(
        dims, info, stages[-1], score_weights, None, sel_rows, known, (scores, gs_student)
    )
    rest = stages[-2] + stages[-1] if linked else stages[-1]
    hidden, own = rank(dims, info, rest, None, hidden_weights, sel_rows)
    hiddens.append(hidden)
    owns.append(own)
    got = sum_over_shard(send) if linked else lax.psum(send, "shard")
    mine = target_part(kept, tops, info, got, hiddens, owns, student_rating_vector, base)
    if linked:
        grad, lift = sum_two(mine, shift(mine, [(0, 1), (1, 0)], "group"), sel_rows)
        return grad, lift.reshape(units)
    whole = lax.psum(mine, "group")
    return whole[:sel_rows], whole[sel_rows]


def solution(mesh):
    placed = (
        P(("group", "shard"), None, None),
        P(("group", "shard"), None),
        P(("group", "shard"), None),
        P(("group", "shard")),
        P(("group", "shard"), None, None),
        P(),
        P(),
        P("shard", None, None),
        P("shard", None, None),
        P("shard", None, None),
        P("shard", None),
    )
    return jax.shard_map(
        body, mesh=mesh, in_specs=placed, out_specs=(P("shard", None), P()), check_vma=False
    )
```

profile of v0, /device:TPU:0, one launch (start us, length us, event | category | flops | bytes accessed | tf_op | source)
XLA Modules:
  0.0 145.8 jit_solution(10063259617883432034)
XLA Ops:
  0.7 3.5 %shard_map.122.refs_0_ = bf16[784,512]{1,0:T(8,128)(2,1)} custom-call(s32[4,6]{1,0:T(4,128)} %target_ref.1, s32[4]{0:T(128)} %extent_ref.1, bf16[4,128,1024]{2,1,0:T(8,128)(2,1)} %x_hbm.1, s32[4,32]{1,0:T(4,128)} %kept_ref.1, bf16[512,512]{1,0:T(8,128)(2,1)} %bitcast.21), custom_call_target="tpu_custom_call" | custom-call | flops 100000000 | bytes 3000000 | tf_op jit(solution)/shard_map/pallas_call | solution.py:90
  4.2 3.1 %collective-permute-start.1 = (bf16[784,512]{1,0:T(8,128)(2,1)}, bf16[784,512]{1,0:T(8,128)(2,1)}, u32[]{:S(2)}, u32[]{:S(2)}) collective-permute-start(bf16[784,512]{1,0:T(8,128)(2,1)} %shard_map.122.refs_0_), channel_id=1, source_target_pairs={{0,4},{1,5},{2,6},{3,7},{4,0},{5,1},{6,2},{7,3},{8,12},{9,13},{10,... | collective-permute-start | bytes 2408456 | tf_op jit(solution)/shard_map/ppermute | solution.py:450
  11.5 7.2 %shard_map.123 = (f32[512,1024]{1,0:T(8,128)S(1)}, f32[512,1024]{1,0:T(8,128)}, f32[1,1024]{1,0:T(1,128)S(1)}, bf16[512,256]{1,0:T(8,128)(2,1)S(1)}) custom-call(s32[1]{0:T(128)} %bitcast.5.me_ref, bf16[512,1024]{1,0:T(8,128)(2,1)S(1)} %bitcast.9, bf16[1024,1024]{1,0:T(8,128)(2,1)S(1)} %copy-done, bf16[1,1024]{1,0:T(2,128)(2,1)S(1)} %reshape.23.s_ref, ...), custom_call_target="tpu_custom_call" | custom-call | flops 2147483648 | bytes 8000000 | tf_op jit(solution)/shard_map/pallas_call | solution.py:158
  20.6 5.0 %collective-permute-done.1.refs_2_ = bf16[784,512]{1,0:T(8,128)(2,1)} collective-permute-done((bf16[784,512]{1,0:T(8,128)(2,1)}, bf16[784,512]{1,0:T(8,128)(2,1)}, u32[]{:S(2)}, u32[]{:S(2)}) %collective-permute-start.1) | collective-permute-done | bytes 802848 | tf_op jit(solution)/shard_map/ppermute | solution.py:450
  28.4 10.8 %collective-permute-done.5.refs_0_ = bf16[784,512]{1,0:T(8,128)(2,1)} collective-permute-done((bf16[784,512]{1,0:T(8,128)(2,1)S(1)}, bf16[784,512]{1,0:T(8,128)(2,1)}, u32[]{:S(2)}, u32[]{:S(2)}) %collective-permute-start.5) | collective-permute-done | bytes 802848 | tf_op jit(solution)/shard_map/ppermute | solution.py:450
  48.5 4.0 %shard_map.124 = (f32[2,1,128]{2,1,0:T(1,128)S(1)}, bf16[256,1024]{1,0:T(8,128)(2,1)S(1)}, bf16[64,256]{1,0:T(8,128)(2,1)S(1)}) custom-call(s32[3]{0:T(128)S(1)} %pad_add_fusion.info_ref.me_ref, bf16[784,512]{1,0:T(8,128)(2,1)S(1)} %copy-done.5, bf16[784,512]{1,0:T(8,128)(2,1)S(1)} %copy-done.9, bf16[1024,512]{1,0:T(8,128)(2,1)S(1)} %bitcast.10, ...), custom_call_target="tpu_custom_call" | custom-call | flops 2000000000 | bytes 2000000 | tf_op jit(solution)/shard_map/pallas_call | solution.py:356
  55.9 5.0 %collective-permute-done.15.refs_0_ = bf16[784,512]{1,0:T(8,128)(2,1)} collective-permute-done((bf16[784,512]{1,0:T(8,128)(2,1)}, bf16[784,512]{1,0:T(8,128)(2,1)}, u32[]{:S(2)}, u32[]{:S(2)}) %collective-permute-start.15) | collective-permute-done | bytes 802848 | tf_op jit(solution)/shard_map/ppermute | solution.py:450
  60.8 8.4 %shard_map.125 = (f32[4,1,128]{2,1,0:T(1,128)S(1)}, bf16[512,1024]{1,0:T(8,128)(2,1)S(1)}, bf16[64,512]{1,0:T(8,128)(2,1)S(1)}) custom-call(s32[3]{0:T(128)S(1)} %pad_add_fusion.info_ref.me_ref, bf16[784,512]{1,0:T(8,128)(2,1)} %collective-permute-done.5.refs_0_, bf16[784,512]{1,0:T(8,128)(2,1)} %collective-permute-done.13.refs_1_, ...), custom_call_target="tpu_custom_call" | custom-call | flops 4000000000 | bytes 4000000 | tf_op jit(solution)/shard_map/pallas_call | solution.py:356
  69.9 1.9 %slice_add_fusion.1 = (f32[256,1024]{1,0:T(8,128)S(1)}, f32[256,1024]{1,0:T(8,128)S(1)}) fusion(f32[512,1024]{1,0:T(8,128)} %collective-permute-done.25, f32[512,1024]{1,0:T(8,128)S(1)} %get-tuple-element.24), kind=kLoop, calls=%fused_computation.1 | loop fusion | flops 524288 | bytes 6291456 | tf_op jit(solution)/shard_map/add | solution.py:502
  71.8 6.8 %collective-permute-done.3 = bf16[784,512]{1,0:T(8,128)(2,1)S(1)} collective-permute-done((bf16[784,512]{1,0:T(8,128)(2,1)}, bf16[784,512]{1,0:T(8,128)(2,1)S(1)}, u32[]{:S(2)}, u32[]{:S(2)}) %collective-permute-start.3) | collective-permute-done | bytes 802848 | tf_op jit(solution)/shard_map/ppermute | solution.py:450
  83.4 8.4 %shard_map.126 = (f32[4,1,128]{2,1,0:T(1,128)S(1)}, bf16[512,1024]{1,0:T(8,128)(2,1)S(1)}, bf16[64,512]{1,0:T(8,128)(2,1)S(1)}) custom-call(s32[3]{0:T(128)S(1)} %pad_add_fusion.info_ref.me_ref, bf16[784,512]{1,0:T(8,128)(2,1)} %collective-permute-done.15.refs_0_, bf16[784,512]{1,0:T(8,128)(2,1)S(1)} %collective-permute-done.16.refs_1_, ...), custom_call_target="tpu_custom_call" | custom-call | flops 4000000000 | bytes 4000000 | tf_op jit(solution)/shard_map/pallas_call | solution.py:356
  93.4 4.3 %collective-permute-done.9 = bf16[384,512]{1,0:T(8,128)(2,1)S(1)} collective-permute-done((bf16[384,512]{1,0:T(8,128)(2,1)S(1)}, bf16[384,512]{1,0:T(8,128)(2,1)S(1)}, u32[]{:S(2)}, u32[]{:S(2)}) %collective-permute-start.9) | collective-permute-done | bytes 393248 | tf_op jit(solution)/shard_map/ppermute | solution.py:450
  98.3 2.7 %collective-permute-done.26 = f32[256,1024]{1,0:T(8,128)S(1)} collective-permute-done((f32[256,1024]{1,0:T(8,128)S(1)}, f32[256,1024]{1,0:T(8,128)S(1)}, u32[]{:S(2)}, u32[]{:S(2)}) %collective-permute-start.26) | collective-permute-done | bytes 1048608 | tf_op jit(solution)/shard_map/ppermute | solution.py:450
  101.2 6.8 %collective-permute-start.27 = (bf16[128,1024]{1,0:T(8,128)(2,1)S(1)}, bf16[128,1024]{1,0:T(8,128)(2,1)S(1)}, u32[]{:S(2)}, u32[]{:S(2)}) collective-permute-start(bf16[128,1024]{1,0:T(8,128)(2,1)S(1)} %get-tuple-element.39), channel_id=1, source_target_pairs={{0,4},{1,5},{2,6},{3,7},{4,0},{5,1},{6,2},{7,3},{8,12},{9,13},{10,... | collective-permute-start | bytes 786440 | tf_op jit(solution)/shard_map/ppermute | solution.py:450
  108.0 6.7 %shard_map.127.refs_10_ = f32[4,1,128]{2,1,0:T(1,128)S(1)} custom-call(s32[3]{0:T(128)S(1)} %pad_add_fusion.info_ref.me_ref, bf16[784,512]{1,0:T(8,128)(2,1)S(1)} %collective-permute-done.8.refs_0_, bf16[784,512]{1,0:T(8,128)(2,1)S(1)} %collective-permute-done.18.refs_1_, bf16[400,512]{1,0:T(8,128)(2,1)S(1)} %slice_select_fusion.refs_2_, ...), custom_call_target="tpu_custom_call" | custom-call | flops 2800000000 | bytes 4000000 | tf_op jit(solution)/shard_map/pallas_call | solution.py:356
  115.1 1.7 %collective-permute-start.28 = (bf16[64,1024]{1,0:T(8,128)(2,1)S(1)}, bf16[64,1024]{1,0:T(8,128)(2,1)S(1)}, u32[]{:S(2)}, u32[]{:S(2)}) collective-permute-start(bf16[64,1024]{1,0:T(8,128)(2,1)S(1)} %get-tuple-element.41), channel_id=1, source_target_pairs={{0,8},{1,9},{2,10},{3,11},{4,12},{5,13},{6,14},{7,15},{8,0},{9,1},... | collective-permute-start | bytes 393224 | tf_op jit(solution)/shard_map/ppermute | solution.py:450
  116.8 3.9 %shard_map.128 = f32[24,128]{1,0:T(8,128)S(1)} custom-call(s32[3]{0:T(128)S(1)} %pad_add_fusion.info_ref.me_ref, bf16[400,512]{1,0:T(8,128)(2,1)S(1)} %collective-permute-done.4.refs_0_.refs_6_, bf16[384,512]{1,0:T(8,128)(2,1)S(1)} %broadcast_select_fusion.1.refs_1_.refs_7_, bf16[400,512]{1,0:T(8,128)(2,1)S(1)} %collective-permute-done.10.refs_2_.refs_8_, ...), custom_call_target="tpu_custom_call" | custom-call | flops 1400000000 | bytes 2000000 | tf_op jit(solution)/shard_map/pallas_call | solution.py:356
  122.0 2.3 %collective-permute-start.22 = (f32[24,128]{1,0:T(8,128)S(1)}, f32[24,128]{1,0:T(8,128)S(1)}, u32[]{:S(2)}, u32[]{:S(2)}) collective-permute-start(f32[24,128]{1,0:T(8,128)S(1)} %add.43), channel_id=1, source_target_pairs={{0,2},{1,3},{2,0},{3,1},{4,6},{5,7},{6,4},{7,5},{8,10},{9,11},{10,... | collective-permute-start | bytes 36872 | tf_op jit(solution)/shard_map/ppermute | solution.py:450
  124.3 1.7 %collective-permute-done.22 = f32[24,128]{1,0:T(8,128)S(1)} collective-permute-done((f32[24,128]{1,0:T(8,128)S(1)}, f32[24,128]{1,0:T(8,128)S(1)}, u32[]{:S(2)}, u32[]{:S(2)}) %collective-permute-start.22) | collective-permute-done | bytes 12320 | tf_op jit(solution)/shard_map/ppermute | solution.py:450
  126.3 3.4 %collective-permute-done.23 = f32[24,128]{1,0:T(8,128)S(1)} collective-permute-done((f32[24,128]{1,0:T(8,128)S(1)}, f32[24,128]{1,0:T(8,128)S(1)}, u32[]{:S(2)}, u32[]{:S(2)}) %collective-permute-start.23) | collective-permute-done | bytes 12320 | tf_op jit(solution)/shard_map/ppermute | solution.py:450
  131.0 2.1 %collective-permute-start.29 = (bf16[32,1024]{1,0:T(8,128)(2,1)S(1)}, bf16[32,1024]{1,0:T(8,128)(2,1)S(1)}, u32[]{:S(2)}, u32[]{:S(2)}) collective-permute-start(bf16[32,1024]{1,0:T(8,128)(2,1)S(1)} %fusion.2), channel_id=1, source_target_pairs={{0,2},{1,3},{2,0},{3,1},{4,6},{5,7},{6,4},{7,5},{8,10},{9,11},{10,... | collective-permute-start | bytes 196616 | tf_op jit(solution)/shard_map/ppermute | solution.py:450
  133.1 2.9 %shard_map.129 = (bf16[768,1024]{1,0:T(8,128)(2,1)S(1)}, bf16[64,768]{1,0:T(8,128)(2,1)S(1)}) custom-call(s32[3]{0:T(128)S(1)} %pad_add_fusion.info_ref.me_ref, bf16[784,512]{1,0:T(8,128)(2,1)S(1)} %collective-permute-done.8.refs_0_, bf16[784,512]{1,0:T(8,128)(2,1)S(1)} %collective-permute-done.18.refs_1_, bf16[400,512]{1,0:T(8,128)(2,1)S(1)} %slice_select_fusion.refs_2_, ...), custom_call_target="tpu_custom_call" | custom-call | flops 1800000000 | bytes 6000000 | tf_op jit(solution)/shard_map/pallas_call | solution.py:356
  136.1 2.2 %shard_map.130.a_ref = f32[72,1024]{1,0:T(8,128)S(1)} custom-call(s32[3]{0:T(128)S(1)} %pad_add_fusion.info_ref.me_ref, f32[24,128]{1,0:T(8,128)S(1)} %add.46.got_ref, bf16[1,1024]{1,0:T(2,128)(2,1)S(1)} %reshape.23.s_ref, f32[32,1024]{1,0:T(8,128)S(1)} %fusion.3.base_ref, bf16[64,256]{1,0:T(8,128)(2,1)S(1)} %get-tuple-element.26.refs_0_, ...), custom_call_target="tpu_custom_call" | custom-call | flops 1000000000 | bytes 6000000 | tf_op jit(solution)/shard_map/pallas_call | solution.py:421
  139.8 5.2 %collective-permute-done.30.b_ref = f32[72,1024]{1,0:T(8,128)S(1)} collective-permute-done((f32[72,1024]{1,0:T(8,128)S(1)}, f32[72,1024]{1,0:T(8,128)S(1)}, u32[]{:S(2)}, u32[]{:S(2)}) %collective-permute-start.30) | collective-permute-done | bytes 294944 | tf_op jit(solution)/shard_map/ppermute | solution.py:450
  (97 shorter events, 34.7 us)
Async XLA Ops:
  4.2 21.3 %collective-permute-start.1 = (bf16[784,512]{1,0:T(8,128)(2,1)}, bf16[784,512]{1,0:T(8,128)(2,1)}, u32[]{:S(2)}, u32[]{:S(2)}) collective-permute-start(bf16[784,512]{1,0:T(8,128)(2,1)} %shard_map.122.refs_0_), channel_id=1, source_target_pairs={{0,4},{1,5},{2,6},{3,7},{4,0},{5,1},{6,2},{7,3},{8,12},{9,13},{10,... | collective-permute-start | bytes 2408456 | tf_op jit(solution)/shard_map/ppermute | solution.py:450
  7.3 19.8 %collective-permute-start = (bf16[784,512]{1,0:T(8,128)(2,1)}, bf16[784,512]{1,0:T(8,128)(2,1)}, u32[]{:S(2)}, u32[]{:S(2)}) collective-permute-start(bf16[784,512]{1,0:T(8,128)(2,1)} %shard_map.122.refs_0_), channel_id=1, source_target_pairs={{4,8},{5,9},{6,10},{7,11},{8,4},{9,5},{10,6},{11,7},{20,24},{21,25... | collective-permute-start | bytes 2408456 | tf_op jit(solution)/shard_map/ppermute | solution.py:450
  18.8 50.4 %collective-permute-start.25 = (f32[512,1024]{1,0:T(8,128)}, f32[512,1024]{1,0:T(8,128)}, u32[]{:S(2)}, u32[]{:S(2)}) collective-permute-start(f32[512,1024]{1,0:T(8,128)} %get-tuple-element.25), channel_id=1, source_target_pairs={{0,1},{1,0},{2,3},{3,2},{4,5},{5,4},{6,7},{7,6},{8,9},{9,8},{10,11... | collective-permute-start | bytes 6291464 | tf_op jit(solution)/shard_map/ppermute | solution.py:450
  18.8 20.4 %collective-permute-start.5 = (bf16[784,512]{1,0:T(8,128)(2,1)S(1)}, bf16[784,512]{1,0:T(8,128)(2,1)}, u32[]{:S(2)}, u32[]{:S(2)}) collective-permute-start(bf16[784,512]{1,0:T(8,128)(2,1)S(1)} %copy-done.4), channel_id=1, source_target_pairs={{0,2},{1,3},{2,0},{3,1},{4,6},{5,7},{6,4},{7,5},{8,10},{9,11},{10,... | collective-permute-start | bytes 2408456 | tf_op jit(solution)/shard_map/ppermute | solution.py:450
  20.3 18.9 %collective-permute-start.12 = (bf16[784,512]{1,0:T(8,128)(2,1)S(1)}, bf16[784,512]{1,0:T(8,128)(2,1)S(1)}, u32[]{:S(2)}, u32[]{:S(2)}) collective-permute-start(bf16[784,512]{1,0:T(8,128)(2,1)S(1)} %copy-done.4), channel_id=1, source_target_pairs={{0,1},{1,0},{2,3},{3,2},{4,5},{5,4},{6,7},{7,6},{8,9},{9,8},{10,11... | collective-permute-start | bytes 2408456 | tf_op jit(solution)/shard_map/ppermute | solution.py:450
  25.5 14.2 %collective-permute-start.2 = (bf16[784,512]{1,0:T(8,128)(2,1)}, bf16[784,512]{1,0:T(8,128)(2,1)}, u32[]{:S(2)}, u32[]{:S(2)}) collective-permute-start(bf16[784,512]{1,0:T(8,128)(2,1)} %collective-permute-done.1.refs_2_), channel_id=1, source_target_pairs={{4,8},{5,9},{6,10},{7,11},{8,4},{9,5},{10,6},{11,7},{20,24},{21,25... | collective-permute-start | bytes 2408456 | tf_op jit(solution)/shard_map/ppermute | solution.py:450
  27.1 25.5 %collective-permute-start.7 = (bf16[784,512]{1,0:T(8,128)(2,1)}, bf16[784,512]{1,0:T(8,128)(2,1)}, u32[]{:S(2)}, u32[]{:S(2)}) collective-permute-start(bf16[784,512]{1,0:T(8,128)(2,1)} %collective-permute-done), channel_id=1, source_target_pairs={{4,0},{5,1},{6,2},{7,3},{8,12},{9,13},{10,14},{11,15},{20,16},{21,... | collective-permute-start | bytes 2408456 | tf_op jit(solution)/shard_map/ppermute | solution.py:450
  39.2 16.1 %collective-permute-start.13 = (bf16[784,512]{1,0:T(8,128)(2,1)}, bf16[784,512]{1,0:T(8,128)(2,1)}, u32[]{:S(2)}, u32[]{:S(2)}) collective-permute-start(bf16[784,512]{1,0:T(8,128)(2,1)} %collective-permute-done.5.refs_0_), channel_id=1, source_target_pairs={{0,1},{1,0},{2,3},{3,2},{4,5},{5,4},{6,7},{7,6},{8,9},{9,8},{10,11... | collective-permute-start | bytes 2408456 | tf_op jit(solution)/shard_map/ppermute | solution.py:450
  39.2 16.6 %collective-permute-start.14 = (bf16[784,512]{1,0:T(8,128)(2,1)}, bf16[784,512]{1,0:T(8,128)(2,1)}, u32[]{:S(2)}, u32[]{:S(2)}) collective-permute-start(bf16[784,512]{1,0:T(8,128)(2,1)} %collective-permute-done.1.refs_2_), channel_id=1, source_target_pairs={{0,1},{1,0},{2,3},{3,2},{4,5},{5,4},{6,7},{7,6},{8,9},{9,8},{10,11... | collective-permute-start | bytes 2408456 | tf_op jit(solution)/shard_map/ppermute | solution.py:450
  39.7 21.1 %collective-permute-start.15 = (bf16[784,512]{1,0:T(8,128)(2,1)}, bf16[784,512]{1,0:T(8,128)(2,1)}, u32[]{:S(2)}, u32[]{:S(2)}) collective-permute-start(bf16[784,512]{1,0:T(8,128)(2,1)} %collective-permute-done.1.refs_2_), channel_id=1, source_target_pairs={{0,2},{1,3},{2,0},{3,1},{4,6},{5,7},{6,4},{7,5},{8,10},{9,11},{10,... | collective-permute-start | bytes 2408456 | tf_op jit(solution)/shard_map/ppermute | solution.py:450
  52.6 26.0 %collective-permute-start.3 = (bf16[784,512]{1,0:T(8,128)(2,1)}, bf16[784,512]{1,0:T(8,128)(2,1)S(1)}, u32[]{:S(2)}, u32[]{:S(2)}) collective-permute-start(bf16[784,512]{1,0:T(8,128)(2,1)} %collective-permute-done.2), channel_id=1, source_target_pairs={{4,0},{5,1},{6,2},{7,3},{8,12},{9,13},{10,14},{11,15},{20,16},{21,... | collective-permute-start | bytes 2408456 | tf_op jit(solution)/shard_map/ppermute | solution.py:450
  55.3 25.9 %collective-permute-start.8 = (bf16[784,512]{1,0:T(8,128)(2,1)S(1)}, bf16[784,512]{1,0:T(8,128)(2,1)S(1)}, u32[]{:S(2)}, u32[]{:S(2)}) collective-permute-start(bf16[784,512]{1,0:T(8,128)(2,1)S(1)} %broadcast_select_fusion.refs_2_), channel_id=1, source_target_pairs={{0,2},{1,3},{2,0},{3,1},{4,6},{5,7},{6,4},{7,5},{8,10},{9,11},{10,... | collective-permute-start | bytes 2408456 | tf_op jit(solution)/shard_map/ppermute | solution.py:450
  55.9 27.4 %collective-permute-start.17 = (bf16[784,512]{1,0:T(8,128)(2,1)S(1)}, bf16[784,512]{1,0:T(8,128)(2,1)S(1)}, u32[]{:S(2)}, u32[]{:S(2)}) collective-permute-start(bf16[784,512]{1,0:T(8,128)(2,1)S(1)} %broadcast_select_fusion.refs_2_), channel_id=1, source_target_pairs={{0,1},{1,0},{2,3},{3,2},{4,5},{5,4},{6,7},{7,6},{8,9},{9,8},{10,11... | collective-permute-start | bytes 2408456 | tf_op jit(solution)/shard_map/ppermute | solution.py:450
  60.8 21.0 %collective-permute-start.16 = (bf16[784,512]{1,0:T(8,128)(2,1)}, bf16[784,512]{1,0:T(8,128)(2,1)S(1)}, u32[]{:S(2)}, u32[]{:S(2)}) collective-permute-start(bf16[784,512]{1,0:T(8,128)(2,1)} %collective-permute-done.15.refs_0_), channel_id=1, source_target_pairs={{0,1},{1,0},{2,3},{3,2},{4,5},{5,4},{6,7},{7,6},{8,9},{9,8},{10,11... | collective-permute-start | bytes 2408456 | tf_op jit(solution)/shard_map/ppermute | solution.py:450
  69.2 23.6 %collective-permute-start.6 = (bf16[384,512]{1,0:T(8,128)(2,1)S(1)}, bf16[384,512]{1,0:T(8,128)(2,1)S(1)}, u32[]{:S(2)}, u32[]{:S(2)}) collective-permute-start(bf16[384,512]{1,0:T(8,128)(2,1)S(1)} %slice.90), channel_id=1, source_target_pairs={{4,8},{5,9},{6,10},{7,11},{8,4},{9,5},{10,6},{11,7},{20,24},{21,25... | collective-permute-start | bytes 1179656 | tf_op jit(solution)/shard_map/ppermute | solution.py:450
  78.6 22.3 %collective-permute-start.26 = (f32[256,1024]{1,0:T(8,128)S(1)}, f32[256,1024]{1,0:T(8,128)S(1)}, u32[]{:S(2)}, u32[]{:S(2)}) collective-permute-start(f32[256,1024]{1,0:T(8,128)S(1)} %get-tuple-element.37), channel_id=1, source_target_pairs={{0,16},{16,0},{1,17},{17,1},{2,18},{18,2},{3,19},{19,3},{4,20},{20... | collective-permute-start | bytes 3145736 | tf_op jit(solution)/shard_map/ppermute | solution.py:450
  81.2 16.5 %collective-permute-start.4 = (bf16[400,512]{1,0:T(8,128)(2,1)S(1)}, bf16[400,512]{1,0:T(8,128)(2,1)S(1)}, u32[]{:S(2)}, u32[]{:S(2)}) collective-permute-start(bf16[400,512]{1,0:T(8,128)(2,1)S(1)} %slice_select_fusion.refs_2_), channel_id=1, source_target_pairs={{0,2},{1,3},{2,0},{3,1},{4,6},{5,7},{6,4},{7,5},{8,10},{9,11},{10,... | collective-permute-start | bytes 1228808 | tf_op jit(solution)/shard_map/ppermute | solution.py:450
  81.8 15.8 %collective-permute-start.9 = (bf16[384,512]{1,0:T(8,128)(2,1)S(1)}, bf16[384,512]{1,0:T(8,128)(2,1)S(1)}, u32[]{:S(2)}, u32[]{:S(2)}) collective-permute-start(bf16[384,512]{1,0:T(8,128)(2,1)S(1)} %slice.91), channel_id=1, source_target_pairs={{4,0},{5,1},{6,2},{7,3},{8,12},{9,13},{10,14},{11,15},{20,16},{21,... | collective-permute-start | bytes 1179656 | tf_op jit(solution)/shard_map/ppermute | solution.py:450
  83.3 24.7 %collective-permute-start.18 = (bf16[784,512]{1,0:T(8,128)(2,1)S(1)}, bf16[784,512]{1,0:T(8,128)(2,1)S(1)}, u32[]{:S(2)}, u32[]{:S(2)}) collective-permute-start(bf16[784,512]{1,0:T(8,128)(2,1)S(1)} %collective-permute-done.8.refs_0_), channel_id=1, source_target_pairs={{0,1},{1,0},{2,3},{3,2},{4,5},{5,4},{6,7},{7,6},{8,9},{9,8},{10,11... | collective-permute-start | bytes 2408456 | tf_op jit(solution)/shard_map/ppermute | solution.py:450
  92.8 15.2 %collective-permute-start.19 = (bf16[400,512]{1,0:T(8,128)(2,1)S(1)}, bf16[400,512]{1,0:T(8,128)(2,1)S(1)}, u32[]{:S(2)}, u32[]{:S(2)}) collective-permute-start(bf16[400,512]{1,0:T(8,128)(2,1)S(1)} %slice_select_fusion.refs_2_), channel_id=1, source_target_pairs={{0,1},{1,0},{2,3},{3,2},{4,5},{5,4},{6,7},{7,6},{8,9},{9,8},{10,11... | collective-permute-start | bytes 1228808 | tf_op jit(solution)/shard_map/ppermute | solution.py:450
  97.7 19.1 %collective-permute-start.11 = (bf16[384,512]{1,0:T(8,128)(2,1)S(1)}, bf16[384,512]{1,0:T(8,128)(2,1)S(1)}, u32[]{:S(2)}, u32[]{:S(2)}) collective-permute-start(bf16[384,512]{1,0:T(8,128)(2,1)S(1)} %broadcast_select_fusion.1.refs_1_.refs_7_), channel_id=1, source_target_pairs={{0,1},{1,0},{2,3},{3,2},{4,5},{5,4},{6,7},{7,6},{8,9},{9,8},{10,11... | collective-permute-start | bytes 1179656 | tf_op jit(solution)/shard_map/ppermute | solution.py:450
  101.0 15.8 %collective-permute-start.10 = (bf16[400,512]{1,0:T(8,128)(2,1)S(1)}, bf16[400,512]{1,0:T(8,128)(2,1)S(1)}, u32[]{:S(2)}, u32[]{:S(2)}) collective-permute-start(bf16[400,512]{1,0:T(8,128)(2,1)S(1)} %collective-permute-done.4.refs_0_.refs_6_), channel_id=1, source_target_pairs={{0,1},{1,0},{2,3},{3,2},{4,5},{5,4},{6,7},{7,6},{8,9},{9,8},{10,11... | collective-permute-start | bytes 1228808 | tf_op jit(solution)/shard_map/ppermute | solution.py:450
  101.2 13.8 %collective-permute-start.27 = (bf16[128,1024]{1,0:T(8,128)(2,1)S(1)}, bf16[128,1024]{1,0:T(8,128)(2,1)S(1)}, u32[]{:S(2)}, u32[]{:S(2)}) collective-permute-start(bf16[128,1024]{1,0:T(8,128)(2,1)S(1)} %get-tuple-element.39), channel_id=1, source_target_pairs={{0,4},{1,5},{2,6},{3,7},{4,0},{5,1},{6,2},{7,3},{8,12},{9,13},{10,... | collective-permute-start | bytes 786440 | tf_op jit(solution)/shard_map/ppermute | solution.py:450
  115.1 15.9 %collective-permute-start.28 = (bf16[64,1024]{1,0:T(8,128)(2,1)S(1)}, bf16[64,1024]{1,0:T(8,128)(2,1)S(1)}, u32[]{:S(2)}, u32[]{:S(2)}) collective-permute-start(bf16[64,1024]{1,0:T(8,128)(2,1)S(1)} %get-tuple-element.41), channel_id=1, source_target_pairs={{0,8},{1,9},{2,10},{3,11},{4,12},{5,13},{6,14},{7,15},{8,0},{9,1},... | collective-permute-start | bytes 393224 | tf_op jit(solution)/shard_map/ppermute | solution.py:450
  (22 other events, 107.4 us)
where the time goes:
time: 147 us; the launch traced here: 146 us
  Pallas kernels  48 us (33%)
  waiting for transfers between devices  46.3 us (31%)
  starting transfers between devices  34.8 us (24%)
  local copies, waits for them, and re-layouts  9.84 us (7%)
  other arithmetic  5.77 us (4%)
    ppermute x31, waiting for transfers between devices, shift(): return lax.ppermute(x, axis, table)  46.3 us
    ppermute x31, starting transfers between devices, shift(): return lax.ppermute(x, axis, table)  34.8 us
    pallas_call x6, Pallas kernels, rank(): pl.pallas_call(functools.partial(rank_kernel, dims, sel_rows, layout, (wa...  34.3 us
    unnamed x30, local copies, waits for them, and re-layouts  8.79 us
    pallas_call x1, Pallas kernels, student_part(): pl.pallas_call(functools.partial(student_kernel, requests, feats // piece...  7.25 us
    pallas_call x1, Pallas kernels, pack(): pl.pallas_call(pack_kernel, out_shape=jax.ShapeDtypeStruct((total, focus)...  3.54 us
  transfers between devices with their start and end apart: 31, of which 11 were waited for; matrix products, arithmetic and copies ran while one was open for 5% of the time, Pallas kernels for 28%

commit v1 on v0

--- a/solution.py
+++ b/solution.py
@@ -94,7 +94,7 @@
         out_specs=full_vmem(),
         scratch_shapes=[VMEM(x.shape, BF16), pltpu.SemaphoreType.DMA((requests + 1,))],
         cost_estimate=pl.CostEstimate(flops=10**8, bytes_accessed=3 * 10**6, transcendentals=0),
-    )(targets, extents, stays(x), kept, stays(flat_hist))
+    )(targets, extents, stays(x), stays(kept), stays(flat_hist))
 
 
 def student_kernel(requests, chunk, order, me_ref, x_ref, w_ref, s_ref, c_ref, e_ref, *refs):
@@ -372,7 +372,7 @@
 
 def target_kernel(kept, tops, n_parts, me_ref, got_ref, s_ref, base_ref, *refs):
     sel_refs, hid_refs = refs[:n_parts], refs[n_parts : 2 * n_parts]
-    out_ref, target_ref = refs[2 * n_parts :]
+    out_ref, short_ref, target_ref = refs[2 * n_parts :]
     kept_rows = got_ref.shape[1]
     units = s_ref.shape[1]
     blocks = got_ref.shape[0] - units // kept_rows
@@ -398,8 +398,13 @@
         hidden = hid_ref[...]
         slot += count
         live = jnp.where(hidden > 0, jnp.ones((), BF16), jnp.zeros((), BF16))
-        scaled = (sel_ref[...].astype(F32) * target).astype(BF16)
-        grad += jnp.dot(scaled, live, preferred_element_type=F32)
+        scaled = sel_ref[...].astype(F32) * target
+        upper = scaled.astype(BF16)
+        lower = (scaled - upper.astype(F32)).astype(BF16)
+        halves = jnp.dot(
+            jnp.concatenate([upper, lower], axis=0), live, preferred_element_type=F32
+        )
+        grad += halves[:sel_rows, :] + halves[sel_rows:, :]
         both = jnp.concatenate([high, target - high], axis=0).astype(BF16)
         pair = jnp.dot(both, hidden, preferred_element_type=F32)
         lift += pair[0:1, :] + pair[1:2, :]
@@ -411,6 +416,9 @@
         at = slice(i * kept_rows, (i + 1) * kept_rows)
         out_ref[sel_rows : sel_rows + 1, at] = total[blocks + i : blocks + i + 1, :] - lift[:, at]
     out_ref[sel_rows + 1 :, :] = jnp.zeros((out_ref.shape[0] - sel_rows - 1, units), F32)
+    row = out_ref[sel_rows : sel_rows + 1, :]
+    short_ref[...] = out_ref[...].astype(BF16)
+    short_ref[sel_rows + 1 : sel_rows + 2, :] = (row - row.astype(BF16).astype(F32)).astype(BF16)
 
 
 def target_part(kept, tops, me, got, hiddens, owns, s, base):
@@ -420,9 +428,9 @@
     parts = len(hiddens)
     return pl.pallas_call(
         functools.partial(target_kernel, kept, tops, parts),
-        out_shape=jax.ShapeDtypeStruct((sel_rows + 8, units), F32),
+        out_shape=tuple(jax.ShapeDtypeStruct((sel_rows + 16, units), t) for t in (F32, BF16)),
         in_specs=[scalars()] + [full_vmem()] * (3 + 2 * parts),
-        out_specs=full_vmem(),
+        out_specs=(full_vmem(),) * 2,
         scratch_shapes=[VMEM((blocks, got.shape[1]), F32)],
         compiler_params=room(22),
         cost_estimate=pl.CostEstimate(flops=10**9, bytes_accessed=6 * 10**6, transcendentals=0),
@@ -472,8 +480,7 @@
         return [list(pieces), [shift(p, SIBLING) for p in pieces]]
 
     return [
-        both(b),
-        both(over) + both(near),
+        both(b) + both(over) + both(near),
         both(over_near) + both(far),
         both(over_far) + both(*last),
         both(over_last, over_rest),
@@ -510,8 +517,9 @@
 
 def sum_kernel(a_ref, b_ref, grad_ref, score_ref):
     rows = grad_ref.shape[0]
-    grad_ref[...] = a_ref[:rows, :] + b_ref[:rows, :]
-    score_ref[...] = a_ref[rows : rows + 1, :] + b_ref[rows : rows + 1, :]
+    grad_ref[...] = a_ref[:rows, :] + b_ref[:rows, :].astype(F32)
+    pair = b_ref[rows : rows + 2, :].astype(F32)
+    score_ref[...] = a_ref[rows : rows + 1, :] + (pair[0:1, :] + pair[1:2, :])
 
 
 def sum_two(a, b, rows):
@@ -603,9 +611,9 @@
     hiddens.append(hidden)
     owns.append(own)
     got = sum_over_shard(send) if linked else lax.psum(send, "shard")
-    mine = target_part(kept, tops, info, got, hiddens, owns, student_rating_vector, base)
+    mine, short = target_part(kept, tops, info, got, hiddens, owns, student_rating_vector, base)
     if linked:
-        grad, lift = sum_two(mine, shift(mine, [(0, 1), (1, 0)], "group"), sel_rows)
+        grad, lift = sum_two(mine, shift(short, [(0, 1), (1, 0)], "group"), sel_rows)
         return grad, lift.reshape(units)
     whole = lax.psum(mine, "group")
     return whole[:sel_rows], whole[sel_rows]

time: 147 us -> 150 us (1.020)
  waiting for transfers between devices: 46.3 us -> 59.3 us
  local copies, waits for them, and re-layouts: 9.84 us -> 4.88 us
  starting transfers between devices: 34.8 us -> 31.3 us
    ppermute x31, waiting for transfers between devices: 46.3 us -> 59.3 us  [shift(): return lax.ppermute(x, axis, table)]
    unnamed x30 -> x18, local copies, waits for them, and re-layouts: 8.79 us -> 3.69 us
    ppermute x31, starting transfers between devices: 34.8 us -> 31.3 us  [shift(): return lax.ppermute(x, axis, table)]
    pallas_call x6 -> x5, Pallas kernels: 34.3 us -> 33.4 us  [rank(): pl.pallas_call(functools.partial(rank_kernel, dims, sel_rows, layout, (wa...]
  transfers between devices with their start and end apart: 31 -> 31, of which waited for: 11 -> 10; matrix products, arithmetic and copies ran while one was open for 5% -> 5% of each run, Pallas kernels for 28% -> 27%
where the time goes in v1:
time: 150 us; the launch traced here: 149 us
  waiting for transfers between devices  59.3 us (40%)
  Pallas kernels  47.1 us (31%)
  starting transfers between devices  31.3 us (21%)
  other arithmetic  5.76 us (4%)
  local copies, waits for them, and re-layouts  4.88 us (3%)
    ppermute x31, waiting for transfers between devices, shift(): return lax.ppermute(x, axis, table)  59.3 us
    pallas_call x5, Pallas kernels, rank(): pl.pallas_call(functools.partial(rank_kernel, dims, sel_rows, layout, (wa...  33.4 us
    ppermute x31, starting transfers between devices, shift(): return lax.ppermute(x, axis, table)  31.3 us
    pallas_call x1, Pallas kernels, student_part(): pl.pallas_call(functools.partial(student_kernel, requests, feats // piece...  7.25 us
    unnamed x18, local copies, waits for them, and re-layouts  3.69 us
    pallas_call x1, Pallas kernels, pack(): pl.pallas_call(pack_kernel, out_shape=jax.ShapeDtypeStruct((total, focus)...  3.57 us
  transfers between devices with their start and end apart: 31, of which 10 were waited for; matrix products, arithmetic and copies ran while one was open for 5% of the time, Pallas kernels for 27%

profile of v1, /device:TPU:0, one launch (start us, length us, event | category | flops | bytes accessed | tf_op | source)
XLA Modules:
  0.0 149.3 jit_solution(16546702822197107541)
XLA Ops:
  0.7 3.6 %shard_map.122.refs_0_ = bf16[784,512]{1,0:T(8,128)(2,1)} custom-call(s32[4,6]{1,0:T(4,128)} %target_ref.1, s32[4]{0:T(128)} %extent_ref.1, bf16[4,128,1024]{2,1,0:T(8,128)(2,1)} %x_hbm.1, s32[4,32]{1,0:T(4,128)} %kept_ref.1, bf16[512,512]{1,0:T(8,128)(2,1)} %bitcast.19), custom_call_target="tpu_custom_call" | custom-call | flops 100000000 | bytes 3000000 | tf_op jit(solution)/shard_map/pallas_call | solution.py:90
  4.2 3.1 %collective-permute-start.1 = (bf16[784,512]{1,0:T(8,128)(2,1)}, bf16[784,512]{1,0:T(8,128)(2,1)}, u32[]{:S(2)}, u32[]{:S(2)}) collective-permute-start(bf16[784,512]{1,0:T(8,128)(2,1)} %shard_map.122.refs_0_), channel_id=1, source_target_pairs={{0,4},{1,5},{2,6},{3,7},{4,0},{5,1},{6,2},{7,3},{8,12},{9,13},{10,... | collective-permute-start | bytes 2408456 | tf_op jit(solution)/shard_map/ppermute | solution.py:458
  7.4 1.6 %collective-permute-start = (bf16[784,512]{1,0:T(8,128)(2,1)}, bf16[784,512]{1,0:T(8,128)(2,1)}, u32[]{:S(2)}, u32[]{:S(2)}) collective-permute-start(bf16[784,512]{1,0:T(8,128)(2,1)} %shard_map.122.refs_0_), channel_id=1, source_target_pairs={{4,8},{5,9},{6,10},{7,11},{8,4},{9,5},{10,6},{11,7},{20,24},{21,25... | collective-permute-start | bytes 2408456 | tf_op jit(solution)/shard_map/ppermute | solution.py:458
  10.5 15.1 %collective-permute-done.1.refs_4_ = bf16[784,512]{1,0:T(8,128)(2,1)} collective-permute-done((bf16[784,512]{1,0:T(8,128)(2,1)}, bf16[784,512]{1,0:T(8,128)(2,1)}, u32[]{:S(2)}, u32[]{:S(2)}) %collective-permute-start.1) | collective-permute-done | bytes 802848 | tf_op jit(solution)/shard_map/ppermute | solution.py:458
  25.6 1.6 %collective-permute-start.2 = (bf16[784,512]{1,0:T(8,128)(2,1)}, bf16[784,512]{1,0:T(8,128)(2,1)}, u32[]{:S(2)}, u32[]{:S(2)}) collective-permute-start(bf16[784,512]{1,0:T(8,128)(2,1)} %collective-permute-done.1.refs_4_), channel_id=1, source_target_pairs={{4,8},{5,9},{6,10},{7,11},{8,4},{9,5},{10,6},{11,7},{20,24},{21,25... | collective-permute-start | bytes 2408456 | tf_op jit(solution)/shard_map/ppermute | solution.py:458
  28.5 1.6 %copy-done = bf16[1024,1024]{1,0:T(8,128)(2,1)S(1)} copy-done((bf16[1024,1024]{1,0:T(8,128)(2,1)S(1)}, bf16[1024,1024]{1,0:T(8,128)(2,1)}, u32[]{:S(2)}) %copy-start) | copy-done | bytes 2097176
  31.1 7.2 %shard_map.123 = (f32[512,1024]{1,0:T(8,128)S(1)}, f32[512,1024]{1,0:T(8,128)}, f32[1,1024]{1,0:T(1,128)S(1)}, bf16[512,256]{1,0:T(8,128)(2,1)S(1)}) custom-call(s32[1]{0:T(128)} %bitcast.5.me_ref, bf16[512,1024]{1,0:T(8,128)(2,1)S(1)} %bitcast.9, bf16[1024,1024]{1,0:T(8,128)(2,1)S(1)} %copy-done, bf16[1,1024]{1,0:T(2,128)(2,1)S(1)} %reshape.23.s_ref, ...), custom_call_target="tpu_custom_call" | custom-call | flops 2147483648 | bytes 8000000 | tf_op jit(solution)/shard_map/pallas_call | solution.py:158
  39.4 9.8 %collective-permute-done.7 = bf16[784,512]{1,0:T(8,128)(2,1)} collective-permute-done((bf16[784,512]{1,0:T(8,128)(2,1)}, bf16[784,512]{1,0:T(8,128)(2,1)}, u32[]{:S(2)}, u32[]{:S(2)}) %collective-permute-start.7) | collective-permute-done | bytes 802848 | tf_op jit(solution)/shard_map/ppermute | solution.py:458
  55.0 15.2 %collective-permute-done.15.refs_0_ = bf16[784,512]{1,0:T(8,128)(2,1)} collective-permute-done((bf16[784,512]{1,0:T(8,128)(2,1)}, bf16[784,512]{1,0:T(8,128)(2,1)}, u32[]{:S(2)}, u32[]{:S(2)}) %collective-permute-start.15) | collective-permute-done | bytes 802848 | tf_op jit(solution)/shard_map/ppermute | solution.py:458
  71.3 11.6 %shard_map.124 = (f32[6,1,128]{2,1,0:T(1,128)S(1)}, bf16[768,1024]{1,0:T(8,128)(2,1)S(1)}, bf16[64,768]{1,0:T(8,128)(2,1)S(1)}) custom-call(s32[3]{0:T(128)S(1)} %pad_add_fusion.info_ref.me_ref, bf16[784,512]{1,0:T(8,128)(2,1)} %shard_map.122.refs_0_, bf16[784,512]{1,0:T(8,128)(2,1)} %collective-permute-done.12.refs_1_, ...), custom_call_target="tpu_custom_call" | custom-call | flops 6000000000 | bytes 6000000 | tf_op jit(solution)/shard_map/pallas_call | solution.py:356
  83.6 2.0 %slice_add_fusion.1 = (f32[256,1024]{1,0:T(8,128)S(1)}, f32[256,1024]{1,0:T(8,128)S(1)}) fusion(f32[512,1024]{1,0:T(8,128)} %collective-permute-done.25, f32[512,1024]{1,0:T(8,128)S(1)} %get-tuple-element.22), kind=kLoop, calls=%fused_computation.1 | loop fusion | flops 524288 | bytes 6291456 | tf_op jit(solution)/shard_map/add | solution.py:509
  85.6 1.6 %collective-permute-start.26 = (f32[256,1024]{1,0:T(8,128)S(1)}, f32[256,1024]{1,0:T(8,128)S(1)}, u32[]{:S(2)}, u32[]{:S(2)}) collective-permute-start(f32[256,1024]{1,0:T(8,128)S(1)} %get-tuple-element.35), channel_id=1, source_target_pairs={{0,16},{16,0},{1,17},{17,1},{2,18},{18,2},{3,19},{19,3},{4,20},{20... | collective-permute-start | bytes 3145736 | tf_op jit(solution)/shard_map/ppermute | solution.py:458
  88.2 1.6 %collective-permute-start.4 = (bf16[400,512]{1,0:T(8,128)(2,1)S(1)}, bf16[400,512]{1,0:T(8,128)(2,1)S(1)}, u32[]{:S(2)}, u32[]{:S(2)}) collective-permute-start(bf16[400,512]{1,0:T(8,128)(2,1)S(1)} %slice_select_fusion.refs_2_), channel_id=1, source_target_pairs={{0,2},{1,3},{2,0},{3,1},{4,6},{5,7},{6,4},{7,5},{8,10},{9,11},{10,... | collective-permute-start | bytes 1228808 | tf_op jit(solution)/shard_map/ppermute | solution.py:458
  91.4 8.3 %shard_map.125 = (f32[4,1,128]{2,1,0:T(1,128)S(1)}, bf16[512,1024]{1,0:T(8,128)(2,1)S(1)}, bf16[64,512]{1,0:T(8,128)(2,1)S(1)}) custom-call(s32[3]{0:T(128)S(1)} %pad_add_fusion.info_ref.me_ref, bf16[784,512]{1,0:T(8,128)(2,1)} %collective-permute-done.15.refs_0_, bf16[784,512]{1,0:T(8,128)(2,1)S(1)} %collective-permute-done.16.refs_1_, ...), custom_call_target="tpu_custom_call" | custom-call | flops 4000000000 | bytes 4000000 | tf_op jit(solution)/shard_map/pallas_call | solution.py:356
  103.3 7.9 %collective-permute-done.26 = f32[256,1024]{1,0:T(8,128)S(1)} collective-permute-done((f32[256,1024]{1,0:T(8,128)S(1)}, f32[256,1024]{1,0:T(8,128)S(1)}, u32[]{:S(2)}, u32[]{:S(2)}) %collective-permute-start.26) | collective-permute-done | bytes 1048608 | tf_op jit(solution)/shard_map/ppermute | solution.py:458
  111.4 2.4 %collective-permute-start.27 = (bf16[128,1024]{1,0:T(8,128)(2,1)S(1)}, bf16[128,1024]{1,0:T(8,128)(2,1)S(1)}, u32[]{:S(2)}, u32[]{:S(2)}) collective-permute-start(bf16[128,1024]{1,0:T(8,128)(2,1)S(1)} %get-tuple-element.37), channel_id=1, source_target_pairs={{0,4},{1,5},{2,6},{3,7},{4,0},{5,1},{6,2},{7,3},{8,12},{9,13},{10,... | collective-permute-start | bytes 786440 | tf_op jit(solution)/shard_map/ppermute | solution.py:458
  113.8 6.6 %shard_map.126.refs_9_ = f32[4,1,128]{2,1,0:T(1,128)S(1)} custom-call(s32[3]{0:T(128)S(1)} %pad_add_fusion.info_ref.me_ref, bf16[784,512]{1,0:T(8,128)(2,1)S(1)} %collective-permute-done.8.refs_0_, bf16[784,512]{1,0:T(8,128)(2,1)S(1)} %collective-permute-done.18.refs_1_, bf16[400,512]{1,0:T(8,128)(2,1)S(1)} %slice_select_fusion.refs_2_, ...), custom_call_target="tpu_custom_call" | custom-call | flops 2800000000 | bytes 4000000 | tf_op jit(solution)/shard_map/pallas_call | solution.py:356
  122.4 3.9 %shard_map.127 = f32[24,128]{1,0:T(8,128)S(1)} custom-call(s32[3]{0:T(128)S(1)} %pad_add_fusion.info_ref.me_ref, bf16[400,512]{1,0:T(8,128)(2,1)S(1)} %collective-permute-done.4.refs_0_.refs_6_, bf16[384,512]{1,0:T(8,128)(2,1)S(1)} %broadcast_select_fusion.1.refs_1_.refs_7_, bf16[400,512]{1,0:T(8,128)(2,1)S(1)} %collective-permute-done.10.refs_2_.refs_8_, ...), custom_call_target="tpu_custom_call" | custom-call | flops 1400000000 | bytes 2000000 | tf_op jit(solution)/shard_map/pallas_call | solution.py:356
  129.1 2.2 %collective-permute-done.22 = f32[24,128]{1,0:T(8,128)S(1)} collective-permute-done((f32[24,128]{1,0:T(8,128)S(1)}, f32[24,128]{1,0:T(8,128)S(1)}, u32[]{:S(2)}, u32[]{:S(2)}) %collective-permute-start.22) | collective-permute-done | bytes 12320 | tf_op jit(solution)/shard_map/ppermute | solution.py:458
  132.5 2.4 %collective-permute-done.23 = f32[24,128]{1,0:T(8,128)S(1)} collective-permute-done((f32[24,128]{1,0:T(8,128)S(1)}, f32[24,128]{1,0:T(8,128)S(1)}, u32[]{:S(2)}, u32[]{:S(2)}) %collective-permute-start.23) | collective-permute-done | bytes 12320 | tf_op jit(solution)/shard_map/ppermute | solution.py:458
  136.5 1.6 %collective-permute-start.29 = (bf16[32,1024]{1,0:T(8,128)(2,1)S(1)}, bf16[32,1024]{1,0:T(8,128)(2,1)S(1)}, u32[]{:S(2)}, u32[]{:S(2)}) collective-permute-start(bf16[32,1024]{1,0:T(8,128)(2,1)S(1)} %fusion.2), channel_id=1, source_target_pairs={{0,2},{1,3},{2,0},{3,1},{4,6},{5,7},{6,4},{7,5},{8,10},{9,11},{10,... | collective-permute-start | bytes 196616 | tf_op jit(solution)/shard_map/ppermute | solution.py:458
  138.1 2.9 %shard_map.128 = (bf16[768,1024]{1,0:T(8,128)(2,1)S(1)}, bf16[64,768]{1,0:T(8,128)(2,1)S(1)}) custom-call(s32[3]{0:T(128)S(1)} %pad_add_fusion.info_ref.me_ref, bf16[784,512]{1,0:T(8,128)(2,1)S(1)} %collective-permute-done.8.refs_0_, bf16[784,512]{1,0:T(8,128)(2,1)S(1)} %collective-permute-done.18.refs_1_, bf16[400,512]{1,0:T(8,128)(2,1)S(1)} %slice_select_fusion.refs_2_, ...), custom_call_target="tpu_custom_call" | custom-call | flops 1800000000 | bytes 6000000 | tf_op jit(solution)/shard_map/pallas_call | solution.py:356
  141.1 2.2 %shard_map.129 = (f32[80,1024]{1,0:T(8,128)S(1)}, bf16[80,1024]{1,0:T(8,128)(2,1)S(1)}) custom-call(s32[3]{0:T(128)S(1)} %pad_add_fusion.info_ref.me_ref, f32[24,128]{1,0:T(8,128)S(1)} %add.46.got_ref, bf16[1,1024]{1,0:T(2,128)(2,1)S(1)} %reshape.23.s_ref, f32[32,1024]{1,0:T(8,128)S(1)} %fusion.3.base_ref, bf16[64,768]{1,0:T(8,128)(2,1)S(1)} %get-tuple-element.24.refs_0_, ...), custom_call_target="tpu_custom_call" | custom-call | flops 1000000000 | bytes 6000000 | tf_op jit(solution)/shard_map/pallas_call | solution.py:429
  144.8 3.8 %collective-permute-done.30.b_ref = bf16[80,1024]{1,0:T(8,128)(2,1)S(1)} collective-permute-done((bf16[80,1024]{1,0:T(8,128)(2,1)S(1)}, bf16[80,1024]{1,0:T(8,128)(2,1)S(1)}, u32[]{:S(2)}, u32[]{:S(2)}) %collective-permute-start.30) | collective-permute-done | bytes 163872 | tf_op jit(solution)/shard_map/ppermute | solution.py:458
  (84 shorter events, 28.7 us)
Async XLA Ops:
  4.2 21.3 %collective-permute-start.1 = (bf16[784,512]{1,0:T(8,128)(2,1)}, bf16[784,512]{1,0:T(8,128)(2,1)}, u32[]{:S(2)}, u32[]{:S(2)}) collective-permute-start(bf16[784,512]{1,0:T(8,128)(2,1)} %shard_map.122.refs_0_), channel_id=1, source_target_pairs={{0,4},{1,5},{2,6},{3,7},{4,0},{5,1},{6,2},{7,3},{8,12},{9,13},{10,... | collective-permute-start | bytes 2408456 | tf_op jit(solution)/shard_map/ppermute | solution.py:458
  7.4 19.8 %collective-permute-start = (bf16[784,512]{1,0:T(8,128)(2,1)}, bf16[784,512]{1,0:T(8,128)(2,1)}, u32[]{:S(2)}, u32[]{:S(2)}) collective-permute-start(bf16[784,512]{1,0:T(8,128)(2,1)} %shard_map.122.refs_0_), channel_id=1, source_target_pairs={{4,8},{5,9},{6,10},{7,11},{8,4},{9,5},{10,6},{11,7},{20,24},{21,25... | collective-permute-start | bytes 2408456 | tf_op jit(solution)/shard_map/ppermute | solution.py:458
  8.9 29.9 %collective-permute-start.5 = (bf16[784,512]{1,0:T(8,128)(2,1)}, bf16[784,512]{1,0:T(8,128)(2,1)}, u32[]{:S(2)}, u32[]{:S(2)}) collective-permute-start(bf16[784,512]{1,0:T(8,128)(2,1)} %shard_map.122.refs_0_), channel_id=1, source_target_pairs={{0,2},{1,3},{2,0},{3,1},{4,6},{5,7},{6,4},{7,5},{8,10},{9,11},{10,... | collective-permute-start | bytes 2408456 | tf_op jit(solution)/shard_map/ppermute | solution.py:458
  25.6 13.3 %collective-permute-start.2 = (bf16[784,512]{1,0:T(8,128)(2,1)}, bf16[784,512]{1,0:T(8,128)(2,1)}, u32[]{:S(2)}, u32[]{:S(2)}) collective-permute-start(bf16[784,512]{1,0:T(8,128)(2,1)} %collective-permute-done.1.refs_4_), channel_id=1, source_target_pairs={{4,8},{5,9},{6,10},{7,11},{8,4},{9,5},{10,6},{11,7},{20,24},{21,25... | collective-permute-start | bytes 2408456 | tf_op jit(solution)/shard_map/ppermute | solution.py:458
  27.1 22.0 %collective-permute-start.7 = (bf16[784,512]{1,0:T(8,128)(2,1)}, bf16[784,512]{1,0:T(8,128)(2,1)}, u32[]{:S(2)}, u32[]{:S(2)}) collective-permute-start(bf16[784,512]{1,0:T(8,128)(2,1)} %collective-permute-done), channel_id=1, source_target_pairs={{4,0},{5,1},{6,2},{7,3},{8,12},{9,13},{10,14},{11,15},{20,16},{21,... | collective-permute-start | bytes 2408456 | tf_op jit(solution)/shard_map/ppermute | solution.py:458
  38.3 44.5 %collective-permute-start.25 = (f32[512,1024]{1,0:T(8,128)}, f32[512,1024]{1,0:T(8,128)}, u32[]{:S(2)}, u32[]{:S(2)}) collective-permute-start(f32[512,1024]{1,0:T(8,128)} %get-tuple-element.23), channel_id=1, source_target_pairs={{0,1},{1,0},{2,3},{3,2},{4,5},{5,4},{6,7},{7,6},{8,9},{9,8},{10,11... | collective-permute-start | bytes 6291464 | tf_op jit(solution)/shard_map/ppermute | solution.py:458
  38.3 14.8 %collective-permute-start.12 = (bf16[784,512]{1,0:T(8,128)(2,1)}, bf16[784,512]{1,0:T(8,128)(2,1)}, u32[]{:S(2)}, u32[]{:S(2)}) collective-permute-start(bf16[784,512]{1,0:T(8,128)(2,1)} %shard_map.122.refs_0_), channel_id=1, source_target_pairs={{0,1},{1,0},{2,3},{3,2},{4,5},{5,4},{6,7},{7,6},{8,9},{9,8},{10,11... | collective-permute-start | bytes 2408456 | tf_op jit(solution)/shard_map/ppermute | solution.py:458
  38.9 14.9 %collective-permute-start.13 = (bf16[784,512]{1,0:T(8,128)(2,1)}, bf16[784,512]{1,0:T(8,128)(2,1)}, u32[]{:S(2)}, u32[]{:S(2)}) collective-permute-start(bf16[784,512]{1,0:T(8,128)(2,1)} %collective-permute-done.5.refs_2_), channel_id=1, source_target_pairs={{0,1},{1,0},{2,3},{3,2},{4,5},{5,4},{6,7},{7,6},{8,9},{9,8},{10,11... | collective-permute-start | bytes 2408456 | tf_op jit(solution)/shard_map/ppermute | solution.py:458
  38.9 14.9 %collective-permute-start.14 = (bf16[784,512]{1,0:T(8,128)(2,1)}, bf16[784,512]{1,0:T(8,128)(2,1)}, u32[]{:S(2)}, u32[]{:S(2)}) collective-permute-start(bf16[784,512]{1,0:T(8,128)(2,1)} %collective-permute-done.1.refs_4_), channel_id=1, source_target_pairs={{0,1},{1,0},{2,3},{3,2},{4,5},{5,4},{6,7},{7,6},{8,9},{9,8},{10,11... | collective-permute-start | bytes 2408456 | tf_op jit(solution)/shard_map/ppermute | solution.py:458
  49.2 21.1 %collective-permute-start.15 = (bf16[784,512]{1,0:T(8,128)(2,1)}, bf16[784,512]{1,0:T(8,128)(2,1)}, u32[]{:S(2)}, u32[]{:S(2)}) collective-permute-start(bf16[784,512]{1,0:T(8,128)(2,1)} %collective-permute-done.1.refs_4_), channel_id=1, source_target_pairs={{0,2},{1,3},{2,0},{3,1},{4,6},{5,7},{6,4},{7,5},{8,10},{9,11},{10,... | collective-permute-start | bytes 2408456 | tf_op jit(solution)/shard_map/ppermute | solution.py:458
  53.2 35.0 %collective-permute-start.8 = (bf16[784,512]{1,0:T(8,128)(2,1)S(1)}, bf16[784,512]{1,0:T(8,128)(2,1)S(1)}, u32[]{:S(2)}, u32[]{:S(2)}) collective-permute-start(bf16[784,512]{1,0:T(8,128)(2,1)S(1)} %broadcast_select_fusion.refs_2_), channel_id=1, source_target_pairs={{0,2},{1,3},{2,0},{3,1},{4,6},{5,7},{6,4},{7,5},{8,10},{9,11},{10,... | collective-permute-start | bytes 2408456 | tf_op jit(solution)/shard_map/ppermute | solution.py:458
  53.7 37.6 %collective-permute-start.17 = (bf16[784,512]{1,0:T(8,128)(2,1)S(1)}, bf16[784,512]{1,0:T(8,128)(2,1)S(1)}, u32[]{:S(2)}, u32[]{:S(2)}) collective-permute-start(bf16[784,512]{1,0:T(8,128)(2,1)S(1)} %broadcast_select_fusion.refs_2_), channel_id=1, source_target_pairs={{0,1},{1,0},{2,3},{3,2},{4,5},{5,4},{6,7},{7,6},{8,9},{9,8},{10,11... | collective-permute-start | bytes 2408456 | tf_op jit(solution)/shard_map/ppermute | solution.py:458
  53.7 31.8 %collective-permute-start.3 = (bf16[784,512]{1,0:T(8,128)(2,1)}, bf16[784,512]{1,0:T(8,128)(2,1)S(1)}, u32[]{:S(2)}, u32[]{:S(2)}) collective-permute-start(bf16[784,512]{1,0:T(8,128)(2,1)} %collective-permute-done.2), channel_id=1, source_target_pairs={{4,0},{5,1},{6,2},{7,3},{8,12},{9,13},{10,14},{11,15},{20,16},{21,... | collective-permute-start | bytes 2408456 | tf_op jit(solution)/shard_map/ppermute | solution.py:458
  70.2 19.6 %collective-permute-start.16 = (bf16[784,512]{1,0:T(8,128)(2,1)}, bf16[784,512]{1,0:T(8,128)(2,1)S(1)}, u32[]{:S(2)}, u32[]{:S(2)}) collective-permute-start(bf16[784,512]{1,0:T(8,128)(2,1)} %collective-permute-done.15.refs_0_), channel_id=1, source_target_pairs={{0,1},{1,0},{2,3},{3,2},{4,5},{5,4},{6,7},{7,6},{8,9},{9,8},{10,11... | collective-permute-start | bytes 2408456 | tf_op jit(solution)/shard_map/ppermute | solution.py:458
  82.9 17.9 %collective-permute-start.6 = (bf16[384,512]{1,0:T(8,128)(2,1)S(1)}, bf16[384,512]{1,0:T(8,128)(2,1)S(1)}, u32[]{:S(2)}, u32[]{:S(2)}) collective-permute-start(bf16[384,512]{1,0:T(8,128)(2,1)S(1)} %slice.90), channel_id=1, source_target_pairs={{4,8},{5,9},{6,10},{7,11},{8,4},{9,5},{10,6},{11,7},{20,24},{21,25... | collective-permute-start | bytes 1179656 | tf_op jit(solution)/shard_map/ppermute | solution.py:458
  85.6 25.6 %collective-permute-start.26 = (f32[256,1024]{1,0:T(8,128)S(1)}, f32[256,1024]{1,0:T(8,128)S(1)}, u32[]{:S(2)}, u32[]{:S(2)}) collective-permute-start(f32[256,1024]{1,0:T(8,128)S(1)} %get-tuple-element.35), channel_id=1, source_target_pairs={{0,16},{16,0},{1,17},{17,1},{2,18},{18,2},{3,19},{19,3},{4,20},{20... | collective-permute-start | bytes 3145736 | tf_op jit(solution)/shard_map/ppermute | solution.py:458
  88.2 14.5 %collective-permute-start.4 = (bf16[400,512]{1,0:T(8,128)(2,1)S(1)}, bf16[400,512]{1,0:T(8,128)(2,1)S(1)}, u32[]{:S(2)}, u32[]{:S(2)}) collective-permute-start(bf16[400,512]{1,0:T(8,128)(2,1)S(1)} %slice_select_fusion.refs_2_), channel_id=1, source_target_pairs={{0,2},{1,3},{2,0},{3,1},{4,6},{5,7},{6,4},{7,5},{8,10},{9,11},{10,... | collective-permute-start | bytes 1228808 | tf_op jit(solution)/shard_map/ppermute | solution.py:458
  89.8 12.9 %collective-permute-start.9 = (bf16[384,512]{1,0:T(8,128)(2,1)S(1)}, bf16[384,512]{1,0:T(8,128)(2,1)S(1)}, u32[]{:S(2)}, u32[]{:S(2)}) collective-permute-start(bf16[384,512]{1,0:T(8,128)(2,1)S(1)} %slice.91), channel_id=1, source_target_pairs={{4,0},{5,1},{6,2},{7,3},{8,12},{9,13},{10,14},{11,15},{20,16},{21,... | collective-permute-start | bytes 1179656 | tf_op jit(solution)/shard_map/ppermute | solution.py:458
  91.3 22.5 %collective-permute-start.18 = (bf16[784,512]{1,0:T(8,128)(2,1)S(1)}, bf16[784,512]{1,0:T(8,128)(2,1)S(1)}, u32[]{:S(2)}, u32[]{:S(2)}) collective-permute-start(bf16[784,512]{1,0:T(8,128)(2,1)S(1)} %collective-permute-done.8.refs_0_), channel_id=1, source_target_pairs={{0,1},{1,0},{2,3},{3,2},{4,5},{5,4},{6,7},{7,6},{8,9},{9,8},{10,11... | collective-permute-start | bytes 2408456 | tf_op jit(solution)/shard_map/ppermute | solution.py:458
  100.8 13.0 %collective-permute-start.19 = (bf16[400,512]{1,0:T(8,128)(2,1)S(1)}, bf16[400,512]{1,0:T(8,128)(2,1)S(1)}, u32[]{:S(2)}, u32[]{:S(2)}) collective-permute-start(bf16[400,512]{1,0:T(8,128)(2,1)S(1)} %slice_select_fusion.refs_2_), channel_id=1, source_target_pairs={{0,1},{1,0},{2,3},{3,2},{4,5},{5,4},{6,7},{7,6},{8,9},{9,8},{10,11... | collective-permute-start | bytes 1228808 | tf_op jit(solution)/shard_map/ppermute | solution.py:458
  102.7 19.7 %collective-permute-start.11 = (bf16[384,512]{1,0:T(8,128)(2,1)S(1)}, bf16[384,512]{1,0:T(8,128)(2,1)S(1)}, u32[]{:S(2)}, u32[]{:S(2)}) collective-permute-start(bf16[384,512]{1,0:T(8,128)(2,1)S(1)} %broadcast_select_fusion.1.refs_1_.refs_7_), channel_id=1, source_target_pairs={{0,1},{1,0},{2,3},{3,2},{4,5},{5,4},{6,7},{7,6},{8,9},{9,8},{10,11... | collective-permute-start | bytes 1179656 | tf_op jit(solution)/shard_map/ppermute | solution.py:458
  111.2 11.2 %collective-permute-start.10 = (bf16[400,512]{1,0:T(8,128)(2,1)S(1)}, bf16[400,512]{1,0:T(8,128)(2,1)S(1)}, u32[]{:S(2)}, u32[]{:S(2)}) collective-permute-start(bf16[400,512]{1,0:T(8,128)(2,1)S(1)} %collective-permute-done.4.refs_0_.refs_6_), channel_id=1, source_target_pairs={{0,1},{1,0},{2,3},{3,2},{4,5},{5,4},{6,7},{7,6},{8,9},{9,8},{10,11... | collective-permute-start | bytes 1228808 | tf_op jit(solution)/shard_map/ppermute | solution.py:458
  111.4 9.4 %collective-permute-start.27 = (bf16[128,1024]{1,0:T(8,128)(2,1)S(1)}, bf16[128,1024]{1,0:T(8,128)(2,1)S(1)}, u32[]{:S(2)}, u32[]{:S(2)}) collective-permute-start(bf16[128,1024]{1,0:T(8,128)(2,1)S(1)} %get-tuple-element.37), channel_id=1, source_target_pairs={{0,4},{1,5},{2,6},{3,7},{4,0},{5,1},{6,2},{7,3},{8,12},{9,13},{10,... | collective-permute-start | bytes 786440 | tf_op jit(solution)/shard_map/ppermute | solution.py:458
  120.9 15.6 %collective-permute-start.28 = (bf16[64,1024]{1,0:T(8,128)(2,1)S(1)}, bf16[64,1024]{1,0:T(8,128)(2,1)S(1)}, u32[]{:S(2)}, u32[]{:S(2)}) collective-permute-start(bf16[64,1024]{1,0:T(8,128)(2,1)S(1)} %get-tuple-element.39), channel_id=1, source_target_pairs={{0,8},{1,9},{2,10},{3,11},{4,12},{5,13},{6,14},{7,15},{8,0},{9,1},... | collective-permute-start | bytes 393224 | tf_op jit(solution)/shard_map/ppermute | solution.py:458
  (16 other events, 161.7 us)

commit v2 on v1

--- a/solution.py
+++ b/solution.py
@@ -48,7 +48,9 @@
     return hist_rows, kept_rows, pieces, hist_rows + kept_rows * pieces
 
 
-def pack_kernel(target_ref, extent_ref, x_hbm, kept_ref, hist_hbm, out_ref, x_ref, sems):
+def pack_kernel(
+    target_ref, extent_ref, x_hbm, kept_ref, hist_hbm, out_hbm, x_ref, out_ref, sems
+):
     requests, cand, _ = x_ref.shape
     kept = kept_ref.shape[1]
     focus = hist_hbm.shape[1]
@@ -56,8 +58,8 @@
     tops = target_ref.shape[1]
     pieces = x_ref.shape[2] // focus
     meta_at = hist_rows + pieces * requests * kept
+    wait_hist = fetch(hist_hbm, out_ref.at[pl.ds(0, hist_rows), :], sems.at[requests])
     waits = [fetch(x_hbm.at[r], x_ref.at[r], sems.at[r]) for r in range(requests)]
-    wait_hist = fetch(hist_hbm, out_ref.at[pl.ds(0, hist_rows), :], sems.at[requests])
     row = lax.broadcasted_iota(jnp.int32, (META_ROWS, focus), 0)
     lane = lax.broadcasted_iota(jnp.int32, (META_ROWS, focus), 1)
     meta = jnp.zeros((META_ROWS, focus), jnp.int32)
@@ -66,6 +68,9 @@
             meta = jnp.where((row == r) & (lane == t), target_ref[r, t], meta)
         meta = jnp.where((row == r) & (lane == tops), extent_ref[r], meta)
     out_ref[meta_at:, :] = meta.astype(F32).astype(BF16)
+    wait_hist()
+    at = pl.ds(0, hist_rows)
+    wait_out = fetch(out_ref.at[at, :], out_hbm.at[at, :], sems.at[requests])
     for r in range(requests):
         waits[r]()
         cand_of = lax.broadcasted_iota(jnp.int32, (cand, kept), 0)
@@ -79,7 +84,10 @@
             )
             at = hist_rows + p * requests * kept + r * kept
             out_ref[at : at + kept, :] = rows.astype(BF16)
-    wait_hist()
+    at = pl.ds(hist_rows, out_ref.shape[0] - hist_rows)
+    wait_rest = fetch(out_ref.at[at, :], out_hbm.at[at, :], sems.at[0])
+    wait_out()
+    wait_rest()
 
 
 def pack(x, kept, hist, targets, extents):
@@ -91,14 +99,18 @@
         pack_kernel,
         out_shape=jax.ShapeDtypeStruct((total, focus), BF16),
         in_specs=[scalars(), scalars(), in_place(), full_vmem(), in_place()],
-        out_specs=full_vmem(),
-        scratch_shapes=[VMEM(x.shape, BF16), pltpu.SemaphoreType.DMA((requests + 1,))],
+        out_specs=in_place(),
+        scratch_shapes=[
+            VMEM(x.shape, BF16),
+            VMEM((total, focus), BF16),
+            pltpu.SemaphoreType.DMA((requests + 1,)),
+        ],
         cost_estimate=pl.CostEstimate(flops=10**8, bytes_accessed=3 * 10**6, transcendentals=0),
     )(targets, extents, stays(x), stays(kept), stays(flat_hist))
 
 
 def student_kernel(requests, chunk, order, me_ref, x_ref, w_ref, s_ref, c_ref, e_ref, *refs):
-    grad_refs, (gs_ref, rate_ref, part_ref) = refs[:-3], refs[-3:]
+    grad_refs, (gs_ref, rate_ref, part_ref, less_ref) = refs[:-4], refs[-4:]
     rows, feats = x_ref.shape
     units = w_ref.shape[1]
     cand = rows // requests
@@ -111,7 +123,9 @@
         exp_scores = jnp.exp(jnp.sum(hidden * score_vec, axis=-1, keepdims=True))
         student = exp_scores / jnp.sum(exp_scores, axis=0, keepdims=True)
         live = jnp.where(preact > 0, student * score_vec, 0.0)
-        part_ref[at, :] = live.astype(BF16)
+        high = live.astype(BF16)
+        part_ref[at, :] = high
+        less_ref[at, :] = (live - high.astype(F32)).astype(BF16)
         return total + jnp.sum(student * hidden, axis=0, keepdims=True)
 
     gs_ref[...] = lax.fori_loop(0, requests, one, jnp.zeros((1, units), F32))
@@ -120,9 +134,9 @@
 
     def block(i, carry):
         at = pl.ds(pl.multiple_of(i * step, step), step)
-        grad = lax.dot_general(
-            x_ref[:, at], part_ref[...], (((0,), (0,)), ((), ())), preferred_element_type=F32
-        )
+        across = (((0,), (0,)), ((), ()))
+        grad = lax.dot_general(x_ref[:, at], part_ref[...], across, preferred_element_type=F32)
+        grad += lax.dot_general(x_ref[:, at], less_ref[...], across, preferred_element_type=F32)
         for j in range(step // chunk):
             piece = grad[j * chunk : (j + 1) * chunk, :]
             spot = order(i * (step // chunk) + j, me_ref[0])
@@ -164,7 +178,7 @@
         ),
         in_specs=[scalars()] + [full_vmem()] * 5,
         out_specs=(full_vmem(),) * (halves + 2),
-        scratch_shapes=[VMEM((rows, units), BF16)],
+        scratch_shapes=[VMEM((rows, units), BF16)] * 2,
         compiler_params=room(20),
         cost_estimate=pl.CostEstimate(
             flops=4 * requests * cand * feats * units, bytes_accessed=8 * 10**6, transcendentals=0
@@ -238,7 +252,7 @@
 def rank_kernel(dims, sel_rows, layout, wants, first, info_ref, *refs):
     want_scores, want_hidden, parts = wants
     requests, hist_slots, kept, _, _ = dims
-    n_in = sum(layout) if layout else 1
+    n_in = sum(sum(pieces) for pieces in layout) if layout else 1
     arrays, refs = refs[:n_in], refs[n_in:]
     if want_scores:
         (a_ref, l_ref, r_ref), refs = refs[:3], refs[3:]
@@ -261,17 +275,26 @@
         if not layout:
             fetch(arrays[0].at[b, pl.ds(low, high - low), :], buf.at[b], sems.at[b])
             return
-        at, i = 0, sum(layout[:b])
-        for array in arrays[i : i + layout[b]]:
-            rows = array.shape[0]
+        at, i = 0, sum(sum(pieces) for pieces in layout[:b])
+        for choices in layout[b]:
+            rows = arrays[i].shape[0]
             begin, end = max(at, low), min(at + rows, high)
             if begin < end:
-                fetch(
-                    array.at[pl.ds(begin - at, end - begin), :],
-                    buf.at[b, pl.ds(begin - low, end - begin), :],
-                    sems.at[b],
-                )
+                for choice in range(choices):
+
+                    def start(array=arrays[i + choice], at=at, begin=begin, end=end):
+                        fetch(
+                            array.at[pl.ds(begin - at, end - begin), :],
+                            buf.at[b, pl.ds(begin - low, end - begin), :],
+                            sems.at[b],
+                        )
+
+                    if choices == 1:
+                        start()
+                    else:
+                        pl.when(info_ref[3] == choice)(start)
             at += rows
+            i += choices
 
     def wait_block(b):
         pltpu.make_async_copy(buf.at[b], buf.at[b], sems.at[b]).wait()
@@ -326,9 +349,10 @@
     want_scores, want_hidden = score_weights is not None, hidden_weights is not None
     if isinstance(payloads, list):
         blocks = len(payloads)
-        layout = [len(p) for p in payloads]
-        arrays = [a for p in payloads for a in p]
-        rows, focus = sum(a.shape[0] for a in payloads[0]), arrays[0].shape[1]
+        payloads = [[p if isinstance(p, tuple) else (p,) for p in block] for block in payloads]
+        layout = [[len(p) for p in block] for block in payloads]
+        arrays = [a for block in payloads for p in block for a in p]
+        rows, focus = sum(p[0].shape[0] for p in payloads[0]), arrays[0].shape[1]
     else:
         blocks, rows, focus = payloads.shape
         layout, arrays = None, [payloads]
@@ -428,7 +452,7 @@
     parts = len(hiddens)
     return pl.pallas_call(
         functools.partial(target_kernel, kept, tops, parts),
-        out_shape=tuple(jax.ShapeDtypeStruct((sel_rows + 16, units), t) for t in (F32, BF16)),
+        out_shape=tuple(jax.ShapeDtypeStruct((sel_rows + 8, units), t) for t in (F32, BF16)),
         in_specs=[scalars()] + [full_vmem()] * (3 + 2 * parts),
         out_specs=(full_vmem(),) * 2,
         scratch_shapes=[VMEM((blocks, got.shape[1]), F32)],
@@ -458,9 +482,7 @@
     return lax.ppermute(x, axis, table)
 
 
-def gather_stages(b, me):
-    inner = ((me >> 2) ^ (me >> 3)) & 1 == 1
-    cut = -(-b.shape[0] // 32) * 16
+def gather_stages(b, inner, cut):
     near = shift(b, Z_NEAR)
     over = shift(b, Y_OVER)
     mid = shift(b, Z_INNER)
@@ -474,23 +496,27 @@
     over_last = shift(last[0], Y_OVER)
     rest_out = shift(over_far[cut:], Z_OUT)
     rest_mid = shift(over[cut:], Z_INNER)
-    over_rest = jnp.where(inner, rest_mid, rest_out)
+
+    def beside(p):
+        if isinstance(p, tuple):
+            return tuple(shift(a, SIBLING) for a in p)
+        return shift(p, SIBLING)
 
     def both(*pieces):
-        return [list(pieces), [shift(p, SIBLING) for p in pieces]]
+        return [list(pieces), [beside(p) for p in pieces]]
 
     return [
         both(b) + both(over) + both(near),
         both(over_near) + both(far),
         both(over_far) + both(*last),
-        both(over_last, over_rest),
+        both(over_last, (rest_out, rest_mid)),
     ]
 
 
 def halving_order(block, me):
     away = block ^ me
     z1, z0, y, core, grp = [(away >> i) & 1 for i in (4, 3, 2, 1, 0)]
-    return (core << 4) | (grp << 3) | (z0 << 2) | (z1 << 1) | y
+    return (core << 4) | (grp << 3) | (z0 << 2) | (y << 1) | z1
 
 
 def halve(keep, sent):
@@ -498,21 +524,23 @@
         (SIBLING, "shard"),
         ([(0, 1), (1, 0)], "group"),
         (Z_NEAR, "shard"),
+        (Y_OVER, "shard"),
         (Z_FAR, "shard"),
-        (Y_OVER, "shard"),
     ):
         wide = axis == "group" or table is SIBLING
         got = shift(sent if wide else sent.astype(BF16), table, axis).astype(F32)
         half = keep.shape[0] // 2
-        if table is Y_OVER:
+        if table is Z_FAR:
             return keep + got
         keep, sent = keep[:half] + got[:half], keep[half:] + got[half:]
 
 
 def sum_over_shard(x):
-    for table in (SIBLING, Y_OVER, Z_NEAR, Z_FAR):
-        x = x + shift(x, table)
-    return x
+    for table in (SIBLING, Y_OVER):
+        got = shift(x, table)
+        x = x + got
+    near, far, last = shift(x, Z_NEAR), shift(x, Z_FAR), shift(x, flip(12))
+    return (x + near) + (far + last)
 
 
 def sum_kernel(a_ref, b_ref, grad_ref, score_ref):
@@ -574,12 +602,13 @@
         place,
     )
     if linked:
-        stages = gather_stages(payload, me)
+        inner = ((me >> 2) ^ (me >> 3)) & 1
+        stages = gather_stages(payload, inner == 1, requests * hist_slots)
         keep, sent, gs_student, rate = student_part(
             *stack, n_shard * n_group, 2, halving_order
         )
         base = halve(keep, sent)
-        info = jnp.stack([me, me, grp]).astype(jnp.int32)
+        info = jnp.stack([me, me, grp, inner]).astype(jnp.int32)
     else:
         payloads = lax.all_gather(payload, "shard", axis=0, tiled=False)
         stages = [payloads[b : b + 4] for b in range(0, n_shard, 4)]
@@ -587,7 +616,7 @@
             *stack, n_shard, 1, lambda block, at: block
         )
         base = lax.psum_scatter(grad_student, "shard", scatter_dimension=0, tiled=True)
-        info = jnp.stack([me, 0 * me, 0 * me]).astype(jnp.int32)
+        info = jnp.stack([me, 0 * me, 0 * me, 0 * me]).astype(jnp.int32)
 
     dims = (requests, hist_slots, kept, tops, ATTENDER_GANGS)
     score_weights = (asking_matrix[0], lookup_matrix[0], rate)

time: 150 us -> 146 us (0.973)
  starting transfers between devices: 31.3 us -> 28.7 us
  local copies, waits for them, and re-layouts: 4.88 us -> 2.7 us
  waiting for transfers between devices: 59.3 us -> 61.1 us
    ppermute x31 -> x33, starting transfers between devices: 31.3 us -> 28.7 us  [shift(): return lax.ppermute(x, axis, table)]
    pallas_call x5, Pallas kernels: 33.4 us -> 31.4 us  [rank(): pl.pallas_call(functools.partial(rank_kernel, dims, sel_rows, layout, (wa...]
    ppermute x31 -> x33, waiting for transfers between devices: 59.3 us -> 61.1 us  [shift(): return lax.ppermute(x, axis, table)]
    unnamed x18 -> x16, local copies, waits for them, and re-layouts: 3.69 us -> 2.66 us
  transfers between devices with their start and end apart: 31 -> 33, of which waited for: 10 -> 12; matrix products, arithmetic and copies ran while one was open for 5% -> 4% of each run, Pallas kernels for 27% -> 25%
where the time goes in v2:
time: 146 us
  waiting for transfers between devices  61.1 us (42%)
  Pallas kernels  46.5 us (32%)
  starting transfers between devices  28.7 us (20%)
  other arithmetic  5.87 us (4%)
  local copies, waits for them, and re-layouts  2.7 us (2%)
    ppermute x33, waiting for transfers between devices, shift(): return lax.ppermute(x, axis, table)  61.1 us
    pallas_call x5, Pallas kernels, rank(): pl.pallas_call(functools.partial(rank_kernel, dims, sel_rows, layout, (wa...  31.4 us
    ppermute x33, starting transfers between devices, shift(): return lax.ppermute(x, axis, table)  28.7 us
    pallas_call x1, Pallas kernels, student_part(): pl.pallas_call(functools.partial(student_kernel, requests, feats // piece...  8.71 us
    pallas_call x1, Pallas kernels, pack(): pl.pallas_call(pack_kernel, out_shape=jax.ShapeDtypeStruct((total, focus)...  3.51 us
  transfers between devices with their start and end apart: 33, of which 12 were waited for; matrix products, arithmetic and copies ran while one was open for 4% of the time, Pallas kernels for 25%

profile of v2, /device:TPU:0, one launch (start us, length us, event | category | flops | bytes accessed | tf_op | source)
XLA Modules:
  0.0 145.9 jit_solution(9524639266482381901)
XLA Ops:
  0.7 3.5 %shard_map.122.refs_0_ = bf16[784,512]{1,0:T(8,128)(2,1)} custom-call(s32[4,6]{1,0:T(4,128)} %target_ref.1, s32[4]{0:T(128)} %extent_ref.1, bf16[4,128,1024]{2,1,0:T(8,128)(2,1)} %x_hbm.1, s32[4,32]{1,0:T(4,128)} %kept_ref.1, bf16[512,512]{1,0:T(8,128)(2,1)} %bitcast.20), custom_call_target="tpu_custom_call" | custom-call | flops 100000000 | bytes 3000000 | tf_op jit(solution)/shard_map/pallas_call | solution.py:98
  4.2 3.1 %collective-permute-start.1 = (bf16[784,512]{1,0:T(8,128)(2,1)}, bf16[784,512]{1,0:T(8,128)(2,1)}, u32[]{:S(2)}, u32[]{:S(2)}) collective-permute-start(bf16[784,512]{1,0:T(8,128)(2,1)} %shard_map.122.refs_0_), channel_id=1, source_target_pairs={{0,4},{1,5},{2,6},{3,7},{4,0},{5,1},{6,2},{7,3},{8,12},{9,13},{10,... | collective-permute-start | bytes 2408456 | tf_op jit(solution)/shard_map/ppermute | solution.py:482
  11.5 8.7 %shard_map.123 = (f32[512,1024]{1,0:T(8,128)S(1)}, f32[512,1024]{1,0:T(8,128)}, f32[1,1024]{1,0:T(1,128)S(1)}, bf16[512,256]{1,0:T(8,128)(2,1)S(1)}) custom-call(s32[1]{0:T(128)} %bitcast.6.me_ref, bf16[512,1024]{1,0:T(8,128)(2,1)S(1)} %bitcast.10, bf16[1024,1024]{1,0:T(8,128)(2,1)S(1)} %copy-done, bf16[1,1024]{1,0:T(2,128)(2,1)S(1)} %reshape.23.s_ref, ...), custom_call_target="tpu_custom_call" | custom-call | flops 2147483648 | bytes 8000000 | tf_op jit(solution)/shard_map/pallas_call | solution.py:172
  21.8 3.8 %collective-permute-done.1.refs_4_ = bf16[784,512]{1,0:T(8,128)(2,1)} collective-permute-done((bf16[784,512]{1,0:T(8,128)(2,1)}, bf16[784,512]{1,0:T(8,128)(2,1)}, u32[]{:S(2)}, u32[]{:S(2)}) %collective-permute-start.1) | collective-permute-done | bytes 802848 | tf_op jit(solution)/shard_map/ppermute | solution.py:482
  28.4 12.3 %collective-permute-done.8.refs_2_ = bf16[784,512]{1,0:T(8,128)(2,1)S(1)} collective-permute-done((bf16[784,512]{1,0:T(8,128)(2,1)}, bf16[784,512]{1,0:T(8,128)(2,1)S(1)}, u32[]{:S(2)}, u32[]{:S(2)}) %collective-permute-start.8) | collective-permute-done | bytes 802848 | tf_op jit(solution)/shard_map/ppermute | solution.py:482
  42.3 6.8 %collective-permute-done.5 = bf16[784,512]{1,0:T(8,128)(2,1)} collective-permute-done((bf16[784,512]{1,0:T(8,128)(2,1)}, bf16[784,512]{1,0:T(8,128)(2,1)}, u32[]{:S(2)}, u32[]{:S(2)}) %collective-permute-start.5) | collective-permute-done | bytes 802848 | tf_op jit(solution)/shard_map/ppermute | solution.py:482
  50.3 1.6 %collective-permute-start.6 = (bf16[784,512]{1,0:T(8,128)(2,1)S(1)}, bf16[784,512]{1,0:T(8,128)(2,1)S(1)}, u32[]{:S(2)}, u32[]{:S(2)}) collective-permute-start(bf16[784,512]{1,0:T(8,128)(2,1)S(1)} %broadcast_select_fusion.refs_2_), channel_id=1, source_target_pairs={{0,2},{1,3},{2,0},{3,1},{4,6},{5,7},{6,4},{7,5},{8,10},{9,11},{10,... | collective-permute-start | bytes 2408456 | tf_op jit(solution)/shard_map/ppermute | solution.py:482
  53.4 2.1 %slice_add_fusion.1 = (f32[256,1024]{1,0:T(8,128)S(1)}, f32[256,1024]{1,0:T(8,128)S(1)}) fusion(f32[512,1024]{1,0:T(8,128)} %collective-permute-done.27, f32[512,1024]{1,0:T(8,128)S(1)} %get-tuple-element.22), kind=kLoop, calls=%fused_computation.1 | loop fusion | flops 524288 | bytes 6291456 | tf_op jit(solution)/shard_map/add | solution.py:535
  55.5 6.3 %collective-permute-done.16.refs_0_ = bf16[784,512]{1,0:T(8,128)(2,1)S(1)} collective-permute-done((bf16[784,512]{1,0:T(8,128)(2,1)}, bf16[784,512]{1,0:T(8,128)(2,1)S(1)}, u32[]{:S(2)}, u32[]{:S(2)}) %collective-permute-start.16) | collective-permute-done | bytes 802848 | tf_op jit(solution)/shard_map/ppermute | solution.py:482
  63.0 14.7 %collective-permute-done.6.refs_0_ = bf16[784,512]{1,0:T(8,128)(2,1)S(1)} collective-permute-done((bf16[784,512]{1,0:T(8,128)(2,1)S(1)}, bf16[784,512]{1,0:T(8,128)(2,1)S(1)}, u32[]{:S(2)}, u32[]{:S(2)}) %collective-permute-start.6) | collective-permute-done | bytes 802848 | tf_op jit(solution)/shard_map/ppermute | solution.py:482
  79.2 11.6 %shard_map.124 = (f32[6,1,128]{2,1,0:T(1,128)S(1)}, bf16[768,1024]{1,0:T(8,128)(2,1)S(1)}, bf16[64,768]{1,0:T(8,128)(2,1)S(1)}) custom-call(s32[4]{0:T(128)S(1)} %pad_add_fusion.info_ref.me_ref, bf16[784,512]{1,0:T(8,128)(2,1)} %shard_map.122.refs_0_, bf16[784,512]{1,0:T(8,128)(2,1)} %collective-permute-done.13.refs_1_, ...), custom_call_target="tpu_custom_call" | custom-call | flops 6000000000 | bytes 6000000 | tf_op jit(solution)/shard_map/pallas_call | solution.py:380
  96.4 4.6 %collective-permute-done.7.refs_1_.refs_7_ = bf16[272,512]{1,0:T(8,128)(2,1)S(1)} collective-permute-done((bf16[272,512]{1,0:T(8,128)(2,1)S(1)}, bf16[272,512]{1,0:T(8,128)(2,1)S(1)}, u32[]{:S(2)}, u32[]{:S(2)}) %collective-permute-start.7) | collective-permute-done | bytes 278560 | tf_op jit(solution)/shard_map/ppermute | solution.py:482
  101.1 7.5 %shard_map.125 = (f32[4,1,128]{2,1,0:T(1,128)S(1)}, bf16[512,1024]{1,0:T(8,128)(2,1)S(1)}, bf16[64,512]{1,0:T(8,128)(2,1)S(1)}) custom-call(s32[4]{0:T(128)S(1)} %pad_add_fusion.info_ref.me_ref, bf16[784,512]{1,0:T(8,128)(2,1)S(1)} %collective-permute-done.16.refs_0_, bf16[784,512]{1,0:T(8,128)(2,1)S(1)} %collective-permute-done.17.refs_1_, ...), custom_call_target="tpu_custom_call" | custom-call | flops 4000000000 | bytes 4000000 | tf_op jit(solution)/shard_map/pallas_call | solution.py:380
  110.1 6.0 %shard_map.126.refs_11_ = f32[4,1,128]{2,1,0:T(1,128)S(1)} custom-call(s32[4]{0:T(128)S(1)} %pad_add_fusion.info_ref.me_ref, bf16[784,512]{1,0:T(8,128)(2,1)S(1)} %collective-permute-done.6.refs_0_, bf16[784,512]{1,0:T(8,128)(2,1)S(1)} %collective-permute-done.19.refs_1_, bf16[512,512]{1,0:T(8,128)(2,1)S(1)} %slice_select_fusion.refs_2_, ...), custom_call_target="tpu_custom_call" | custom-call | flops 2800000000 | bytes 4000000 | tf_op jit(solution)/shard_map/pallas_call | solution.py:380
  116.1 2.1 %collective-permute-done.29 = bf16[128,1024]{1,0:T(8,128)(2,1)S(1)} collective-permute-done((bf16[128,1024]{1,0:T(8,128)(2,1)S(1)}, bf16[128,1024]{1,0:T(8,128)(2,1)S(1)}, u32[]{:S(2)}, u32[]{:S(2)}) %collective-permute-start.29) | collective-permute-done | bytes 262176 | tf_op jit(solution)/shard_map/ppermute | solution.py:482
  118.3 3.5 %shard_map.127 = f32[24,128]{1,0:T(8,128)S(1)} custom-call(s32[4]{0:T(128)S(1)} %pad_add_fusion.info_ref.me_ref, bf16[512,512]{1,0:T(8,128)(2,1)S(1)} %collective-permute-done.4.refs_0_.refs_6_, bf16[272,512]{1,0:T(8,128)(2,1)S(1)} %collective-permute-done.7.refs_1_.refs_7_, bf16[272,512]{1,0:T(8,128)(2,1)S(1)} %collective-permute-done.9.refs_2_.refs_8_, ...), custom_call_target="tpu_custom_call" | custom-call | flops 1400000000 | bytes 2000000 | tf_op jit(solution)/shard_map/pallas_call | solution.py:380
  121.9 1.6 %collective-permute-start.30 = (bf16[64,1024]{1,0:T(8,128)(2,1)S(1)}, bf16[64,1024]{1,0:T(8,128)(2,1)S(1)}, u32[]{:S(2)}, u32[]{:S(2)}) collective-permute-start(bf16[64,1024]{1,0:T(8,128)(2,1)S(1)} %get-tuple-element.39), channel_id=1, source_target_pairs={{0,2},{1,3},{2,0},{3,1},{4,6},{5,7},{6,4},{7,5},{8,10},{9,11},{10,... | collective-permute-start | bytes 393224 | tf_op jit(solution)/shard_map/ppermute | solution.py:482
  124.5 2.9 %shard_map.128 = (bf16[768,1024]{1,0:T(8,128)(2,1)S(1)}, bf16[64,768]{1,0:T(8,128)(2,1)S(1)}) custom-call(s32[4]{0:T(128)S(1)} %pad_add_fusion.info_ref.me_ref, bf16[784,512]{1,0:T(8,128)(2,1)S(1)} %collective-permute-done.6.refs_0_, bf16[784,512]{1,0:T(8,128)(2,1)S(1)} %collective-permute-done.19.refs_1_, bf16[512,512]{1,0:T(8,128)(2,1)S(1)} %slice_select_fusion.refs_2_, ...), custom_call_target="tpu_custom_call" | custom-call | flops 1800000000 | bytes 6000000 | tf_op jit(solution)/shard_map/pallas_call | solution.py:380
  128.4 1.6 %collective-permute-start.25 = (f32[24,128]{1,0:T(8,128)S(1)}, f32[24,128]{1,0:T(8,128)S(1)}, u32[]{:S(2)}, u32[]{:S(2)}) collective-permute-start(f32[24,128]{1,0:T(8,128)S(1)} %add.47), channel_id=1, source_target_pairs={{0,8},{1,9},{2,10},{3,11},{4,12},{5,13},{6,14},{7,15},{8,0},{9,1},... | collective-permute-start | bytes 36872 | tf_op jit(solution)/shard_map/ppermute | solution.py:482
  130.0 2.5 %collective-permute-start.26 = (f32[24,128]{1,0:T(8,128)S(1)}, f32[24,128]{1,0:T(8,128)S(1)}, u32[]{:S(2)}, u32[]{:S(2)}) collective-permute-start(f32[24,128]{1,0:T(8,128)S(1)} %add.47), channel_id=1, source_target_pairs={{0,12},{1,13},{2,14},{3,15},{4,8},{5,9},{6,10},{7,11},{8,4},{9,5},... | collective-permute-start | bytes 36872 | tf_op jit(solution)/shard_map/ppermute | solution.py:482
  133.0 2.6 %collective-permute-done.26 = f32[24,128]{1,0:T(8,128)S(1)} collective-permute-done((f32[24,128]{1,0:T(8,128)S(1)}, f32[24,128]{1,0:T(8,128)S(1)}, u32[]{:S(2)}, u32[]{:S(2)}) %collective-permute-start.26) | collective-permute-done | bytes 12320 | tf_op jit(solution)/shard_map/ppermute | solution.py:482
  135.6 2.2 %collective-permute-done.31 = bf16[32,1024]{1,0:T(8,128)(2,1)S(1)} collective-permute-done((bf16[32,1024]{1,0:T(8,128)(2,1)S(1)}, bf16[32,1024]{1,0:T(8,128)(2,1)S(1)}, u32[]{:S(2)}, u32[]{:S(2)}) %collective-permute-start.31) | collective-permute-done | bytes 65568 | tf_op jit(solution)/shard_map/ppermute | solution.py:482
  137.8 2.1 %shard_map.129 = (f32[72,1024]{1,0:T(8,128)S(1)}, bf16[72,1024]{1,0:T(8,128)(2,1)S(1)}) custom-call(s32[4]{0:T(128)S(1)} %pad_add_fusion.info_ref.me_ref, f32[24,128]{1,0:T(8,128)S(1)} %add_add_fusion.got_ref, bf16[1,1024]{1,0:T(2,128)(2,1)S(1)} %reshape.23.s_ref, f32[32,1024]{1,0:T(8,128)S(1)} %fusion.3.base_ref, ...), custom_call_target="tpu_custom_call" | custom-call | flops 1000000000 | bytes 6000000 | tf_op jit(solution)/shard_map/pallas_call | solution.py:453
  140.6 4.6 %collective-permute-done.32.b_ref = bf16[72,1024]{1,0:T(8,128)(2,1)S(1)} collective-permute-done((bf16[72,1024]{1,0:T(8,128)(2,1)S(1)}, bf16[72,1024]{1,0:T(8,128)(2,1)S(1)}, u32[]{:S(2)}, u32[]{:S(2)}) %collective-permute-start.32) | collective-permute-done | bytes 147488 | tf_op jit(solution)/shard_map/ppermute | solution.py:482
  (84 shorter events, 26.6 us)
Async XLA Ops:
  4.2 21.3 %collective-permute-start.1 = (bf16[784,512]{1,0:T(8,128)(2,1)}, bf16[784,512]{1,0:T(8,128)(2,1)}, u32[]{:S(2)}, u32[]{:S(2)}) collective-permute-start(bf16[784,512]{1,0:T(8,128)(2,1)} %shard_map.122.refs_0_), channel_id=1, source_target_pairs={{0,4},{1,5},{2,6},{3,7},{4,0},{5,1},{6,2},{7,3},{8,12},{9,13},{10,... | collective-permute-start | bytes 2408456 | tf_op jit(solution)/shard_map/ppermute | solution.py:482
  7.3 19.8 %collective-permute-start = (bf16[784,512]{1,0:T(8,128)(2,1)}, bf16[784,512]{1,0:T(8,128)(2,1)}, u32[]{:S(2)}, u32[]{:S(2)}) collective-permute-start(bf16[784,512]{1,0:T(8,128)(2,1)} %shard_map.122.refs_0_), channel_id=1, source_target_pairs={{4,8},{5,9},{6,10},{7,11},{8,4},{9,5},{10,6},{11,7},{20,24},{21,25... | collective-permute-start | bytes 2408456 | tf_op jit(solution)/shard_map/ppermute | solution.py:482
  20.3 31.8 %collective-permute-start.27 = (f32[512,1024]{1,0:T(8,128)}, f32[512,1024]{1,0:T(8,128)}, u32[]{:S(2)}, u32[]{:S(2)}) collective-permute-start(f32[512,1024]{1,0:T(8,128)} %get-tuple-element.23), channel_id=1, source_target_pairs={{0,1},{1,0},{2,3},{3,2},{4,5},{5,4},{6,7},{7,6},{8,9},{9,8},{10,11... | collective-permute-start | bytes 6291464 | tf_op jit(solution)/shard_map/ppermute | solution.py:482
  20.3 20.5 %collective-permute-start.8 = (bf16[784,512]{1,0:T(8,128)(2,1)}, bf16[784,512]{1,0:T(8,128)(2,1)S(1)}, u32[]{:S(2)}, u32[]{:S(2)}) collective-permute-start(bf16[784,512]{1,0:T(8,128)(2,1)} %shard_map.122.refs_0_), channel_id=1, source_target_pairs={{0,2},{1,3},{2,0},{3,1},{4,6},{5,7},{6,4},{7,5},{8,10},{9,11},{10,... | collective-permute-start | bytes 2408456 | tf_op jit(solution)/shard_map/ppermute | solution.py:482
  25.5 16.8 %collective-permute-start.2 = (bf16[784,512]{1,0:T(8,128)(2,1)}, bf16[784,512]{1,0:T(8,128)(2,1)}, u32[]{:S(2)}, u32[]{:S(2)}) collective-permute-start(bf16[784,512]{1,0:T(8,128)(2,1)} %collective-permute-done.1.refs_4_), channel_id=1, source_target_pairs={{4,8},{5,9},{6,10},{7,11},{8,4},{9,5},{10,6},{11,7},{20,24},{21,25... | collective-permute-start | bytes 2408456 | tf_op jit(solution)/shard_map/ppermute | solution.py:482
  27.1 22.0 %collective-permute-start.5 = (bf16[784,512]{1,0:T(8,128)(2,1)}, bf16[784,512]{1,0:T(8,128)(2,1)}, u32[]{:S(2)}, u32[]{:S(2)}) collective-permute-start(bf16[784,512]{1,0:T(8,128)(2,1)} %collective-permute-done), channel_id=1, source_target_pairs={{4,0},{5,1},{6,2},{7,3},{8,12},{9,13},{10,14},{11,15},{20,16},{21,... | collective-permute-start | bytes 2408456 | tf_op jit(solution)/shard_map/ppermute | solution.py:482
  28.4 22.0 %collective-permute-start.13 = (bf16[784,512]{1,0:T(8,128)(2,1)}, bf16[784,512]{1,0:T(8,128)(2,1)}, u32[]{:S(2)}, u32[]{:S(2)}) collective-permute-start(bf16[784,512]{1,0:T(8,128)(2,1)} %shard_map.122.refs_0_), channel_id=1, source_target_pairs={{0,1},{1,0},{2,3},{3,2},{4,5},{5,4},{6,7},{7,6},{8,9},{9,8},{10,11... | collective-permute-start | bytes 2408456 | tf_op jit(solution)/shard_map/ppermute | solution.py:482
  40.8 21.0 %collective-permute-start.16 = (bf16[784,512]{1,0:T(8,128)(2,1)}, bf16[784,512]{1,0:T(8,128)(2,1)S(1)}, u32[]{:S(2)}, u32[]{:S(2)}) collective-permute-start(bf16[784,512]{1,0:T(8,128)(2,1)} %collective-permute-done.1.refs_4_), channel_id=1, source_target_pairs={{0,2},{1,3},{2,0},{3,1},{4,6},{5,7},{6,4},{7,5},{8,10},{9,11},{10,... | collective-permute-start | bytes 2408456 | tf_op jit(solution)/shard_map/ppermute | solution.py:482
  42.3 20.1 %collective-permute-start.15 = (bf16[784,512]{1,0:T(8,128)(2,1)}, bf16[784,512]{1,0:T(8,128)(2,1)S(1)}, u32[]{:S(2)}, u32[]{:S(2)}) collective-permute-start(bf16[784,512]{1,0:T(8,128)(2,1)} %collective-permute-done.1.refs_4_), channel_id=1, source_target_pairs={{0,1},{1,0},{2,3},{3,2},{4,5},{5,4},{6,7},{7,6},{8,9},{9,8},{10,11... | collective-permute-start | bytes 2408456 | tf_op jit(solution)/shard_map/ppermute | solution.py:482
  49.1 13.4 %collective-permute-start.14 = (bf16[784,512]{1,0:T(8,128)(2,1)S(1)}, bf16[784,512]{1,0:T(8,128)(2,1)S(1)}, u32[]{:S(2)}, u32[]{:S(2)}) collective-permute-start(bf16[784,512]{1,0:T(8,128)(2,1)S(1)} %collective-permute-done.8.refs_2_), channel_id=1, source_target_pairs={{0,1},{1,0},{2,3},{3,2},{4,5},{5,4},{6,7},{7,6},{8,9},{9,8},{10,11... | collective-permute-start | bytes 2408456 | tf_op jit(solution)/shard_map/ppermute | solution.py:482
  50.3 27.4 %collective-permute-start.6 = (bf16[784,512]{1,0:T(8,128)(2,1)S(1)}, bf16[784,512]{1,0:T(8,128)(2,1)S(1)}, u32[]{:S(2)}, u32[]{:S(2)}) collective-permute-start(bf16[784,512]{1,0:T(8,128)(2,1)S(1)} %broadcast_select_fusion.refs_2_), channel_id=1, source_target_pairs={{0,2},{1,3},{2,0},{3,1},{4,6},{5,7},{6,4},{7,5},{8,10},{9,11},{10,... | collective-permute-start | bytes 2408456 | tf_op jit(solution)/shard_map/ppermute | solution.py:482
  52.0 38.8 %collective-permute-start.3 = (bf16[784,512]{1,0:T(8,128)(2,1)}, bf16[784,512]{1,0:T(8,128)(2,1)S(1)}, u32[]{:S(2)}, u32[]{:S(2)}) collective-permute-start(bf16[784,512]{1,0:T(8,128)(2,1)} %collective-permute-done.2), channel_id=1, source_target_pairs={{4,0},{5,1},{6,2},{7,3},{8,12},{9,13},{10,14},{11,15},{20,16},{21,... | collective-permute-start | bytes 2408456 | tf_op jit(solution)/shard_map/ppermute | solution.py:482
  61.7 31.5 %collective-permute-start.9 = (bf16[272,512]{1,0:T(8,128)(2,1)S(1)}, bf16[272,512]{1,0:T(8,128)(2,1)S(1)}, u32[]{:S(2)}, u32[]{:S(2)}) collective-permute-start(bf16[272,512]{1,0:T(8,128)(2,1)S(1)} %slice.91), channel_id=1, source_target_pairs={{4,8},{5,9},{6,10},{7,11},{8,4},{9,5},{10,6},{11,7},{20,24},{21,25... | collective-permute-start | bytes 835592 | tf_op jit(solution)/shard_map/ppermute | solution.py:482
  62.4 32.4 %collective-permute-start.18 = (bf16[784,512]{1,0:T(8,128)(2,1)S(1)}, bf16[784,512]{1,0:T(8,128)(2,1)S(1)}, u32[]{:S(2)}, u32[]{:S(2)}) collective-permute-start(bf16[784,512]{1,0:T(8,128)(2,1)S(1)} %broadcast_select_fusion.refs_2_), channel_id=1, source_target_pairs={{0,1},{1,0},{2,3},{3,2},{4,5},{5,4},{6,7},{7,6},{8,9},{9,8},{10,11... | collective-permute-start | bytes 2408456 | tf_op jit(solution)/shard_map/ppermute | solution.py:482
  62.5 33.3 %collective-permute-start.17 = (bf16[784,512]{1,0:T(8,128)(2,1)S(1)}, bf16[784,512]{1,0:T(8,128)(2,1)S(1)}, u32[]{:S(2)}, u32[]{:S(2)}) collective-permute-start(bf16[784,512]{1,0:T(8,128)(2,1)S(1)} %collective-permute-done.16.refs_0_), channel_id=1, source_target_pairs={{0,1},{1,0},{2,3},{3,2},{4,5},{5,4},{6,7},{7,6},{8,9},{9,8},{10,11... | collective-permute-start | bytes 2408456 | tf_op jit(solution)/shard_map/ppermute | solution.py:482
  77.7 31.5 %collective-permute-start.28 = (f32[256,1024]{1,0:T(8,128)S(1)}, f32[256,1024]{1,0:T(8,128)S(1)}, u32[]{:S(2)}, u32[]{:S(2)}) collective-permute-start(f32[256,1024]{1,0:T(8,128)S(1)} %get-tuple-element.35), channel_id=1, source_target_pairs={{0,16},{16,0},{1,17},{17,1},{2,18},{18,2},{3,19},{19,3},{4,20},{20... | collective-permute-start | bytes 3145736 | tf_op jit(solution)/shard_map/ppermute | solution.py:482
  90.8 10.2 %collective-permute-start.7 = (bf16[272,512]{1,0:T(8,128)(2,1)S(1)}, bf16[272,512]{1,0:T(8,128)(2,1)S(1)}, u32[]{:S(2)}, u32[]{:S(2)}) collective-permute-start(bf16[272,512]{1,0:T(8,128)(2,1)S(1)} %slice.90), channel_id=1, source_target_pairs={{4,0},{5,1},{6,2},{7,3},{8,12},{9,13},{10,14},{11,15},{20,16},{21,... | collective-permute-start | bytes 835592 | tf_op jit(solution)/shard_map/ppermute | solution.py:482
  93.3 15.9 %collective-permute-start.4 = (bf16[512,512]{1,0:T(8,128)(2,1)S(1)}, bf16[512,512]{1,0:T(8,128)(2,1)S(1)}, u32[]{:S(2)}, u32[]{:S(2)}) collective-permute-start(bf16[512,512]{1,0:T(8,128)(2,1)S(1)} %slice_select_fusion.refs_2_), channel_id=1, source_target_pairs={{0,2},{1,3},{2,0},{3,1},{4,6},{5,7},{6,4},{7,5},{8,10},{9,11},{10,... | collective-permute-start | bytes 1572872 | tf_op jit(solution)/shard_map/ppermute | solution.py:482
  94.8 15.2 %collective-permute-start.19 = (bf16[784,512]{1,0:T(8,128)(2,1)S(1)}, bf16[784,512]{1,0:T(8,128)(2,1)S(1)}, u32[]{:S(2)}, u32[]{:S(2)}) collective-permute-start(bf16[784,512]{1,0:T(8,128)(2,1)S(1)} %collective-permute-done.6.refs_0_), channel_id=1, source_target_pairs={{0,1},{1,0},{2,3},{3,2},{4,5},{5,4},{6,7},{7,6},{8,9},{9,8},{10,11... | collective-permute-start | bytes 2408456 | tf_op jit(solution)/shard_map/ppermute | solution.py:482
  95.9 14.0 %collective-permute-start.20 = (bf16[512,512]{1,0:T(8,128)(2,1)S(1)}, bf16[512,512]{1,0:T(8,128)(2,1)S(1)}, u32[]{:S(2)}, u32[]{:S(2)}) collective-permute-start(bf16[512,512]{1,0:T(8,128)(2,1)S(1)} %slice_select_fusion.refs_2_), channel_id=1, source_target_pairs={{0,1},{1,0},{2,3},{3,2},{4,5},{5,4},{6,7},{7,6},{8,9},{9,8},{10,11... | collective-permute-start | bytes 1572872 | tf_op jit(solution)/shard_map/ppermute | solution.py:482
  108.5 9.7 %collective-permute-start.12 = (bf16[272,512]{1,0:T(8,128)(2,1)S(1)}, bf16[272,512]{1,0:T(8,128)(2,1)S(1)}, u32[]{:S(2)}, u32[]{:S(2)}) collective-permute-start(bf16[272,512]{1,0:T(8,128)(2,1)S(1)} %collective-permute-done.9.refs_2_.refs_8_), channel_id=1, source_target_pairs={{0,1},{1,0},{2,3},{3,2},{4,5},{5,4},{6,7},{7,6},{8,9},{9,8},{10,11... | collective-permute-start | bytes 835592 | tf_op jit(solution)/shard_map/ppermute | solution.py:482
  109.1 9.1 %collective-permute-start.11 = (bf16[272,512]{1,0:T(8,128)(2,1)S(1)}, bf16[272,512]{1,0:T(8,128)(2,1)S(1)}, u32[]{:S(2)}, u32[]{:S(2)}) collective-permute-start(bf16[272,512]{1,0:T(8,128)(2,1)S(1)} %collective-permute-done.7.refs_1_.refs_7_), channel_id=1, source_target_pairs={{0,1},{1,0},{2,3},{3,2},{4,5},{5,4},{6,7},{7,6},{8,9},{9,8},{10,11... | collective-permute-start | bytes 835592 | tf_op jit(solution)/shard_map/ppermute | solution.py:482
  109.2 9.1 %collective-permute-start.10 = (bf16[512,512]{1,0:T(8,128)(2,1)S(1)}, bf16[512,512]{1,0:T(8,128)(2,1)S(1)}, u32[]{:S(2)}, u32[]{:S(2)}) collective-permute-start(bf16[512,512]{1,0:T(8,128)(2,1)S(1)} %collective-permute-done.4.refs_0_.refs_6_), channel_id=1, source_target_pairs={{0,1},{1,0},{2,3},{3,2},{4,5},{5,4},{6,7},{7,6},{8,9},{9,8},{10,11... | collective-permute-start | bytes 1572872 | tf_op jit(solution)/shard_map/ppermute | solution.py:482
  121.9 10.6 %collective-permute-start.30 = (bf16[64,1024]{1,0:T(8,128)(2,1)S(1)}, bf16[64,1024]{1,0:T(8,128)(2,1)S(1)}, u32[]{:S(2)}, u32[]{:S(2)}) collective-permute-start(bf16[64,1024]{1,0:T(8,128)(2,1)S(1)} %get-tuple-element.39), channel_id=1, source_target_pairs={{0,2},{1,3},{2,0},{3,1},{4,6},{5,7},{6,4},{7,5},{8,10},{9,11},{10,... | collective-permute-start | bytes 393224 | tf_op jit(solution)/shard_map/ppermute | solution.py:482
  (17 other events, 152.4 us)

commit v3 on v2

--- a/solution.py
+++ b/solution.py
@@ -603,7 +603,7 @@
     )
     if linked:
         inner = ((me >> 2) ^ (me >> 3)) & 1
-        stages = gather_stages(payload, inner == 1, requests * hist_slots)
+        stages = gather_stages(payload, inner == 1, requests * hist_slots + META_ROWS)
         keep, sent, gs_student, rate = student_part(
             *stack, n_shard * n_group, 2, halving_order
         )
@@ -622,21 +622,16 @@
     score_weights = (asking_matrix[0], lookup_matrix[0], rate)
     hidden_weights = (inner_projection_matrix,)
     scores, hiddens, owns = [], [], []
-    late = len(stages) - 2 if linked else len(stages) - 1
-    for number, stage in enumerate(stages[:-1]):
-        if number < late:
-            score, hidden, own = rank(dims, info, stage, score_weights, hidden_weights, sel_rows)
-            hiddens.append(hidden)
-            owns.append(own)
-        else:
-            (score,) = rank(dims, info, stage, score_weights, None, sel_rows)
+    for stage in stages[:-1]:
+        score, hidden, own = rank(dims, info, stage, score_weights, hidden_weights, sel_rows)
+        hiddens.append(hidden)
+        owns.append(own)
         scores.append(score)
     known = sum(s.shape[0] for s in scores)
     (send,) = rank(
         dims, info, stages[-1], score_weights, None, sel_rows, known, (scores, gs_student)
     )
-    rest = stages[-2] + stages[-1] if linked else stages[-1]
-    hidden, own = rank(dims, info, rest, None, hidden_weights, sel_rows)
+    hidden, own = rank(dims, info, stages[-1], None, hidden_weights, sel_rows)
     hiddens.append(hidden)
     owns.append(own)
     got = sum_over_shard(send) if linked else lax.psum(send, "shard")

time: 146 us -> 147 us (level)
  local copies, waits for them, and re-layouts: 2.7 us -> 6.2 us
  other arithmetic: 5.87 us -> 4.05 us
    unnamed x16 -> x26, local copies, waits for them, and re-layouts: 2.66 us -> 5.47 us
  transfers between devices with their start and end apart: 33 -> 33, of which waited for: 12 -> 12; matrix products, arithmetic and copies ran while one was open for 4% -> 3% of each run, Pallas kernels for 25% -> 24%
where the time goes in v3:
time: 147 us
  waiting for transfers between devices  61.1 us (42%)
  Pallas kernels  46.8 us (32%)
  starting transfers between devices  27.9 us (19%)
  local copies, waits for them, and re-layouts  6.2 us (4%)
  other arithmetic  4.05 us (3%)
    ppermute x33, waiting for transfers between devices, shift(): return lax.ppermute(x, axis, table)  61.1 us
    pallas_call x5, Pallas kernels, rank(): pl.pallas_call(functools.partial(rank_kernel, dims, sel_rows, layout, (wa...  31.9 us
    ppermute x33, starting transfers between devices, shift(): return lax.ppermute(x, axis, table)  27.9 us
    pallas_call x1, Pallas kernels, student_part(): pl.pallas_call(functools.partial(student_kernel, requests, feats // piece...  8.71 us
    unnamed x26, local copies, waits for them, and re-layouts  5.47 us
    pallas_call x1, Pallas kernels, pack(): pl.pallas_call(pack_kernel, out_shape=jax.ShapeDtypeStruct((total, focus)...  3.39 us
  transfers between devices with their start and end apart: 33, of which 12 were waited for; matrix products, arithmetic and copies ran while one was open for 3% of the time, Pallas kernels for 24%

profile of v3, /device:TPU:0, one launch (start us, length us, event | category | flops | bytes accessed | tf_op | source)
XLA Modules:
  0.0 147.0 jit_solution(1061785938402167672)
XLA Ops:
  1.3 1.6 %copy-done = bf16[1024,1024]{1,0:T(8,128)(2,1)S(1)} copy-done((bf16[1024,1024]{1,0:T(8,128)(2,1)S(1)}, bf16[1024,1024]{1,0:T(8,128)(2,1)}, u32[]{:S(2)}) %copy-start) | copy-done | bytes 2097176
  5.9 8.7 %shard_map.123 = (f32[512,1024]{1,0:T(8,128)S(1)}, f32[512,1024]{1,0:T(8,128)}, f32[1,1024]{1,0:T(1,128)S(1)}, bf16[512,256]{1,0:T(8,128)(2,1)S(1)}) custom-call(s32[1]{0:T(128)} %bitcast.6.me_ref, bf16[512,1024]{1,0:T(8,128)(2,1)S(1)} %bitcast.10, bf16[1024,1024]{1,0:T(8,128)(2,1)S(1)} %copy-done, bf16[1,1024]{1,0:T(2,128)(2,1)S(1)} %reshape.23.s_ref, ...), custom_call_target="tpu_custom_call" | custom-call | flops 2147483648 | bytes 8000000 | tf_op jit(solution)/shard_map/pallas_call | solution.py:172
  15.0 3.4 %shard_map.122.refs_0_ = bf16[784,512]{1,0:T(8,128)(2,1)} custom-call(s32[4,6]{1,0:T(4,128)} %target_ref.1, s32[4]{0:T(128)} %extent_ref.1, bf16[4,128,1024]{2,1,0:T(8,128)(2,1)} %x_hbm.1, s32[4,32]{1,0:T(4,128)} %kept_ref.1, bf16[512,512]{1,0:T(8,128)(2,1)} %bitcast.20), custom_call_target="tpu_custom_call" | custom-call | flops 100000000 | bytes 3000000 | tf_op jit(solution)/shard_map/pallas_call | solution.py:98
  18.4 2.6 %collective-permute-start.1 = (bf16[784,512]{1,0:T(8,128)(2,1)}, bf16[784,512]{1,0:T(8,128)(2,1)}, u32[]{:S(2)}, u32[]{:S(2)}) collective-permute-start(bf16[784,512]{1,0:T(8,128)(2,1)} %shard_map.122.refs_0_), channel_id=1, source_target_pairs={{0,4},{1,5},{2,6},{3,7},{4,0},{5,1},{6,2},{7,3},{8,12},{9,13},{10,... | collective-permute-start | bytes 2408456 | tf_op jit(solution)/shard_map/ppermute | solution.py:482
  21.8 1.6 %collective-permute-start.8 = (bf16[784,512]{1,0:T(8,128)(2,1)}, bf16[784,512]{1,0:T(8,128)(2,1)S(1)}, u32[]{:S(2)}, u32[]{:S(2)}) collective-permute-start(bf16[784,512]{1,0:T(8,128)(2,1)} %shard_map.122.refs_0_), channel_id=1, source_target_pairs={{0,2},{1,3},{2,0},{3,1},{4,6},{5,7},{6,4},{7,5},{8,10},{9,11},{10,... | collective-permute-start | bytes 2408456 | tf_op jit(solution)/shard_map/ppermute | solution.py:482
  23.4 16.6 %collective-permute-done.1.refs_4_ = bf16[784,512]{1,0:T(8,128)(2,1)} collective-permute-done((bf16[784,512]{1,0:T(8,128)(2,1)}, bf16[784,512]{1,0:T(8,128)(2,1)}, u32[]{:S(2)}, u32[]{:S(2)}) %collective-permute-start.1) | collective-permute-done | bytes 802848 | tf_op jit(solution)/shard_map/ppermute | solution.py:482
  42.1 1.7 %collective-permute-start.16 = (bf16[784,512]{1,0:T(8,128)(2,1)}, bf16[784,512]{1,0:T(8,128)(2,1)}, u32[]{:S(2)}, u32[]{:S(2)}) collective-permute-start(bf16[784,512]{1,0:T(8,128)(2,1)} %collective-permute-done.1.refs_4_), channel_id=1, source_target_pairs={{0,2},{1,3},{2,0},{3,1},{4,6},{5,7},{6,4},{7,5},{8,10},{9,11},{10,... | collective-permute-start | bytes 2408456 | tf_op jit(solution)/shard_map/ppermute | solution.py:482
  44.0 19.9 %collective-permute-done.5 = bf16[784,512]{1,0:T(8,128)(2,1)S(1)} collective-permute-done((bf16[784,512]{1,0:T(8,128)(2,1)S(1)}, bf16[784,512]{1,0:T(8,128)(2,1)S(1)}, u32[]{:S(2)}, u32[]{:S(2)}) %collective-permute-start.5) | collective-permute-done | bytes 802848 | tf_op jit(solution)/shard_map/ppermute | solution.py:482
  67.6 2.2 %slice_add_fusion.1 = (f32[256,1024]{1,0:T(8,128)S(1)}, f32[256,1024]{1,0:T(8,128)S(1)}) fusion(f32[512,1024]{1,0:T(8,128)} %collective-permute-done.27, f32[512,1024]{1,0:T(8,128)S(1)} %get-tuple-element.26), kind=kLoop, calls=%fused_computation.1 | loop fusion | flops 524288 | bytes 6291456 | tf_op jit(solution)/shard_map/add | solution.py:535
  69.9 1.6 %collective-permute-start.6 = (bf16[784,512]{1,0:T(8,128)(2,1)S(1)}, bf16[784,512]{1,0:T(8,128)(2,1)S(1)}, u32[]{:S(2)}, u32[]{:S(2)}) collective-permute-start(bf16[784,512]{1,0:T(8,128)(2,1)S(1)} %broadcast_select_fusion.refs_2_), channel_id=1, source_target_pairs={{0,2},{1,3},{2,0},{3,1},{4,6},{5,7},{6,4},{7,5},{8,10},{9,11},{10,... | collective-permute-start | bytes 2408456 | tf_op jit(solution)/shard_map/ppermute | solution.py:482
  73.5 10.6 %shard_map.124 = (f32[6,1,128]{2,1,0:T(1,128)S(1)}, bf16[768,1024]{1,0:T(8,128)(2,1)S(1)}, bf16[64,768]{1,0:T(8,128)(2,1)S(1)}) custom-call(s32[4]{0:T(128)S(1)} %pad_add_fusion.info_ref.me_ref, bf16[784,512]{1,0:T(8,128)(2,1)S(1)} %copy-done.3, bf16[784,512]{1,0:T(8,128)(2,1)} %collective-permute-done.13.refs_1_, ...), custom_call_target="tpu_custom_call" | custom-call | flops 6000000000 | bytes 6000000 | tf_op jit(solution)/shard_map/pallas_call | solution.py:380
  84.1 4.3 %collective-permute-done.3 = bf16[784,512]{1,0:T(8,128)(2,1)S(1)} collective-permute-done((bf16[784,512]{1,0:T(8,128)(2,1)S(1)}, bf16[784,512]{1,0:T(8,128)(2,1)S(1)}, u32[]{:S(2)}, u32[]{:S(2)}) %collective-permute-start.3) | collective-permute-done | bytes 802848 | tf_op jit(solution)/shard_map/ppermute | solution.py:482
  92.3 8.3 %shard_map.125 = (f32[4,1,128]{2,1,0:T(1,128)S(1)}, bf16[512,1024]{1,0:T(8,128)(2,1)S(1)}, bf16[64,512]{1,0:T(8,128)(2,1)S(1)}) custom-call(s32[4]{0:T(128)S(1)} %pad_add_fusion.info_ref.me_ref, bf16[784,512]{1,0:T(8,128)(2,1)} %collective-permute-done.16.refs_0_, bf16[784,512]{1,0:T(8,128)(2,1)S(1)} %collective-permute-done.17.refs_1_, ...), custom_call_target="tpu_custom_call" | custom-call | flops 4000000000 | bytes 4000000 | tf_op jit(solution)/shard_map/pallas_call | solution.py:380
  102.4 8.4 %collective-permute-done.7.refs_1_ = bf16[256,512]{1,0:T(8,128)(2,1)S(1)} collective-permute-done((bf16[256,512]{1,0:T(8,128)(2,1)S(1)}, bf16[256,512]{1,0:T(8,128)(2,1)S(1)}, u32[]{:S(2)}, u32[]{:S(2)}) %collective-permute-start.7) | collective-permute-done | bytes 262176 | tf_op jit(solution)/shard_map/ppermute | solution.py:482
  111.5 7.5 %shard_map.126 = (f32[4,1,128]{2,1,0:T(1,128)S(1)}, bf16[512,1024]{1,0:T(8,128)(2,1)S(1)}, bf16[64,512]{1,0:T(8,128)(2,1)S(1)}) custom-call(s32[4]{0:T(128)S(1)} %pad_add_fusion.info_ref.me_ref, bf16[784,512]{1,0:T(8,128)(2,1)S(1)} %collective-permute-done.6.refs_0_, bf16[784,512]{1,0:T(8,128)(2,1)S(1)} %collective-permute-done.19.refs_1_, ...), custom_call_target="tpu_custom_call" | custom-call | flops 4000000000 | bytes 4000000 | tf_op jit(solution)/shard_map/pallas_call | solution.py:380
  120.8 3.3 %shard_map.127 = f32[24,128]{1,0:T(8,128)S(1)} custom-call(s32[4]{0:T(128)S(1)} %pad_add_fusion.info_ref.me_ref, bf16[528,512]{1,0:T(8,128)(2,1)S(1)} %collective-permute-done.4.refs_0_, bf16[256,512]{1,0:T(8,128)(2,1)S(1)} %collective-permute-done.7.refs_1_, bf16[256,512]{1,0:T(8,128)(2,1)S(1)} %collective-permute-done.9.refs_2_, ...), custom_call_target="tpu_custom_call" | custom-call | flops 1400000000 | bytes 2000000 | tf_op jit(solution)/shard_map/pallas_call | solution.py:380
  126.9 2.1 %shard_map.128 = (bf16[256,1024]{1,0:T(8,128)(2,1)S(1)}, bf16[64,256]{1,0:T(8,128)(2,1)S(1)}) custom-call(s32[4]{0:T(128)S(1)} %pad_add_fusion.info_ref.me_ref, bf16[528,512]{1,0:T(8,128)(2,1)S(1)} %collective-permute-done.4.refs_0_, bf16[256,512]{1,0:T(8,128)(2,1)S(1)} %collective-permute-done.7.refs_1_, ...), custom_call_target="tpu_custom_call" | custom-call | flops 600000000 | bytes 2000000 | tf_op jit(solution)/shard_map/pallas_call | solution.py:380
  130.0 1.7 %collective-permute-start.25 = (f32[24,128]{1,0:T(8,128)S(1)}, f32[24,128]{1,0:T(8,128)S(1)}, u32[]{:S(2)}, u32[]{:S(2)}) collective-permute-start(f32[24,128]{1,0:T(8,128)S(1)} %add.47), channel_id=1, source_target_pairs={{0,8},{1,9},{2,10},{3,11},{4,12},{5,13},{6,14},{7,15},{8,0},{9,1},... | collective-permute-start | bytes 36872 | tf_op jit(solution)/shard_map/ppermute | solution.py:482
  131.7 1.8 %collective-permute-start.26 = (f32[24,128]{1,0:T(8,128)S(1)}, f32[24,128]{1,0:T(8,128)S(1)}, u32[]{:S(2)}, u32[]{:S(2)}) collective-permute-start(f32[24,128]{1,0:T(8,128)S(1)} %add.47), channel_id=1, source_target_pairs={{0,12},{1,13},{2,14},{3,15},{4,8},{5,9},{6,10},{7,11},{8,4},{9,5},... | collective-permute-start | bytes 36872 | tf_op jit(solution)/shard_map/ppermute | solution.py:482
  134.6 2.6 %collective-permute-done.26 = f32[24,128]{1,0:T(8,128)S(1)} collective-permute-done((f32[24,128]{1,0:T(8,128)S(1)}, f32[24,128]{1,0:T(8,128)S(1)}, u32[]{:S(2)}, u32[]{:S(2)}) %collective-permute-start.26) | collective-permute-done | bytes 12320 | tf_op jit(solution)/shard_map/ppermute | solution.py:482
  137.2 1.7 %collective-permute-done.31 = bf16[32,1024]{1,0:T(8,128)(2,1)S(1)} collective-permute-done((bf16[32,1024]{1,0:T(8,128)(2,1)S(1)}, bf16[32,1024]{1,0:T(8,128)(2,1)S(1)}, u32[]{:S(2)}, u32[]{:S(2)}) %collective-permute-start.31) | collective-permute-done | bytes 65568 | tf_op jit(solution)/shard_map/ppermute | solution.py:482
  138.9 2.1 %shard_map.129 = (f32[72,1024]{1,0:T(8,128)S(1)}, bf16[72,1024]{1,0:T(8,128)(2,1)S(1)}) custom-call(s32[4]{0:T(128)S(1)} %pad_add_fusion.info_ref.me_ref, f32[24,128]{1,0:T(8,128)S(1)} %add_add_fusion.got_ref, bf16[1,1024]{1,0:T(2,128)(2,1)S(1)} %reshape.23.s_ref, f32[32,1024]{1,0:T(8,128)S(1)} %fusion.3.base_ref, ...), custom_call_target="tpu_custom_call" | custom-call | flops 1000000000 | bytes 6000000 | tf_op jit(solution)/shard_map/pallas_call | solution.py:453
  141.1 1.6 %collective-permute-start.32 = (bf16[72,1024]{1,0:T(8,128)(2,1)S(1)}, bf16[72,1024]{1,0:T(8,128)(2,1)S(1)}, u32[]{:S(2)}, u32[]{:S(2)}) collective-permute-start(bf16[72,1024]{1,0:T(8,128)(2,1)S(1)} %get-tuple-element.37), channel_id=1, source_target_pairs={{0,16},{16,0},{1,17},{17,1},{2,18},{18,2},{3,19},{19,3},{4,20},{20... | collective-permute-start | bytes 442376 | tf_op jit(solution)/shard_map/ppermute | solution.py:482
  142.6 3.6 %collective-permute-done.32.b_ref = bf16[72,1024]{1,0:T(8,128)(2,1)S(1)} collective-permute-done((bf16[72,1024]{1,0:T(8,128)(2,1)S(1)}, bf16[72,1024]{1,0:T(8,128)(2,1)S(1)}, u32[]{:S(2)}, u32[]{:S(2)}) %collective-permute-start.32) | collective-permute-done | bytes 147488 | tf_op jit(solution)/shard_map/ppermute | solution.py:482
  (94 shorter events, 26.3 us)
Async XLA Ops:
  14.6 51.7 %collective-permute-start.27 = (f32[512,1024]{1,0:T(8,128)}, f32[512,1024]{1,0:T(8,128)}, u32[]{:S(2)}, u32[]{:S(2)}) collective-permute-start(f32[512,1024]{1,0:T(8,128)} %get-tuple-element.27), channel_id=1, source_target_pairs={{0,1},{1,0},{2,3},{3,2},{4,5},{5,4},{6,7},{7,6},{8,9},{9,8},{10,11... | collective-permute-start | bytes 6291464 | tf_op jit(solution)/shard_map/ppermute | solution.py:482
  18.4 21.5 %collective-permute-start.1 = (bf16[784,512]{1,0:T(8,128)(2,1)}, bf16[784,512]{1,0:T(8,128)(2,1)}, u32[]{:S(2)}, u32[]{:S(2)}) collective-permute-start(bf16[784,512]{1,0:T(8,128)(2,1)} %shard_map.122.refs_0_), channel_id=1, source_target_pairs={{0,4},{1,5},{2,6},{3,7},{4,0},{5,1},{6,2},{7,3},{8,12},{9,13},{10,... | collective-permute-start | bytes 2408456 | tf_op jit(solution)/shard_map/ppermute | solution.py:482
  21.1 19.6 %collective-permute-start = (bf16[784,512]{1,0:T(8,128)(2,1)}, bf16[784,512]{1,0:T(8,128)(2,1)S(1)}, u32[]{:S(2)}, u32[]{:S(2)}) collective-permute-start(bf16[784,512]{1,0:T(8,128)(2,1)} %shard_map.122.refs_0_), channel_id=1, source_target_pairs={{4,8},{5,9},{6,10},{7,11},{8,4},{9,5},{10,6},{11,7},{20,24},{21,25... | collective-permute-start | bytes 2408456 | tf_op jit(solution)/shard_map/ppermute | solution.py:482
  21.8 20.3 %collective-permute-start.8 = (bf16[784,512]{1,0:T(8,128)(2,1)}, bf16[784,512]{1,0:T(8,128)(2,1)S(1)}, u32[]{:S(2)}, u32[]{:S(2)}) collective-permute-start(bf16[784,512]{1,0:T(8,128)(2,1)} %shard_map.122.refs_0_), channel_id=1, source_target_pairs={{0,2},{1,3},{2,0},{3,1},{4,6},{5,7},{6,4},{7,5},{8,10},{9,11},{10,... | collective-permute-start | bytes 2408456 | tf_op jit(solution)/shard_map/ppermute | solution.py:482
  40.7 23.2 %collective-permute-start.5 = (bf16[784,512]{1,0:T(8,128)(2,1)S(1)}, bf16[784,512]{1,0:T(8,128)(2,1)S(1)}, u32[]{:S(2)}, u32[]{:S(2)}) collective-permute-start(bf16[784,512]{1,0:T(8,128)(2,1)S(1)} %collective-permute-done), channel_id=1, source_target_pairs={{4,0},{5,1},{6,2},{7,3},{8,12},{9,13},{10,14},{11,15},{20,16},{21,... | collective-permute-start | bytes 2408456 | tf_op jit(solution)/shard_map/ppermute | solution.py:482
  42.0 27.8 %collective-permute-start.13 = (bf16[784,512]{1,0:T(8,128)(2,1)}, bf16[784,512]{1,0:T(8,128)(2,1)}, u32[]{:S(2)}, u32[]{:S(2)}) collective-permute-start(bf16[784,512]{1,0:T(8,128)(2,1)} %shard_map.122.refs_0_), channel_id=1, source_target_pairs={{0,1},{1,0},{2,3},{3,2},{4,5},{5,4},{6,7},{7,6},{8,9},{9,8},{10,11... | collective-permute-start | bytes 2408456 | tf_op jit(solution)/shard_map/ppermute | solution.py:482
  42.1 29.3 %collective-permute-start.16 = (bf16[784,512]{1,0:T(8,128)(2,1)}, bf16[784,512]{1,0:T(8,128)(2,1)}, u32[]{:S(2)}, u32[]{:S(2)}) collective-permute-start(bf16[784,512]{1,0:T(8,128)(2,1)} %collective-permute-done.1.refs_4_), channel_id=1, source_target_pairs={{0,2},{1,3},{2,0},{3,1},{4,6},{5,7},{6,4},{7,5},{8,10},{9,11},{10,... | collective-permute-start | bytes 2408456 | tf_op jit(solution)/shard_map/ppermute | solution.py:482
  43.8 27.8 %collective-permute-start.15 = (bf16[784,512]{1,0:T(8,128)(2,1)}, bf16[784,512]{1,0:T(8,128)(2,1)}, u32[]{:S(2)}, u32[]{:S(2)}) collective-permute-start(bf16[784,512]{1,0:T(8,128)(2,1)} %collective-permute-done.1.refs_4_), channel_id=1, source_target_pairs={{0,1},{1,0},{2,3},{3,2},{4,5},{5,4},{6,7},{7,6},{8,9},{9,8},{10,11... | collective-permute-start | bytes 2408456 | tf_op jit(solution)/shard_map/ppermute | solution.py:482
  66.2 22.2 %collective-permute-start.3 = (bf16[784,512]{1,0:T(8,128)(2,1)S(1)}, bf16[784,512]{1,0:T(8,128)(2,1)S(1)}, u32[]{:S(2)}, u32[]{:S(2)}) collective-permute-start(bf16[784,512]{1,0:T(8,128)(2,1)S(1)} %copy-done.11), channel_id=1, source_target_pairs={{4,0},{5,1},{6,2},{7,3},{8,12},{9,13},{10,14},{11,15},{20,16},{21,... | collective-permute-start | bytes 2408456 | tf_op jit(solution)/shard_map/ppermute | solution.py:482
  69.9 20.4 %collective-permute-start.6 = (bf16[784,512]{1,0:T(8,128)(2,1)S(1)}, bf16[784,512]{1,0:T(8,128)(2,1)S(1)}, u32[]{:S(2)}, u32[]{:S(2)}) collective-permute-start(bf16[784,512]{1,0:T(8,128)(2,1)S(1)} %broadcast_select_fusion.refs_2_), channel_id=1, source_target_pairs={{0,2},{1,3},{2,0},{3,1},{4,6},{5,7},{6,4},{7,5},{8,10},{9,11},{10,... | collective-permute-start | bytes 2408456 | tf_op jit(solution)/shard_map/ppermute | solution.py:482
  71.4 20.3 %collective-permute-start.18 = (bf16[784,512]{1,0:T(8,128)(2,1)S(1)}, bf16[784,512]{1,0:T(8,128)(2,1)S(1)}, u32[]{:S(2)}, u32[]{:S(2)}) collective-permute-start(bf16[784,512]{1,0:T(8,128)(2,1)S(1)} %broadcast_select_fusion.refs_2_), channel_id=1, source_target_pairs={{0,1},{1,0},{2,3},{3,2},{4,5},{5,4},{6,7},{7,6},{8,9},{9,8},{10,11... | collective-permute-start | bytes 2408456 | tf_op jit(solution)/shard_map/ppermute | solution.py:482
  71.7 20.1 %collective-permute-start.17 = (bf16[784,512]{1,0:T(8,128)(2,1)}, bf16[784,512]{1,0:T(8,128)(2,1)S(1)}, u32[]{:S(2)}, u32[]{:S(2)}) collective-permute-start(bf16[784,512]{1,0:T(8,128)(2,1)} %collective-permute-done.16.refs_0_), channel_id=1, source_target_pairs={{0,1},{1,0},{2,3},{3,2},{4,5},{5,4},{6,7},{7,6},{8,9},{9,8},{10,11... | collective-permute-start | bytes 2408456 | tf_op jit(solution)/shard_map/ppermute | solution.py:482
  72.0 30.2 %collective-permute-start.28 = (f32[256,1024]{1,0:T(8,128)S(1)}, f32[256,1024]{1,0:T(8,128)S(1)}, u32[]{:S(2)}, u32[]{:S(2)}) collective-permute-start(f32[256,1024]{1,0:T(8,128)S(1)} %get-tuple-element.41), channel_id=1, source_target_pairs={{0,16},{16,0},{1,17},{17,1},{2,18},{18,2},{3,19},{19,3},{4,20},{20... | collective-permute-start | bytes 3145736 | tf_op jit(solution)/shard_map/ppermute | solution.py:482
  88.4 12.2 %collective-permute-start.9 = (bf16[256,512]{1,0:T(8,128)(2,1)S(1)}, bf16[256,512]{1,0:T(8,128)(2,1)S(1)}, u32[]{:S(2)}, u32[]{:S(2)}) collective-permute-start(bf16[256,512]{1,0:T(8,128)(2,1)S(1)} %slice.91), channel_id=1, source_target_pairs={{4,8},{5,9},{6,10},{7,11},{8,4},{9,5},{10,6},{11,7},{20,24},{21,25... | collective-permute-start | bytes 786440 | tf_op jit(solution)/shard_map/ppermute | solution.py:482
  90.2 21.2 %collective-permute-start.4 = (bf16[528,512]{1,0:T(8,128)(2,1)S(1)}, bf16[528,512]{1,0:T(8,128)(2,1)S(1)}, u32[]{:S(2)}, u32[]{:S(2)}) collective-permute-start(bf16[528,512]{1,0:T(8,128)(2,1)S(1)} %slice_select_fusion.refs_2_), channel_id=1, source_target_pairs={{0,2},{1,3},{2,0},{3,1},{4,6},{5,7},{6,4},{7,5},{8,10},{9,11},{10,... | collective-permute-start | bytes 1622024 | tf_op jit(solution)/shard_map/ppermute | solution.py:482
  91.7 19.7 %collective-permute-start.20 = (bf16[528,512]{1,0:T(8,128)(2,1)S(1)}, bf16[528,512]{1,0:T(8,128)(2,1)S(1)}, u32[]{:S(2)}, u32[]{:S(2)}) collective-permute-start(bf16[528,512]{1,0:T(8,128)(2,1)S(1)} %slice_select_fusion.refs_2_), channel_id=1, source_target_pairs={{0,1},{1,0},{2,3},{3,2},{4,5},{5,4},{6,7},{7,6},{8,9},{9,8},{10,11... | collective-permute-start | bytes 1622024 | tf_op jit(solution)/shard_map/ppermute | solution.py:482
  91.8 19.7 %collective-permute-start.19 = (bf16[784,512]{1,0:T(8,128)(2,1)S(1)}, bf16[784,512]{1,0:T(8,128)(2,1)S(1)}, u32[]{:S(2)}, u32[]{:S(2)}) collective-permute-start(bf16[784,512]{1,0:T(8,128)(2,1)S(1)} %collective-permute-done.6.refs_0_), channel_id=1, source_target_pairs={{0,1},{1,0},{2,3},{3,2},{4,5},{5,4},{6,7},{7,6},{8,9},{9,8},{10,11... | collective-permute-start | bytes 2408456 | tf_op jit(solution)/shard_map/ppermute | solution.py:482
  100.7 10.2 %collective-permute-start.7 = (bf16[256,512]{1,0:T(8,128)(2,1)S(1)}, bf16[256,512]{1,0:T(8,128)(2,1)S(1)}, u32[]{:S(2)}, u32[]{:S(2)}) collective-permute-start(bf16[256,512]{1,0:T(8,128)(2,1)S(1)} %slice.90), channel_id=1, source_target_pairs={{4,0},{5,1},{6,2},{7,3},{8,12},{9,13},{10,14},{11,15},{20,16},{21,... | collective-permute-start | bytes 786440 | tf_op jit(solution)/shard_map/ppermute | solution.py:482
  102.2 8.7 %collective-permute-start.21 = (bf16[256,512]{1,0:T(8,128)(2,1)S(1)}, bf16[256,512]{1,0:T(8,128)(2,1)S(1)}, u32[]{:S(2)}, u32[]{:S(2)}) collective-permute-start(bf16[256,512]{1,0:T(8,128)(2,1)S(1)} %slice_select_fusion.1.refs_3_), channel_id=1, source_target_pairs={{0,1},{1,0},{2,3},{3,2},{4,5},{5,4},{6,7},{7,6},{8,9},{9,8},{10,11... | collective-permute-start | bytes 786440 | tf_op jit(solution)/shard_map/ppermute | solution.py:482
  110.9 9.9 %collective-permute-start.12 = (bf16[256,512]{1,0:T(8,128)(2,1)S(1)}, bf16[256,512]{1,0:T(8,128)(2,1)S(1)}, u32[]{:S(2)}, u32[]{:S(2)}) collective-permute-start(bf16[256,512]{1,0:T(8,128)(2,1)S(1)} %collective-permute-done.9.refs_2_), channel_id=1, source_target_pairs={{0,1},{1,0},{2,3},{3,2},{4,5},{5,4},{6,7},{7,6},{8,9},{9,8},{10,11... | collective-permute-start | bytes 786440 | tf_op jit(solution)/shard_map/ppermute | solution.py:482
  110.9 9.9 %collective-permute-start.11 = (bf16[256,512]{1,0:T(8,128)(2,1)S(1)}, bf16[256,512]{1,0:T(8,128)(2,1)S(1)}, u32[]{:S(2)}, u32[]{:S(2)}) collective-permute-start(bf16[256,512]{1,0:T(8,128)(2,1)S(1)} %collective-permute-done.7.refs_1_), channel_id=1, source_target_pairs={{0,1},{1,0},{2,3},{3,2},{4,5},{5,4},{6,7},{7,6},{8,9},{9,8},{10,11... | collective-permute-start | bytes 786440 | tf_op jit(solution)/shard_map/ppermute | solution.py:482
  111.4 9.4 %collective-permute-start.10 = (bf16[528,512]{1,0:T(8,128)(2,1)S(1)}, bf16[528,512]{1,0:T(8,128)(2,1)S(1)}, u32[]{:S(2)}, u32[]{:S(2)}) collective-permute-start(bf16[528,512]{1,0:T(8,128)(2,1)S(1)} %collective-permute-done.4.refs_0_), channel_id=1, source_target_pairs={{0,1},{1,0},{2,3},{3,2},{4,5},{5,4},{6,7},{7,6},{8,9},{9,8},{10,11... | collective-permute-start | bytes 1622024 | tf_op jit(solution)/shard_map/ppermute | solution.py:482
  111.5 8.7 %collective-permute-start.29 = (bf16[128,1024]{1,0:T(8,128)(2,1)S(1)}, bf16[128,1024]{1,0:T(8,128)(2,1)S(1)}, u32[]{:S(2)}, u32[]{:S(2)}) collective-permute-start(bf16[128,1024]{1,0:T(8,128)(2,1)S(1)} %get-tuple-element.43), channel_id=1, source_target_pairs={{0,4},{1,5},{2,6},{3,7},{4,0},{5,1},{6,2},{7,3},{8,12},{9,13},{10,... | collective-permute-start | bytes 786440 | tf_op jit(solution)/shard_map/ppermute | solution.py:482
  120.2 13.3 %collective-permute-start.30 = (bf16[64,1024]{1,0:T(8,128)(2,1)S(1)}, bf16[64,1024]{1,0:T(8,128)(2,1)S(1)}, u32[]{:S(2)}, u32[]{:S(2)}) collective-permute-start(bf16[64,1024]{1,0:T(8,128)(2,1)S(1)} %get-tuple-element.45), channel_id=1, source_target_pairs={{0,2},{1,3},{2,0},{3,1},{4,6},{5,7},{6,4},{7,5},{8,10},{9,11},{10,... | collective-permute-start | bytes 393224 | tf_op jit(solution)/shard_map/ppermute | solution.py:482
  (22 other events, 111.2 us)

commit v4 on v3

--- a/solution.py
+++ b/solution.py
@@ -224,8 +224,10 @@
             preferred_element_type=F32,
         )
         weights = jnp.where(slot < lengths[r : r + 1, :], jnp.exp(logits), 0.0)
-        mixed = weights * values[r * hist_slots : (r + 1) * hist_slots, :]
-        per_head = jnp.sum(mixed, axis=0, keepdims=True) / jnp.sum(weights, axis=0, keepdims=True)
+        whole = jnp.sum(weights, axis=0, keepdims=True)
+        level = jnp.where(whole > 1.0, 2.0**-64, 2.0**64)
+        mixed = (weights * level) * values[r * hist_slots : (r + 1) * hist_slots, :]
+        per_head = jnp.sum(mixed, axis=0, keepdims=True) / (whole * level)
         folded = per_head[:, :kept_rows]
         for b in range(1, wide // kept_rows):
             folded = folded + per_head[:, b * kept_rows : (b + 1) * kept_rows]
@@ -387,7 +389,7 @@
         + [full_vmem()] * (len(weights) + len(small)),
         out_specs=tuple(outs),
         scratch_shapes=scratch,
-        compiler_params=room(22),
+        compiler_params=room(18),
         cost_estimate=pl.CostEstimate(
             flops=flops, bytes_accessed=blocks * 10**6, transcendentals=0
         ),
@@ -456,7 +458,7 @@
         in_specs=[scalars()] + [full_vmem()] * (3 + 2 * parts),
         out_specs=(full_vmem(),) * 2,
         scratch_shapes=[VMEM((blocks, got.shape[1]), F32)],
-        compiler_params=room(22),
+        compiler_params=room(18),
         cost_estimate=pl.CostEstimate(flops=10**9, bytes_accessed=6 * 10**6, transcendentals=0),
     )(me, got, s.reshape(1, units), base, *owns, *hiddens)
 

time: 147 us -> 148 us (level)
  no operation moved by 1% of the time
where the time goes in v4:
time: 148 us; the launch traced here: 147 us
  waiting for transfers between devices  60.9 us (41%)
  Pallas kernels  47.1 us (32%)
  starting transfers between devices  28 us (19%)
  local copies, waits for them, and re-layouts  6.2 us (4%)
  other arithmetic  3.96 us (3%)
    ppermute x33, waiting for transfers between devices, shift(): return lax.ppermute(x, axis, table)  60.9 us
    pallas_call x5, Pallas kernels, rank(): pl.pallas_call(functools.partial(rank_kernel, dims, sel_rows, layout, (wa...  32.2 us
    ppermute x33, starting transfers between devices, shift(): return lax.ppermute(x, axis, table)  28 us
    pallas_call x1, Pallas kernels, student_part(): pl.pallas_call(functools.partial(student_kernel, requests, feats // piece...  8.71 us
    unnamed x26, local copies, waits for them, and re-layouts  5.47 us
    pallas_call x1, Pallas kernels, pack(): pl.pallas_call(pack_kernel, out_shape=jax.ShapeDtypeStruct((total, focus)...  3.39 us
  transfers between devices with their start and end apart: 33, of which 12 were waited for; matrix products, arithmetic and copies ran while one was open for 3% of the time, Pallas kernels for 24%

profile of v4, /device:TPU:0, one launch (start us, length us, event | category | flops | bytes accessed | tf_op | source)
XLA Modules:
  0.0 147.2 jit_solution(824193496292234913)
XLA Ops:
  1.3 1.6 %copy-done = bf16[1024,1024]{1,0:T(8,128)(2,1)S(1)} copy-done((bf16[1024,1024]{1,0:T(8,128)(2,1)S(1)}, bf16[1024,1024]{1,0:T(8,128)(2,1)}, u32[]{:S(2)}) %copy-start) | copy-done | bytes 2097176
  5.9 8.7 %shard_map.123 = (f32[512,1024]{1,0:T(8,128)S(1)}, f32[512,1024]{1,0:T(8,128)}, f32[1,1024]{1,0:T(1,128)S(1)}, bf16[512,256]{1,0:T(8,128)(2,1)S(1)}) custom-call(s32[1]{0:T(128)} %bitcast.6.me_ref, bf16[512,1024]{1,0:T(8,128)(2,1)S(1)} %bitcast.10, bf16[1024,1024]{1,0:T(8,128)(2,1)S(1)} %copy-done, bf16[1,1024]{1,0:T(2,128)(2,1)S(1)} %reshape.23.s_ref, ...), custom_call_target="tpu_custom_call" | custom-call | flops 2147483648 | bytes 8000000 | tf_op jit(solution)/shard_map/pallas_call | solution.py:172
  15.0 3.4 %shard_map.122.refs_0_ = bf16[784,512]{1,0:T(8,128)(2,1)} custom-call(s32[4,6]{1,0:T(4,128)} %target_ref.1, s32[4]{0:T(128)} %extent_ref.1, bf16[4,128,1024]{2,1,0:T(8,128)(2,1)} %x_hbm.1, s32[4,32]{1,0:T(4,128)} %kept_ref.1, bf16[512,512]{1,0:T(8,128)(2,1)} %bitcast.20), custom_call_target="tpu_custom_call" | custom-call | flops 100000000 | bytes 3000000 | tf_op jit(solution)/shard_map/pallas_call | solution.py:98
  18.4 2.6 %collective-permute-start.1 = (bf16[784,512]{1,0:T(8,128)(2,1)}, bf16[784,512]{1,0:T(8,128)(2,1)}, u32[]{:S(2)}, u32[]{:S(2)}) collective-permute-start(bf16[784,512]{1,0:T(8,128)(2,1)} %shard_map.122.refs_0_), channel_id=1, source_target_pairs={{0,4},{1,5},{2,6},{3,7},{4,0},{5,1},{6,2},{7,3},{8,12},{9,13},{10,... | collective-permute-start | bytes 2408456 | tf_op jit(solution)/shard_map/ppermute | solution.py:484
  21.8 1.6 %collective-permute-start.8 = (bf16[784,512]{1,0:T(8,128)(2,1)}, bf16[784,512]{1,0:T(8,128)(2,1)S(1)}, u32[]{:S(2)}, u32[]{:S(2)}) collective-permute-start(bf16[784,512]{1,0:T(8,128)(2,1)} %shard_map.122.refs_0_), channel_id=1, source_target_pairs={{0,2},{1,3},{2,0},{3,1},{4,6},{5,7},{6,4},{7,5},{8,10},{9,11},{10,... | collective-permute-start | bytes 2408456 | tf_op jit(solution)/shard_map/ppermute | solution.py:484
  23.4 16.6 %collective-permute-done.1.refs_4_ = bf16[784,512]{1,0:T(8,128)(2,1)} collective-permute-done((bf16[784,512]{1,0:T(8,128)(2,1)}, bf16[784,512]{1,0:T(8,128)(2,1)}, u32[]{:S(2)}, u32[]{:S(2)}) %collective-permute-start.1) | collective-permute-done | bytes 802848 | tf_op jit(solution)/shard_map/ppermute | solution.py:484
  42.1 1.7 %collective-permute-start.16 = (bf16[784,512]{1,0:T(8,128)(2,1)}, bf16[784,512]{1,0:T(8,128)(2,1)}, u32[]{:S(2)}, u32[]{:S(2)}) collective-permute-start(bf16[784,512]{1,0:T(8,128)(2,1)} %collective-permute-done.1.refs_4_), channel_id=1, source_target_pairs={{0,2},{1,3},{2,0},{3,1},{4,6},{5,7},{6,4},{7,5},{8,10},{9,11},{10,... | collective-permute-start | bytes 2408456 | tf_op jit(solution)/shard_map/ppermute | solution.py:484
  44.0 19.9 %collective-permute-done.5 = bf16[784,512]{1,0:T(8,128)(2,1)S(1)} collective-permute-done((bf16[784,512]{1,0:T(8,128)(2,1)S(1)}, bf16[784,512]{1,0:T(8,128)(2,1)S(1)}, u32[]{:S(2)}, u32[]{:S(2)}) %collective-permute-start.5) | collective-permute-done | bytes 802848 | tf_op jit(solution)/shard_map/ppermute | solution.py:484
  67.6 2.2 %slice_add_fusion.1 = (f32[256,1024]{1,0:T(8,128)S(1)}, f32[256,1024]{1,0:T(8,128)S(1)}) fusion(f32[512,1024]{1,0:T(8,128)} %collective-permute-done.27, f32[512,1024]{1,0:T(8,128)S(1)} %get-tuple-element.26), kind=kLoop, calls=%fused_computation.1 | loop fusion | flops 524288 | bytes 6291456 | tf_op jit(solution)/shard_map/add | solution.py:537
  69.8 1.6 %collective-permute-start.6 = (bf16[784,512]{1,0:T(8,128)(2,1)S(1)}, bf16[784,512]{1,0:T(8,128)(2,1)S(1)}, u32[]{:S(2)}, u32[]{:S(2)}) collective-permute-start(bf16[784,512]{1,0:T(8,128)(2,1)S(1)} %broadcast_select_fusion.refs_2_), channel_id=1, source_target_pairs={{0,2},{1,3},{2,0},{3,1},{4,6},{5,7},{6,4},{7,5},{8,10},{9,11},{10,... | collective-permute-start | bytes 2408456 | tf_op jit(solution)/shard_map/ppermute | solution.py:484
  73.4 10.7 %shard_map.124 = (f32[6,1,128]{2,1,0:T(1,128)S(1)}, bf16[768,1024]{1,0:T(8,128)(2,1)S(1)}, bf16[64,768]{1,0:T(8,128)(2,1)S(1)}) custom-call(s32[4]{0:T(128)S(1)} %pad_add_fusion.info_ref.me_ref, bf16[784,512]{1,0:T(8,128)(2,1)S(1)} %copy-done.3, bf16[784,512]{1,0:T(8,128)(2,1)} %collective-permute-done.13.refs_1_, ...), custom_call_target="tpu_custom_call" | custom-call | flops 6000000000 | bytes 6000000 | tf_op jit(solution)/shard_map/pallas_call | solution.py:382
  84.2 4.3 %collective-permute-done.3 = bf16[784,512]{1,0:T(8,128)(2,1)S(1)} collective-permute-done((bf16[784,512]{1,0:T(8,128)(2,1)S(1)}, bf16[784,512]{1,0:T(8,128)(2,1)S(1)}, u32[]{:S(2)}, u32[]{:S(2)}) %collective-permute-start.3) | collective-permute-done | bytes 802848 | tf_op jit(solution)/shard_map/ppermute | solution.py:484
  92.2 8.4 %shard_map.125 = (f32[4,1,128]{2,1,0:T(1,128)S(1)}, bf16[512,1024]{1,0:T(8,128)(2,1)S(1)}, bf16[64,512]{1,0:T(8,128)(2,1)S(1)}) custom-call(s32[4]{0:T(128)S(1)} %pad_add_fusion.info_ref.me_ref, bf16[784,512]{1,0:T(8,128)(2,1)} %collective-permute-done.16.refs_0_, bf16[784,512]{1,0:T(8,128)(2,1)S(1)} %collective-permute-done.17.refs_1_, ...), custom_call_target="tpu_custom_call" | custom-call | flops 4000000000 | bytes 4000000 | tf_op jit(solution)/shard_map/pallas_call | solution.py:382
  102.5 8.5 %collective-permute-done.7.refs_1_ = bf16[256,512]{1,0:T(8,128)(2,1)S(1)} collective-permute-done((bf16[256,512]{1,0:T(8,128)(2,1)S(1)}, bf16[256,512]{1,0:T(8,128)(2,1)S(1)}, u32[]{:S(2)}, u32[]{:S(2)}) %collective-permute-start.7) | collective-permute-done | bytes 262176 | tf_op jit(solution)/shard_map/ppermute | solution.py:484
  111.5 7.6 %shard_map.126 = (f32[4,1,128]{2,1,0:T(1,128)S(1)}, bf16[512,1024]{1,0:T(8,128)(2,1)S(1)}, bf16[64,512]{1,0:T(8,128)(2,1)S(1)}) custom-call(s32[4]{0:T(128)S(1)} %pad_add_fusion.info_ref.me_ref, bf16[784,512]{1,0:T(8,128)(2,1)S(1)} %collective-permute-done.6.refs_0_, bf16[784,512]{1,0:T(8,128)(2,1)S(1)} %collective-permute-done.19.refs_1_, ...), custom_call_target="tpu_custom_call" | custom-call | flops 4000000000 | bytes 4000000 | tf_op jit(solution)/shard_map/pallas_call | solution.py:382
  120.9 3.3 %shard_map.127 = f32[24,128]{1,0:T(8,128)S(1)} custom-call(s32[4]{0:T(128)S(1)} %pad_add_fusion.info_ref.me_ref, bf16[528,512]{1,0:T(8,128)(2,1)S(1)} %collective-permute-done.4.refs_0_, bf16[256,512]{1,0:T(8,128)(2,1)S(1)} %collective-permute-done.7.refs_1_, bf16[256,512]{1,0:T(8,128)(2,1)S(1)} %collective-permute-done.9.refs_2_, ...), custom_call_target="tpu_custom_call" | custom-call | flops 1400000000 | bytes 2000000 | tf_op jit(solution)/shard_map/pallas_call | solution.py:382
  127.0 2.1 %shard_map.128 = (bf16[256,1024]{1,0:T(8,128)(2,1)S(1)}, bf16[64,256]{1,0:T(8,128)(2,1)S(1)}) custom-call(s32[4]{0:T(128)S(1)} %pad_add_fusion.info_ref.me_ref, bf16[528,512]{1,0:T(8,128)(2,1)S(1)} %collective-permute-done.4.refs_0_, bf16[256,512]{1,0:T(8,128)(2,1)S(1)} %collective-permute-done.7.refs_1_, ...), custom_call_target="tpu_custom_call" | custom-call | flops 600000000 | bytes 2000000 | tf_op jit(solution)/shard_map/pallas_call | solution.py:382
  130.2 1.6 %collective-permute-start.25 = (f32[24,128]{1,0:T(8,128)S(1)}, f32[24,128]{1,0:T(8,128)S(1)}, u32[]{:S(2)}, u32[]{:S(2)}) collective-permute-start(f32[24,128]{1,0:T(8,128)S(1)} %add.47), channel_id=1, source_target_pairs={{0,8},{1,9},{2,10},{3,11},{4,12},{5,13},{6,14},{7,15},{8,0},{9,1},... | collective-permute-start | bytes 36872 | tf_op jit(solution)/shard_map/ppermute | solution.py:484
  131.8 1.8 %collective-permute-start.26 = (f32[24,128]{1,0:T(8,128)S(1)}, f32[24,128]{1,0:T(8,128)S(1)}, u32[]{:S(2)}, u32[]{:S(2)}) collective-permute-start(f32[24,128]{1,0:T(8,128)S(1)} %add.47), channel_id=1, source_target_pairs={{0,12},{1,13},{2,14},{3,15},{4,8},{5,9},{6,10},{7,11},{8,4},{9,5},... | collective-permute-start | bytes 36872 | tf_op jit(solution)/shard_map/ppermute | solution.py:484
  134.7 2.6 %collective-permute-done.26 = f32[24,128]{1,0:T(8,128)S(1)} collective-permute-done((f32[24,128]{1,0:T(8,128)S(1)}, f32[24,128]{1,0:T(8,128)S(1)}, u32[]{:S(2)}, u32[]{:S(2)}) %collective-permute-start.26) | collective-permute-done | bytes 12320 | tf_op jit(solution)/shard_map/ppermute | solution.py:484
  137.4 1.7 %collective-permute-done.31 = bf16[32,1024]{1,0:T(8,128)(2,1)S(1)} collective-permute-done((bf16[32,1024]{1,0:T(8,128)(2,1)S(1)}, bf16[32,1024]{1,0:T(8,128)(2,1)S(1)}, u32[]{:S(2)}, u32[]{:S(2)}) %collective-permute-start.31) | collective-permute-done | bytes 65568 | tf_op jit(solution)/shard_map/ppermute | solution.py:484
  139.1 2.1 %shard_map.129 = (f32[72,1024]{1,0:T(8,128)S(1)}, bf16[72,1024]{1,0:T(8,128)(2,1)S(1)}) custom-call(s32[4]{0:T(128)S(1)} %pad_add_fusion.info_ref.me_ref, f32[24,128]{1,0:T(8,128)S(1)} %add_add_fusion.got_ref, bf16[1,1024]{1,0:T(2,128)(2,1)S(1)} %reshape.23.s_ref, f32[32,1024]{1,0:T(8,128)S(1)} %fusion.3.base_ref, ...), custom_call_target="tpu_custom_call" | custom-call | flops 1000000000 | bytes 6000000 | tf_op jit(solution)/shard_map/pallas_call | solution.py:455
  141.2 1.6 %collective-permute-start.32 = (bf16[72,1024]{1,0:T(8,128)(2,1)S(1)}, bf16[72,1024]{1,0:T(8,128)(2,1)S(1)}, u32[]{:S(2)}, u32[]{:S(2)}) collective-permute-start(bf16[72,1024]{1,0:T(8,128)(2,1)S(1)} %get-tuple-element.37), channel_id=1, source_target_pairs={{0,16},{16,0},{1,17},{17,1},{2,18},{18,2},{3,19},{19,3},{4,20},{20... | collective-permute-start | bytes 442376 | tf_op jit(solution)/shard_map/ppermute | solution.py:484
  142.8 3.7 %collective-permute-done.32.b_ref = bf16[72,1024]{1,0:T(8,128)(2,1)S(1)} collective-permute-done((bf16[72,1024]{1,0:T(8,128)(2,1)S(1)}, bf16[72,1024]{1,0:T(8,128)(2,1)S(1)}, u32[]{:S(2)}, u32[]{:S(2)}) %collective-permute-start.32) | collective-permute-done | bytes 147488 | tf_op jit(solution)/shard_map/ppermute | solution.py:484
  (94 shorter events, 26.3 us)
Async XLA Ops:
  14.6 51.7 %collective-permute-start.27 = (f32[512,1024]{1,0:T(8,128)}, f32[512,1024]{1,0:T(8,128)}, u32[]{:S(2)}, u32[]{:S(2)}) collective-permute-start(f32[512,1024]{1,0:T(8,128)} %get-tuple-element.27), channel_id=1, source_target_pairs={{0,1},{1,0},{2,3},{3,2},{4,5},{5,4},{6,7},{7,6},{8,9},{9,8},{10,11... | collective-permute-start | bytes 6291464 | tf_op jit(solution)/shard_map/ppermute | solution.py:484
  18.4 21.5 %collective-permute-start.1 = (bf16[784,512]{1,0:T(8,128)(2,1)}, bf16[784,512]{1,0:T(8,128)(2,1)}, u32[]{:S(2)}, u32[]{:S(2)}) collective-permute-start(bf16[784,512]{1,0:T(8,128)(2,1)} %shard_map.122.refs_0_), channel_id=1, source_target_pairs={{0,4},{1,5},{2,6},{3,7},{4,0},{5,1},{6,2},{7,3},{8,12},{9,13},{10,... | collective-permute-start | bytes 2408456 | tf_op jit(solution)/shard_map/ppermute | solution.py:484
  21.1 19.6 %collective-permute-start = (bf16[784,512]{1,0:T(8,128)(2,1)}, bf16[784,512]{1,0:T(8,128)(2,1)S(1)}, u32[]{:S(2)}, u32[]{:S(2)}) collective-permute-start(bf16[784,512]{1,0:T(8,128)(2,1)} %shard_map.122.refs_0_), channel_id=1, source_target_pairs={{4,8},{5,9},{6,10},{7,11},{8,4},{9,5},{10,6},{11,7},{20,24},{21,25... | collective-permute-start | bytes 2408456 | tf_op jit(solution)/shard_map/ppermute | solution.py:484
  21.8 20.3 %collective-permute-start.8 = (bf16[784,512]{1,0:T(8,128)(2,1)}, bf16[784,512]{1,0:T(8,128)(2,1)S(1)}, u32[]{:S(2)}, u32[]{:S(2)}) collective-permute-start(bf16[784,512]{1,0:T(8,128)(2,1)} %shard_map.122.refs_0_), channel_id=1, source_target_pairs={{0,2},{1,3},{2,0},{3,1},{4,6},{5,7},{6,4},{7,5},{8,10},{9,11},{10,... | collective-permute-start | bytes 2408456 | tf_op jit(solution)/shard_map/ppermute | solution.py:484
  40.7 23.2 %collective-permute-start.5 = (bf16[784,512]{1,0:T(8,128)(2,1)S(1)}, bf16[784,512]{1,0:T(8,128)(2,1)S(1)}, u32[]{:S(2)}, u32[]{:S(2)}) collective-permute-start(bf16[784,512]{1,0:T(8,128)(2,1)S(1)} %collective-permute-done), channel_id=1, source_target_pairs={{4,0},{5,1},{6,2},{7,3},{8,12},{9,13},{10,14},{11,15},{20,16},{21,... | collective-permute-start | bytes 2408456 | tf_op jit(solution)/shard_map/ppermute | solution.py:484
  42.0 27.8 %collective-permute-start.13 = (bf16[784,512]{1,0:T(8,128)(2,1)}, bf16[784,512]{1,0:T(8,128)(2,1)}, u32[]{:S(2)}, u32[]{:S(2)}) collective-permute-start(bf16[784,512]{1,0:T(8,128)(2,1)} %shard_map.122.refs_0_), channel_id=1, source_target_pairs={{0,1},{1,0},{2,3},{3,2},{4,5},{5,4},{6,7},{7,6},{8,9},{9,8},{10,11... | collective-permute-start | bytes 2408456 | tf_op jit(solution)/shard_map/ppermute | solution.py:484
  42.1 29.3 %collective-permute-start.16 = (bf16[784,512]{1,0:T(8,128)(2,1)}, bf16[784,512]{1,0:T(8,128)(2,1)}, u32[]{:S(2)}, u32[]{:S(2)}) collective-permute-start(bf16[784,512]{1,0:T(8,128)(2,1)} %collective-permute-done.1.refs_4_), channel_id=1, source_target_pairs={{0,2},{1,3},{2,0},{3,1},{4,6},{5,7},{6,4},{7,5},{8,10},{9,11},{10,... | collective-permute-start | bytes 2408456 | tf_op jit(solution)/shard_map/ppermute | solution.py:484
  43.8 27.8 %collective-permute-start.15 = (bf16[784,512]{1,0:T(8,128)(2,1)}, bf16[784,512]{1,0:T(8,128)(2,1)}, u32[]{:S(2)}, u32[]{:S(2)}) collective-permute-start(bf16[784,512]{1,0:T(8,128)(2,1)} %collective-permute-done.1.refs_4_), channel_id=1, source_target_pairs={{0,1},{1,0},{2,3},{3,2},{4,5},{5,4},{6,7},{7,6},{8,9},{9,8},{10,11... | collective-permute-start | bytes 2408456 | tf_op jit(solution)/shard_map/ppermute | solution.py:484
  66.2 22.2 %collective-permute-start.3 = (bf16[784,512]{1,0:T(8,128)(2,1)S(1)}, bf16[784,512]{1,0:T(8,128)(2,1)S(1)}, u32[]{:S(2)}, u32[]{:S(2)}) collective-permute-start(bf16[784,512]{1,0:T(8,128)(2,1)S(1)} %copy-done.11), channel_id=1, source_target_pairs={{4,0},{5,1},{6,2},{7,3},{8,12},{9,13},{10,14},{11,15},{20,16},{21,... | collective-permute-start | bytes 2408456 | tf_op jit(solution)/shard_map/ppermute | solution.py:484
  69.8 20.4 %collective-permute-start.6 = (bf16[784,512]{1,0:T(8,128)(2,1)S(1)}, bf16[784,512]{1,0:T(8,128)(2,1)S(1)}, u32[]{:S(2)}, u32[]{:S(2)}) collective-permute-start(bf16[784,512]{1,0:T(8,128)(2,1)S(1)} %broadcast_select_fusion.refs_2_), channel_id=1, source_target_pairs={{0,2},{1,3},{2,0},{3,1},{4,6},{5,7},{6,4},{7,5},{8,10},{9,11},{10,... | collective-permute-start | bytes 2408456 | tf_op jit(solution)/shard_map/ppermute | solution.py:484
  71.4 20.3 %collective-permute-start.18 = (bf16[784,512]{1,0:T(8,128)(2,1)S(1)}, bf16[784,512]{1,0:T(8,128)(2,1)S(1)}, u32[]{:S(2)}, u32[]{:S(2)}) collective-permute-start(bf16[784,512]{1,0:T(8,128)(2,1)S(1)} %broadcast_select_fusion.refs_2_), channel_id=1, source_target_pairs={{0,1},{1,0},{2,3},{3,2},{4,5},{5,4},{6,7},{7,6},{8,9},{9,8},{10,11... | collective-permute-start | bytes 2408456 | tf_op jit(solution)/shard_map/ppermute | solution.py:484
  71.6 20.1 %collective-permute-start.17 = (bf16[784,512]{1,0:T(8,128)(2,1)}, bf16[784,512]{1,0:T(8,128)(2,1)S(1)}, u32[]{:S(2)}, u32[]{:S(2)}) collective-permute-start(bf16[784,512]{1,0:T(8,128)(2,1)} %collective-permute-done.16.refs_0_), channel_id=1, source_target_pairs={{0,1},{1,0},{2,3},{3,2},{4,5},{5,4},{6,7},{7,6},{8,9},{9,8},{10,11... | collective-permute-start | bytes 2408456 | tf_op jit(solution)/shard_map/ppermute | solution.py:484
  71.9 30.3 %collective-permute-start.28 = (f32[256,1024]{1,0:T(8,128)S(1)}, f32[256,1024]{1,0:T(8,128)S(1)}, u32[]{:S(2)}, u32[]{:S(2)}) collective-permute-start(f32[256,1024]{1,0:T(8,128)S(1)} %get-tuple-element.41), channel_id=1, source_target_pairs={{0,16},{16,0},{1,17},{17,1},{2,18},{18,2},{3,19},{19,3},{4,20},{20... | collective-permute-start | bytes 3145736 | tf_op jit(solution)/shard_map/ppermute | solution.py:484
  88.4 12.2 %collective-permute-start.9 = (bf16[256,512]{1,0:T(8,128)(2,1)S(1)}, bf16[256,512]{1,0:T(8,128)(2,1)S(1)}, u32[]{:S(2)}, u32[]{:S(2)}) collective-permute-start(bf16[256,512]{1,0:T(8,128)(2,1)S(1)} %slice.91), channel_id=1, source_target_pairs={{4,8},{5,9},{6,10},{7,11},{8,4},{9,5},{10,6},{11,7},{20,24},{21,25... | collective-permute-start | bytes 786440 | tf_op jit(solution)/shard_map/ppermute | solution.py:484
  90.2 21.3 %collective-permute-start.4 = (bf16[528,512]{1,0:T(8,128)(2,1)S(1)}, bf16[528,512]{1,0:T(8,128)(2,1)S(1)}, u32[]{:S(2)}, u32[]{:S(2)}) collective-permute-start(bf16[528,512]{1,0:T(8,128)(2,1)S(1)} %slice_select_fusion.refs_2_), channel_id=1, source_target_pairs={{0,2},{1,3},{2,0},{3,1},{4,6},{5,7},{6,4},{7,5},{8,10},{9,11},{10,... | collective-permute-start | bytes 1622024 | tf_op jit(solution)/shard_map/ppermute | solution.py:484
  91.7 19.8 %collective-permute-start.20 = (bf16[528,512]{1,0:T(8,128)(2,1)S(1)}, bf16[528,512]{1,0:T(8,128)(2,1)S(1)}, u32[]{:S(2)}, u32[]{:S(2)}) collective-permute-start(bf16[528,512]{1,0:T(8,128)(2,1)S(1)} %slice_select_fusion.refs_2_), channel_id=1, source_target_pairs={{0,1},{1,0},{2,3},{3,2},{4,5},{5,4},{6,7},{7,6},{8,9},{9,8},{10,11... | collective-permute-start | bytes 1622024 | tf_op jit(solution)/shard_map/ppermute | solution.py:484
  91.7 19.8 %collective-permute-start.19 = (bf16[784,512]{1,0:T(8,128)(2,1)S(1)}, bf16[784,512]{1,0:T(8,128)(2,1)S(1)}, u32[]{:S(2)}, u32[]{:S(2)}) collective-permute-start(bf16[784,512]{1,0:T(8,128)(2,1)S(1)} %collective-permute-done.6.refs_0_), channel_id=1, source_target_pairs={{0,1},{1,0},{2,3},{3,2},{4,5},{5,4},{6,7},{7,6},{8,9},{9,8},{10,11... | collective-permute-start | bytes 2408456 | tf_op jit(solution)/shard_map/ppermute | solution.py:484
  100.7 10.2 %collective-permute-start.7 = (bf16[256,512]{1,0:T(8,128)(2,1)S(1)}, bf16[256,512]{1,0:T(8,128)(2,1)S(1)}, u32[]{:S(2)}, u32[]{:S(2)}) collective-permute-start(bf16[256,512]{1,0:T(8,128)(2,1)S(1)} %slice.90), channel_id=1, source_target_pairs={{4,0},{5,1},{6,2},{7,3},{8,12},{9,13},{10,14},{11,15},{20,16},{21,... | collective-permute-start | bytes 786440 | tf_op jit(solution)/shard_map/ppermute | solution.py:484
  102.2 8.7 %collective-permute-start.21 = (bf16[256,512]{1,0:T(8,128)(2,1)S(1)}, bf16[256,512]{1,0:T(8,128)(2,1)S(1)}, u32[]{:S(2)}, u32[]{:S(2)}) collective-permute-start(bf16[256,512]{1,0:T(8,128)(2,1)S(1)} %slice_select_fusion.1.refs_3_), channel_id=1, source_target_pairs={{0,1},{1,0},{2,3},{3,2},{4,5},{5,4},{6,7},{7,6},{8,9},{9,8},{10,11... | collective-permute-start | bytes 786440 | tf_op jit(solution)/shard_map/ppermute | solution.py:484
  110.9 9.9 %collective-permute-start.12 = (bf16[256,512]{1,0:T(8,128)(2,1)S(1)}, bf16[256,512]{1,0:T(8,128)(2,1)S(1)}, u32[]{:S(2)}, u32[]{:S(2)}) collective-permute-start(bf16[256,512]{1,0:T(8,128)(2,1)S(1)} %collective-permute-done.9.refs_2_), channel_id=1, source_target_pairs={{0,1},{1,0},{2,3},{3,2},{4,5},{5,4},{6,7},{7,6},{8,9},{9,8},{10,11... | collective-permute-start | bytes 786440 | tf_op jit(solution)/shard_map/ppermute | solution.py:484
  110.9 9.9 %collective-permute-start.11 = (bf16[256,512]{1,0:T(8,128)(2,1)S(1)}, bf16[256,512]{1,0:T(8,128)(2,1)S(1)}, u32[]{:S(2)}, u32[]{:S(2)}) collective-permute-start(bf16[256,512]{1,0:T(8,128)(2,1)S(1)} %collective-permute-done.7.refs_1_), channel_id=1, source_target_pairs={{0,1},{1,0},{2,3},{3,2},{4,5},{5,4},{6,7},{7,6},{8,9},{9,8},{10,11... | collective-permute-start | bytes 786440 | tf_op jit(solution)/shard_map/ppermute | solution.py:484
  111.4 9.4 %collective-permute-start.10 = (bf16[528,512]{1,0:T(8,128)(2,1)S(1)}, bf16[528,512]{1,0:T(8,128)(2,1)S(1)}, u32[]{:S(2)}, u32[]{:S(2)}) collective-permute-start(bf16[528,512]{1,0:T(8,128)(2,1)S(1)} %collective-permute-done.4.refs_0_), channel_id=1, source_target_pairs={{0,1},{1,0},{2,3},{3,2},{4,5},{5,4},{6,7},{7,6},{8,9},{9,8},{10,11... | collective-permute-start | bytes 1622024 | tf_op jit(solution)/shard_map/ppermute | solution.py:484
  111.5 8.7 %collective-permute-start.29 = (bf16[128,1024]{1,0:T(8,128)(2,1)S(1)}, bf16[128,1024]{1,0:T(8,128)(2,1)S(1)}, u32[]{:S(2)}, u32[]{:S(2)}) collective-permute-start(bf16[128,1024]{1,0:T(8,128)(2,1)S(1)} %get-tuple-element.43), channel_id=1, source_target_pairs={{0,4},{1,5},{2,6},{3,7},{4,0},{5,1},{6,2},{7,3},{8,12},{9,13},{10,... | collective-permute-start | bytes 786440 | tf_op jit(solution)/shard_map/ppermute | solution.py:484
  120.3 13.3 %collective-permute-start.30 = (bf16[64,1024]{1,0:T(8,128)(2,1)S(1)}, bf16[64,1024]{1,0:T(8,128)(2,1)S(1)}, u32[]{:S(2)}, u32[]{:S(2)}) collective-permute-start(bf16[64,1024]{1,0:T(8,128)(2,1)S(1)} %get-tuple-element.45), channel_id=1, source_target_pairs={{0,2},{1,3},{2,0},{3,1},{4,6},{5,7},{6,4},{7,5},{8,10},{9,11},{10,... | collective-permute-start | bytes 393224 | tf_op jit(solution)/shard_map/ppermute | solution.py:484
  (22 other events, 111.2 us)
